TPU v7x, 32 devices: a whole 2x2x4 slice. The times are simulated.
32 devices in a mesh: wide: 8 (over z, y), narrow: 4 (over x, core).
Axes of the slice: x: 2, y: 2, z: 4, core: 2. Of those that a mesh axis runs over, the one named last changes fastest.
Arguments:
- latents: bfloat16 [32, 256, 768], P('wide', None, 'narrow'), may hold values from -6 to 6
- cotangent: bfloat16 [32, 256, 768], P('wide', None, 'narrow'), may hold values from -6 to 6
- timesteps: int32 [32], replicated, may hold values from 0 to 999, as said below
- time_in: float32 [256, 768], replicated, may hold values from -0.375 to 0.375
- time_out: float32 [768, 768], replicated, may hold values from -0.21875 to 0.21875
- ada_weight: float32 [768, 4608], replicated, may hold values from -0.21875 to 0.21875
- ada_bias: float32 [4608], replicated, may hold values from -3 to 3
- attn_kernel: float32 [9, 768], replicated, may hold values from -2 to 2
- qkv_weight: bfloat16 [3, 768, 768], P(None, None, 'narrow'), may hold values from -0.21875 to 0.21875
- out_weight: bfloat16 [768, 768], P('narrow'), may hold values from -0.875 to 0.875
- up_weight: bfloat16 [768, 3072], P(None, 'narrow'), may hold values from -0.21875 to 0.21875
- ffn_kernel: float32 [9, 3072], P(None, 'narrow'), may hold values from -2 to 2
- down_weight: bfloat16 [3072, 768], P('narrow'), may hold values from -0.21875 to 0.21875
Outputs:
- outputs: bfloat16 [32, 256, 768], P('wide', None, 'narrow')
- input_grad: bfloat16 [32, 256, 768], P('wide', None, 'narrow')
- time_in_grad: float32 [256, 768], replicated
- time_out_grad: float32 [768, 768], replicated
- ada_weight_grad: float32 [768, 4608], replicated
- ada_bias_grad: float32 [4608], replicated
- attn_kernel_grad: float32 [9, 768], replicated
- qkv_weight_grad: float32 [3, 768, 768], P(None, None, 'narrow')
- out_weight_grad: float32 [768, 768], P('narrow')
- up_weight_grad: float32 [768, 3072], P(None, 'narrow')
- ffn_kernel_grad: float32 [9, 3072], P(None, 'narrow')
- down_weight_grad: float32 [3072, 768], P('narrow')
Inputs may be any that keep to these rules, and one draw needn't show every extreme that they name: `timesteps`: no two latents of one wide index fall into the same bucket; each bucket holds at most 2 * 4 latents, and some bucket holds exactly 2 * 4.
All inputs are finite; a program needn't handle non-finite values.
Results may differ from a plain program's by a relative error of at most 0.022.
Values may be sent and summed in bfloat16 or wider, within the bound.
No kernel may reach another device: no remote copies, remote signals or barrier semaphores. Data moves between devices by JAX's collectives and lax.ppermute only.
A program may use at most 256 MiB of HBM per device.

v0:
```python
import functools
import math

import jax
import jax.numpy as jnp
from jax import lax
from jax.experimental import pallas as pl
from jax.experimental.pallas import tpu as pltpu
from jax.sharding import PartitionSpec as P

HEAD_DIM = 64
FREQ = 256
SIDE = 16
PAIR = 2

BF = jnp.bfloat16
F32 = jnp.float32
HIGHEST = lax.Precision.HIGHEST
LANES = 128
ROWS = 128
FEW_ROWS = 64
BAND = 64
GELU_A = math.sqrt(2.0 / math.pi)
GELU_B = 0.044715
EPS = 1e-06
VMEM_LIMIT = 60 * 1024 * 1024
WEIGHT_ROWS = 256
BACK_ROWS = 64
PACKED = 40


def dot(a, b):
    return lax.dot_general(a, b, (((1,), (0,)), ((), ())), preferred_element_type=F32)


def dot_nt(a, b):
    return lax.dot_general(a, b, (((1,), (1,)), ((), ())), preferred_element_type=F32)


def dot_tn(a, b):
    return lax.dot_general(a, b, (((0,), (0,)), ((), ())), preferred_element_type=F32)


def column_of(rows):
    return lax.broadcasted_iota(jnp.int32, (rows, LANES), 0) % SIDE


def from_left(v):
    moved = pltpu.roll(v, 1, 0)
    return jnp.where(column_of(v.shape[0]) == 0, 0.0, moved)


def from_right(v):
    moved = pltpu.roll(v, v.shape[0] - 1, 0)
    return jnp.where(column_of(v.shape[0]) == SIDE - 1, 0.0, moved)


def conv_band(padded, at, lanes, kern):
    rows = [padded[pl.ds(at + SIDE * r, BAND), lanes] for r in range(3)]
    mixed = [
        rows[0] * kern[c] + rows[1] * kern[3 + c] + rows[2] * kern[6 + c] for c in range(3)
    ]
    return from_left(mixed[0]) + mixed[1] + from_right(mixed[2])


def conv_back_band(padded_grad, at, lanes, kern):
    wide = padded_grad[pl.ds(at, BAND + 2 * SIDE), lanes]
    shifted = [from_right(wide), wide, from_left(wide)]
    total = None
    for r in range(3):
        for c in range(3):
            low = SIDE * (2 - r)
            term = shifted[c][low : low + BAND] * kern[3 * r + c]
            total = term if total is None else total + term
    return total, [s[SIDE : SIDE + BAND] for s in shifted]


def fold_rows(v):
    total = v[0:8]
    for at in range(8, v.shape[0], 8):
        total = total + v[at : at + 8]
    return total


def taps_of(kern_ref, lanes):
    block = kern_ref[:, lanes]
    return [block[t : t + 1] for t in range(9)]


def zero_edges(ref):
    edge = jnp.zeros((SIDE, ref.shape[1]), F32)
    tall = ref.shape[0] // PAIR
    for rel in range(PAIR):
        ref[rel * tall : rel * tall + SIDE, :] = edge
        ref[(rel + 1) * tall - SIDE : (rel + 1) * tall, :] = edge


def inside(ref, rel):
    tall = ref.shape[0] // PAIR
    return slice(rel * tall + SIDE, (rel + 1) * tall - SIDE)


def gather_features(n, parts, held, out):
    _, share, tokens = parts[0].shape
    core = jnp.bitwise_and(n, 1)

    def one(rel):
        for step, part in enumerate(parts):
            held[jnp.bitwise_xor(n, step)] = part[jnp.bitwise_xor(rel, core)]
        out[pl.ds(pl.multiple_of(rel * tokens, tokens), tokens), :] = held[...].reshape(len(parts) * share, tokens).T

    pair_loop(one)


def by_core(core, low, share, keep_out, send_out, turned):
    tokens = low.shape[0] // PAIR

    def one(rel):
        lat = jnp.bitwise_xor(rel, core)
        turned[...] = low[pl.ds(pl.multiple_of(rel * tokens, tokens), tokens), :].T
        for x in range(2):
            here = pl.ds(pl.multiple_of((2 * x + core) * share, 16), share)
            there = pl.ds(pl.multiple_of((2 * x + 1 - core) * share, 16), share)
            keep_out[x, lat] = turned[here, :]
            send_out[x, lat] = turned[there, :]

    pair_loop(one)


def norm_stats(v):
    width = v.shape[1]
    mean = jnp.sum(v, -1, keepdims=True) * (1.0 / width)
    center = v - mean
    spread = jnp.sum(center * center, -1, keepdims=True) * (1.0 / width)
    scale = lax.rsqrt(spread + EPS)
    return center * scale, scale


def head_masks(share):
    lane = lax.broadcasted_iota(jnp.int32, (1, share), 1) // HEAD_DIM
    return [(lane == h).astype(F32).astype(BF) for h in range(share // HEAD_DIM)]


def half_rows(v, parity):
    tokens, width = v.shape
    split = v.reshape(tokens // (2 * SIDE), 2, SIDE, width)
    return split[:, parity].reshape(tokens // 2, width)


def join_rows(even, odd):
    half, width = even.shape
    both = jnp.stack([even.reshape(half // SIDE, SIDE, width), odd.reshape(half // SIDE, SIDE, width)], 1)
    return both.reshape(2 * half, width)


def softmax_rows(queries, keys):
    scores = dot_nt(queries, keys) * (1.0 / math.sqrt(HEAD_DIM))
    rows = lax.broadcasted_iota(jnp.int32, scores.shape, 0)
    cols = lax.broadcasted_iota(jnp.int32, scores.shape, 1)
    same = (rows + cols) % 2 == 0
    scores = jnp.where(same, scores, -1e30)
    top = jnp.max(scores, -1, keepdims=True)
    grown = jnp.where(same, jnp.exp(scores - top), 0.0)
    return grown / jnp.sum(grown, -1, keepdims=True)


def beside(stacked, heads):
    rows = stacked.shape[0] // heads
    return jnp.concatenate([stacked[h * rows : (h + 1) * rows] for h in range(heads)], axis=1)


def lane_loop(width, body):
    count = width // LANES

    def step(j, carry):
        body(j // count, pl.ds(pl.multiple_of((j % count) * LANES, LANES), LANES))
        return carry

    lax.fori_loop(0, PAIR * count, step, 0)


def band_loop(tokens, body, carry):
    return lax.fori_loop(0, tokens // BAND, lambda j, c: body(pl.multiple_of(j * BAND, BAND), c), carry)


def row_loop(tokens, body, size=ROWS):
    count = tokens // size

    def step(j, carry):
        body(j // count, pl.multiple_of(j * size, size))
        return carry

    lax.fori_loop(0, PAIR * count, step, 0)


def pair_loop(body):
    def step(j, carry):
        body(j)
        return carry

    lax.fori_loop(0, PAIR, step, 0)


def attn_kernel_body(
    flow, s_ref, xo, xc, xx, xd, mod, kern, wqkv, wout,
    full_out, grouped_out, q_out, k_out, v_out, ctx_out, keep_out, send_out,
    held, padded,
):
    n = s_ref[0]
    core = jnp.bitwise_and(n, 1)
    share, tokens = xo.shape[1], xo.shape[2]
    width = full_out.shape[1]
    tall = tokens + 2 * SIDE
    zero_edges(padded)
    flow.need(xo, xc, xx, xd, mod, kern)
    gather_features(n, (xo, xc, xx, xd), held, full_out)
    flow.sent(full_out)

    def rows(rel, at):
        lat = jnp.bitwise_xor(rel, core)
        normed, _ = norm_stats(full_out[pl.ds(at, ROWS), :].astype(F32))
        here = pl.ds(pl.multiple_of(at + (2 * rel + 1) * SIDE, SIDE), ROWS)
        padded[here, :] = normed * (1.0 + mod[lat, 1:2, :]) + mod[lat, 0:1, :]

    row_loop(tokens, rows)

    def lanes(rel, at):
        taps = taps_of(kern, at)
        for band in range(0, tokens, BAND):
            here = pl.ds(pl.multiple_of(rel * tokens + band, BAND), BAND)
            grouped_out[here, at] = conv_band(padded, pl.multiple_of(rel * tall + band, SIDE), at, taps).astype(BF)

    lane_loop(width, lanes)
    flow.sent(grouped_out)
    flow.need(wqkv, wout)
    grouped = grouped_out[...]
    q_out[...] = dot_nt(grouped, wqkv[0]).astype(BF)
    k_out[...] = dot_nt(grouped, wqkv[1]).astype(BF)
    v_out[...] = dot_nt(grouped, wqkv[2]).astype(BF)
    flow.sent(q_out, k_out, v_out)
    masks = head_masks(share)
    heads = len(masks)

    def attend(rel):
        here = pl.ds(pl.multiple_of(rel * tokens, tokens), tokens)
        query, key, value = q_out[here, :], k_out[here, :], v_out[here, :]
        parts = []
        for parity in range(2):
            q = half_rows(query, parity)
            k = half_rows(key, parity)
            v = half_rows(value, parity)
            probs = softmax_rows(jnp.concatenate([q * m for m in masks], axis=0), k)
            low = beside(probs.astype(BF), heads)
            parts.append(dot(low, jnp.concatenate([v * m for m in masks], axis=0)).astype(BF))
        ctx_out[here, :] = join_rows(*parts)

    pair_loop(attend)
    flow.sent(ctx_out)
    send_out[...] = dot(ctx_out[tokens : 2 * tokens, :], wout[...]).astype(BF)
    flow.sent(send_out)
    keep_out[...] = dot(ctx_out[0:tokens, :], wout[...]).astype(BF)
    flow.sent(keep_out)


def ffn_kernel_body(
    first, flow, s_ref, go, gc, gx, gd, full, att, mod, up, down, kern, kgrad_in,
    g_out, second_out, active_out, gfed_out, ghid_out, keep_out, send_out, mods_out, kgrad_out, fkeep_out, fsend_out,
    held, padded, slope, gpad, mid, fed, low, sums, turned,
):
    n = s_ref[0]
    core = jnp.bitwise_and(n, 1)
    share, tokens = go.shape[1], go.shape[2]
    units = up.shape[1]
    tall = tokens + 2 * SIDE
    zero_edges(padded)
    zero_edges(gpad)
    flow.need(go, gc, gx, gd)
    gather_features(n, (go, gc, gx, gd), held, g_out)
    flow.sent(g_out)
    flow.need(full, att, mod, kgrad_in)
    kgrad_out[...] = jnp.zeros(kgrad_out.shape, F32) if first else kgrad_in[...]

    def rows(rel, at):
        lat = jnp.bitwise_xor(rel, core)
        here = pl.ds(at, ROWS)
        middle = full[here, :].astype(F32) + mod[lat, 2:3, :] * att[here, :].astype(F32)
        mid[here, :] = middle
        normed, _ = norm_stats(middle)
        second_out[here, :] = (normed * (1.0 + mod[lat, 4:5, :]) + mod[lat, 3:4, :]).astype(BF)
        gfed_out[here, :] = (mod[lat, 5:6, :] * g_out[here, :].astype(F32)).astype(BF)

    row_loop(tokens, rows)
    flow.sent(second_out, gfed_out)
    flow.need(up, kern)
    hidden = dot(second_out[...], up[...])
    for rel in range(PAIR):
        padded[inside(padded, rel), :] = hidden[rel * tokens : (rel + 1) * tokens]

    def lanes(rel, at):
        taps = taps_of(kern, at)
        for band in range(0, tokens, BAND):
            here = pl.ds(pl.multiple_of(rel * tokens + band, BAND), BAND)
            mixed = conv_band(padded, pl.multiple_of(rel * tall + band, SIDE), at, taps)
            square = mixed * mixed
            curve = jnp.tanh(GELU_A * mixed * (1.0 + GELU_B * square))
            half = 0.5 * (1.0 + curve)
            active_out[here, at] = (mixed * half).astype(BF)
            slope[here, at] = half + (0.5 * GELU_A) * mixed * (1.0 - curve * curve) * (
                1.0 + (3.0 * GELU_B) * square
            )

    lane_loop(units, lanes)
    flow.sent(active_out)
    flow.need(down)
    fed[...] = dot(active_out[...], down[...])
    sums[...] = jnp.zeros(sums.shape, F32)

    def rows_fed(rel, at):
        lat = jnp.bitwise_xor(rel, core)
        here = pl.ds(at, ROWS)
        term = fed[here, :]
        sums[lat] += fold_rows(term * g_out[here, :].astype(F32))
        low[here, :] = (mod[lat, 5:6, :] * term + 0.25 * mid[here, :]).astype(BF)

    row_loop(tokens, rows_fed)
    for lat in range(PAIR):
        mods_out[lat] = jnp.sum(sums[lat], 0, keepdims=True)
    by_core(core, low, share, fkeep_out, fsend_out, turned)
    flow.sent(fkeep_out, fsend_out, mods_out)
    gact = dot_nt(gfed_out[...], down[...]).astype(BF).astype(F32)
    for rel in range(PAIR):
        here = slice(rel * tokens, (rel + 1) * tokens)
        gpad[inside(gpad, rel), :] = gact[here] * slope[here, :]

    def lanes_back(rel, at):
        taps = taps_of(kern, at)
        sums = [None] * 9
        for band in range(0, tokens, BAND):
            here = pl.ds(pl.multiple_of(rel * tokens + band, BAND), BAND)
            base = pl.multiple_of(rel * tall + band, SIDE)
            total, shifted = conv_back_band(gpad, base, at, taps)
            ghid_out[here, at] = total.astype(BF)
            for r in range(3):
                values = padded[pl.ds(base + SIDE * r, BAND), at]
                for c in range(3):
                    part = fold_rows(values * shifted[c])
                    sums[3 * r + c] = part if sums[3 * r + c] is None else sums[3 * r + c] + part
        for t in range(9):
            kgrad_out[t : t + 1, at] += jnp.sum(sums[t], 0, keepdims=True)

    lane_loop(units, lanes_back)
    flow.sent(ghid_out, kgrad_out)
    send_out[...] = dot_nt(ghid_out[tokens : 2 * tokens, :], up[...]).astype(BF)
    flow.sent(send_out)
    keep_out[...] = dot_nt(ghid_out[0:tokens, :], up[...]).astype(BF)
    flow.sent(keep_out)


def attn_back_body(
    flow, s_ref, full, att, gs, gfull, mod, q_in, k_in, v_in, wout, gates,
    gatt_out, gqkv_out, gmid_out, mods_out,
    sums, gctx,
):
    core = jnp.bitwise_and(s_ref[0], 1)
    tokens = full.shape[0] // PAIR
    width = full.shape[1]
    share = q_in.shape[1]
    mods_out[...] = jnp.zeros(mods_out.shape, F32)
    sums[...] = jnp.zeros(sums.shape, F32)
    flow.need(full, att, gs, gfull, mod)

    def rows(rel, at):
        lat = jnp.bitwise_xor(rel, core)
        here = pl.ds(at, ROWS)
        gate1 = mod[lat, 2:3, :]
        attended = att[here, :].astype(F32)
        normed, inv = norm_stats(full[here, :].astype(F32) + gate1 * attended)
        grad = gs[here, :].astype(F32)
        inner = grad * (1.0 + mod[lat, 4:5, :])
        mean_a = jnp.sum(inner, -1, keepdims=True) * (1.0 / width)
        mean_b = jnp.sum(inner * normed, -1, keepdims=True) * (1.0 / width)
        whole_grad = gfull[here, :].astype(F32) + inv * (inner - mean_a - normed * mean_b)
        gmid_out[here, :] = whole_grad.astype(BF)
        gatt_out[here, :] = (gate1 * whole_grad).astype(BF)
        sums[3 * lat] += fold_rows(attended * whole_grad)
        sums[3 * lat + 1] += fold_rows(grad)
        sums[3 * lat + 2] += fold_rows(grad * normed)

    row_loop(tokens, rows)
    for lat in range(PAIR):
        for k in range(3):
            mods_out[lat, 2 + k : 3 + k, :] = 0.25 * jnp.sum(sums[3 * lat + k], 0, keepdims=True)
    flow.need(wout, q_in, k_in, v_in, gates)
    for lat in range(PAIR):
        mods_out[lat, 5:6, :] = gates[lat]
    flow.sent(gatt_out, gmid_out, mods_out)
    gctx[...] = dot_nt(gatt_out[...], wout[...]).astype(BF)
    masks = head_masks(share)
    heads = len(masks)
    factor = 1.0 / math.sqrt(HEAD_DIM)

    def attend(rel):
        here = pl.ds(pl.multiple_of(rel * tokens, tokens), tokens)
        query, key, value, grads = q_in[here, :], k_in[here, :], v_in[here, :], gctx[here, :]
        parts_q, parts_k, parts_v = [], [], []
        for parity in range(2):
            q = half_rows(query, parity)
            k = half_rows(key, parity)
            v = half_rows(value, parity)
            gc = half_rows(grads, parity)
            q_all = jnp.concatenate([q * m for m in masks], axis=0)
            k_all = jnp.concatenate([k * m for m in masks], axis=0)
            gc_all = jnp.concatenate([gc * m for m in masks], axis=0)
            probs = softmax_rows(q_all, k)
            parts_v.append(dot_tn(probs.astype(BF), gc_all).astype(BF))
            gprobs = dot_nt(gc_all, v).astype(BF).astype(F32)
            gscores = (probs * (gprobs - jnp.sum(probs * gprobs, -1, keepdims=True))).astype(BF)
            parts_q.append((dot(beside(gscores, heads), k_all) * factor).astype(BF))
            parts_k.append((dot_tn(gscores, q_all) * factor).astype(BF))
        for k, parts in enumerate((parts_q, parts_k, parts_v)):
            gqkv_out[here, k * share : (k + 1) * share] = join_rows(*parts)

    pair_loop(attend)
    flow.sent(gqkv_out)


def input_back_body(
    closing, flow, s_ref, full, mod, gqkv, wqkv, kern, kgrad_in, gmid, mods_in, before,
    kgrad_out, mods_out, keep_out, send_out,
    normed1, scale1, first, gpad, gback, low, mods, rows_out, turned,
):
    core = jnp.bitwise_and(s_ref[0], 1)
    tokens = full.shape[0] // PAIR
    width = full.shape[1]
    share = gqkv.shape[1] // 3
    tall = tokens + 2 * SIDE
    zero_edges(first)
    zero_edges(gpad)
    flow.need(full, mod)

    def rows_first(rel, at):
        lat = jnp.bitwise_xor(rel, core)
        here = pl.ds(at, FEW_ROWS)
        normed, inv = norm_stats(full[here, :].astype(F32))
        normed1[here, :] = normed
        scale1[here, :] = jnp.broadcast_to(inv, (FEW_ROWS, LANES))
        inside_rows = pl.ds(pl.multiple_of(at + (2 * rel + 1) * SIDE, SIDE), FEW_ROWS)
        first[inside_rows, :] = normed * (1.0 + mod[lat, 1:2, :]) + mod[lat, 0:1, :]

    row_loop(tokens, rows_first, FEW_ROWS)
    flow.need(gqkv, wqkv, kern, kgrad_in, gmid, mods_in, before)
    kgrad_out[...] = kgrad_in[...] if closing else jnp.zeros(kgrad_out.shape, F32)
    mods[...] = mods_in[...]
    for rel in range(PAIR):
        here = slice(rel * tokens, (rel + 1) * tokens)
        gpad[inside(gpad, rel), :] = dot(gqkv[here, :], wqkv[...])

    def lanes(rel, at):
        taps = taps_of(kern, at)

        def bands(band, sums):
            here = pl.ds(pl.multiple_of(rel * tokens + band, BAND), BAND)
            base = pl.multiple_of(rel * tall + band, SIDE)
            total, shifted = conv_back_band(gpad, base, at, taps)
            gback[here, at] = total
            values = [first[pl.ds(base + SIDE * r, BAND), at] for r in range(3)]
            parts = [fold_rows(values[r] * shifted[c]) for r in range(3) for c in range(3)]
            parts += [fold_rows(total), fold_rows(total * normed1[here, at])]
            return [a + b for a, b in zip(sums, parts)]

        *sums, shift_sum, scale_sum = band_loop(tokens, bands, [jnp.zeros((8, LANES), F32)] * 11)
        for t in range(9):
            kgrad_out[t : t + 1, at] += jnp.sum(sums[t], 0, keepdims=True)
        lat = jnp.bitwise_xor(rel, core)
        mods[lat, 0:1, at] = jnp.sum(shift_sum, 0, keepdims=True)
        mods[lat, 1:2, at] = jnp.sum(scale_sum, 0, keepdims=True)

    lane_loop(width, lanes)
    if closing:
        rows_out[...] = jnp.zeros(rows_out.shape, F32)
        for lat in range(PAIR):
            rows_out[6 * lat : 6 * lat + 6, :] = before[lat, 0:6, :]
            rows_out[6 * (PAIR + lat) : 6 * (PAIR + lat) + 6, :] = mods[lat, 0:6, :]
        rows_out[12 * PAIR : 12 * PAIR + 9, :] = kgrad_out[0:9, :]
        mods_out[...] = rows_out[...].astype(BF)
    else:
        mods_out[...] = mods[...]
    flow.sent(mods_out, kgrad_out)

    def rows_back(rel, at):
        lat = jnp.bitwise_xor(rel, core)
        here = pl.ds(at, FEW_ROWS)
        inner = gback[here, :] * (1.0 + mod[lat, 1:2, :])
        normed = normed1[here, :]
        mean_a = jnp.sum(inner, -1, keepdims=True) * (1.0 / width)
        mean_b = jnp.sum(inner * normed, -1, keepdims=True) * (1.0 / width)
        grad = scale1[here, 0:1] * (inner - mean_a - normed * mean_b)
        low[here, :] = (grad + 0.25 * gmid[here, :].astype(F32)).astype(BF)

    row_loop(tokens, rows_back, FEW_ROWS)
    by_core(core, low, share, keep_out, send_out, turned)
    flow.sent(keep_out, send_out)


class Flow:
    def __init__(self, arrivals, departures):
        self.arrivals, self.departures = arrivals, departures
        self.leaving = []
        for _, copy in arrivals:
            copy.start()

    def need(self, *refs):
        for ref in refs:
            for _, copy in [a for a in self.arrivals if a[0] is ref]:
                copy.wait()
            self.arrivals = [a for a in self.arrivals if a[0] is not ref]

    def sent(self, *refs):
        for ref in refs:
            for held, copy in self.departures:
                if held is ref:
                    copy.start()
                    self.leaving.append(copy)

    def end(self):
        for copy in self.leaving:
            copy.wait()


def call(body, name, scalars, ins, outs, scratch, flops, held=()):
    n_in, n_out = len(ins), len(outs)
    places, buffer_shapes = [], []
    for array, window, into in ins:
        dims = array.shape if window is None else (PAIR,) + array.shape[1:]
        if into is None:
            buffer_shapes.append((dims, array.dtype))
        elif into[0].start == 0:
            buffer_shapes.append(((PAIR * dims[0],) + dims[1:], array.dtype))
        places.append(len(buffer_shapes) - 1)

    def run(s_ref, *refs):
        sources = refs[:n_in]
        targets = refs[n_in + len(held) : n_in + len(held) + n_out]
        buffers = refs[n_in + len(held) + n_out : -1]
        sems = refs[-1]
        n_held = len(buffer_shapes)
        buffers_in, buffers_out = buffers[:n_held], buffers[n_held : n_held + n_out]
        rest = buffers[n_held + n_out :]
        arrivals, departures = [], []
        for k, (source, (_, window, into)) in enumerate(zip(sources, ins)):
            view = source if window is None else source.at[window]
            buffer = buffers_in[places[k]]
            target = buffer if into is None else buffer.at[into]
            arrivals.append((buffer, pltpu.make_async_copy(view, target, sems.at[k])))
        for k, (target, buffer, out) in enumerate(zip(targets, buffers_out, outs)):
            view = target if out[2] is None else target.at[out[2]]
            departures.append((buffer, pltpu.make_async_copy(buffer, view, sems.at[n_in + k])))
        flow = Flow(arrivals, departures)
        body(flow, s_ref, *buffers_in, *buffers_out, *rest)
        flow.end()

    anywhere = pl.BlockSpec(memory_space=pl.ANY)
    return pl.pallas_call(
        run,
        name=name,
        out_shape=[jax.ShapeDtypeStruct(o[0], o[1]) for o in outs],
        grid_spec=pltpu.PrefetchScalarGridSpec(
            num_scalar_prefetch=1,
            grid=(1,),
            in_specs=[anywhere] * (n_in + len(held)),
            out_specs=[anywhere] * n_out,
            scratch_shapes=[pltpu.VMEM(dims, dtype) for dims, dtype in buffer_shapes]
            + [pltpu.VMEM(o[3], o[1]) for o in outs]
            + scratch
            + [pltpu.SemaphoreType.DMA((n_in + n_out,))],
        ),
        input_output_aliases={1 + n_in + k: n_out - len(held) + k for k in range(len(held))},
        compiler_params=pltpu.CompilerParams(vmem_limit_bytes=VMEM_LIMIT),
        cost_estimate=pl.CostEstimate(flops=flops, bytes_accessed=10**6, transcendentals=0),
    )(scalars, *[i[0] for i in ins], *held)


def slices_out(slots, slot, share, tokens):
    return ((2, slots, share, tokens), BF, (slice(None), pl.ds(PAIR * slot, PAIR)), (2, PAIR, share, tokens))


def whole(array):
    return (array, None, None)


def stacked(arrays):
    rows = arrays[0].shape[0]
    return [(v, None, (pl.ds(k * rows, rows),)) for k, v in enumerate(arrays)]


def whole_out(dims, dtype):
    return (dims, dtype, None, dims)


def pair_of(array, pair):
    return (array, (pl.ds(PAIR * pair, PAIR),), None)


def split_low(v):
    high = v.astype(BF)
    return high, (v - high.astype(F32)).astype(BF)


def rows_product(a, b):
    (ah, al), (bh, bl) = split_low(a), split_low(b)
    return dot_tn(jnp.concatenate([ah, al, ah], 0), jnp.concatenate([bh, bh, bl], 0))


def back_product(a, weight):
    (ah, al), (wh, wl) = split_low(a), split_low(weight)
    return dot_nt(ah, wh) + dot_nt(al, wh) + dot_nt(ah, wl)


def product(a, weight):
    (ah, al), (wh, wl) = split_low(a), split_low(weight)
    return dot(ah, wh) + dot(al, wh) + dot(ah, wl)


def silu(v):
    return v / (1.0 + jnp.exp(-v))


def silu_slope(v):
    gate = 1.0 / (1.0 + jnp.exp(-v))
    return gate * (1.0 + v * (1.0 - gate))


def row_blocks(source, target, sems, rows):
    return [
        pltpu.make_async_copy(source.at[pl.ds(at, rows)], target.at[pl.ds(at, rows)], sems.at[at // rows])
        for at in range(0, source.shape[0], rows)
    ]


def condition_body(
    embedded, bias, time_in, time_out, ada, mod_out, inner_pre, inner, outer_pre, outer, held_in, held_out, held, sums, parts, sems,
):
    depth = ada.shape[0]
    per_dev, count, width = mod_out.shape
    first = pltpu.make_async_copy(time_in, held_in, sems.at[0])
    second = pltpu.make_async_copy(time_out, held_out, sems.at[1])
    blocks = row_blocks(ada, held, sems.at[pl.ds(2, depth // WEIGHT_ROWS)], WEIGHT_ROWS)
    for copy in [first, second] + blocks:
        copy.start()
    first.wait()
    inner_pre[...] = product(embedded[...], held_in[...])
    inner[...] = silu(inner_pre[...])
    second.wait()
    outer_pre[...] = product(inner[...], held_out[...])
    outer[...] = silu(outer_pre[...])
    wide_bias = [jnp.concatenate([bias[k + j : k + j + 1, :] for j in range(width // LANES)], 1)
                 for k in range(0, bias.shape[0], width // LANES)]
    total = jnp.concatenate(wide_bias, 1)
    sums[...] = jnp.broadcast_to(total, sums.shape)
    for k in range(depth // WEIGHT_ROWS):
        parts[k] = outer[0:8, k * WEIGHT_ROWS : (k + 1) * WEIGHT_ROWS]

    def add(k, carry):
        rows = pl.ds(pl.multiple_of(k * WEIGHT_ROWS, WEIGHT_ROWS), WEIGHT_ROWS)
        pltpu.make_async_copy(ada.at[rows], held.at[rows], sems.at[2 + k]).wait()
        sums[...] += product(parts[k], held[rows, :])
        return carry

    lax.fori_loop(0, depth // WEIGHT_ROWS, add, 0)
    total = sums[...]
    for lat in range(per_dev):
        for k in range(count):
            mod_out[lat, k : k + 1, :] = total[lat : lat + 1, k * width : (k + 1) * width]


def condition(embedded, time_in, time_out, ada_weight, ada_bias, per_dev, width):
    latent_total = embedded.shape[0]
    depth, columns = ada_weight.shape
    vmem = pl.BlockSpec(memory_space=pltpu.VMEM)
    anywhere = pl.BlockSpec(memory_space=pl.ANY)
    rows = jax.ShapeDtypeStruct((latent_total, depth), F32)
    return pl.pallas_call(
        condition_body,
        name="condition",
        in_specs=[vmem, vmem, anywhere, anywhere, anywhere],
        out_specs=[vmem] * 5,
        out_shape=[jax.ShapeDtypeStruct((per_dev, columns // width, width), F32), rows, rows, rows, rows],
        scratch_shapes=[
            pltpu.VMEM(time_in.shape, F32),
            pltpu.VMEM(time_out.shape, F32),
            pltpu.VMEM(ada_weight.shape, F32),
            pltpu.VMEM((8, columns), F32),
            pltpu.VMEM((depth // WEIGHT_ROWS, 8, WEIGHT_ROWS), F32),
            pltpu.SemaphoreType.DMA((2 + depth // WEIGHT_ROWS,)),
        ],
        compiler_params=pltpu.CompilerParams(vmem_limit_bytes=VMEM_LIMIT),
        cost_estimate=pl.CostEstimate(flops=8 * 10**9, bytes_accessed=10**6, transcendentals=0),
    )(embedded, ada_bias.reshape(columns // LANES, LANES), time_in, time_out, ada_weight)


def condition_back_body(
    factor, gmod, embedded, inner_pre, inner, outer_pre, outer, time_out, ada,
    time_in_grad, time_out_grad, ada_grad, held_out, held, outer_grad, columns, sems, arriving, leaving,
):
    count = ada.shape[0] // BACK_ROWS

    def block_copy(source, target, sem, k):
        rows = pl.ds(k * BACK_ROWS, BACK_ROWS)
        return pltpu.make_async_copy(source.at[rows], target.at[rows], sem.at[k])

    first = pltpu.make_async_copy(time_out, held_out, sems.at[0])
    for k in range(count):
        block_copy(ada, held, arriving, k).start()
    first.start()
    high, low = split_low(outer[...])
    both = jnp.concatenate([high, low], 0)
    for k in range(count):
        columns[k] = both[:, k * BACK_ROWS : (k + 1) * BACK_ROWS]

    def block(k, carry):
        rows = pl.ds(pl.multiple_of(k * BACK_ROWS, BACK_ROWS), BACK_ROWS)
        block_copy(ada, held, arriving, k).wait()
        grads = gmod[...]
        high, low = split_low(held[rows, :])
        outer_grad[rows, :] = dot_nt(high, grads) + dot_nt(low, grads)
        held[rows, :] = dot_tn(columns[k], jnp.concatenate([grads, grads], 0)) * factor
        block_copy(held, ada_grad, leaving, k).start()
        return carry

    lax.fori_loop(0, count, block, 0)
    first.wait()
    back = outer_grad[...].T * factor * silu_slope(outer_pre[...])
    time_out_grad[...] = rows_product(inner[...], back)
    back = back_product(back, held_out[...]) * silu_slope(inner_pre[...])
    time_in_grad[...] = rows_product(embedded[...], back)
    for k in range(count):
        block_copy(held, ada_grad, leaving, k).wait()


def condition_back(gmod, embedded, stages, time_out, ada_weight, factor):
    depth = ada_weight.shape[0]
    latent_total = gmod.shape[0]
    vmem = pl.BlockSpec(memory_space=pltpu.VMEM)
    anywhere = pl.BlockSpec(memory_space=pl.ANY)
    time_in_dims = (embedded.shape[1], time_out.shape[0])
    return pl.pallas_call(
        functools.partial(condition_back_body, factor),
        name="condition_back",
        in_specs=[vmem] * 6 + [anywhere] * 2,
        out_specs=[vmem, vmem, anywhere],
        out_shape=[
            jax.ShapeDtypeStruct(time_in_dims, F32),
            jax.ShapeDtypeStruct(time_out.shape, F32),
            jax.ShapeDtypeStruct(ada_weight.shape, F32),
        ],
        scratch_shapes=[
            pltpu.VMEM(time_out.shape, F32),
            pltpu.VMEM(ada_weight.shape, F32),
            pltpu.VMEM((depth, latent_total), F32),
            pltpu.VMEM((depth // BACK_ROWS, 2 * latent_total, BACK_ROWS), BF),
            pltpu.SemaphoreType.DMA((1,)),
            pltpu.SemaphoreType.DMA((depth // BACK_ROWS,)),
            pltpu.SemaphoreType.DMA((depth // BACK_ROWS,)),
        ],
        compiler_params=pltpu.CompilerParams(vmem_limit_bytes=VMEM_LIMIT),
        cost_estimate=pl.CostEstimate(flops=1, bytes_accessed=1, transcendentals=0),
    )(gmod, embedded, *stages, time_out, ada_weight)


def attn_forward(scalars, pair, x_parts, mod, attn_kernel, qkv_weight, out_weight):
    _, share, tokens = x_parts[0].shape
    width = out_weight.shape[1]
    rows = PAIR * tokens
    thin = whole_out((rows, share), BF)
    half = whole_out((tokens, width), BF)
    return call(
        attn_kernel_body, "attn_fwd", scalars,
        [pair_of(v, pair) for v in x_parts] + [pair_of(mod, pair), whole(attn_kernel), whole(qkv_weight), whole(out_weight)],
        [whole_out((rows, width), BF), whole_out((rows, width), BF), thin, thin, thin, thin, half, half],
        [pltpu.VMEM((4, share, tokens), BF), pltpu.VMEM((PAIR * (tokens + 2 * SIDE), width), F32)],
        6_000_000_000,
    )


def feed_forward(scalars, pair, full, att, g_parts, mod, up_weight, down_weight, ffn_kernel, slots, taps, held):
    _, share, tokens = g_parts[0].shape
    width, units = up_weight.shape
    rows = PAIR * tokens
    tall = PAIR * (tokens + 2 * SIDE)
    broad = whole_out((rows, width), BF)
    hidden = whole_out((rows, units), BF)
    half = whole_out((tokens, width), BF)
    slices = slices_out(slots, pair, share, tokens)
    return call(
        functools.partial(ffn_kernel_body, pair == 0), "ffn", scalars,
        [pair_of(v, pair) for v in g_parts] + [whole(full)] + stacked(att)
        + [pair_of(mod, pair), whole(up_weight), whole(down_weight), whole(ffn_kernel), whole(taps)],
        [broad, broad, hidden, broad, hidden, half, half, whole_out((PAIR, 1, width), F32), whole_out((16, units), F32),
         slices, slices],
        [pltpu.VMEM((4, share, tokens), BF), pltpu.VMEM((tall, units), F32), pltpu.VMEM((rows, units), F32),
         pltpu.VMEM((tall, units), F32), pltpu.VMEM((rows, width), F32), pltpu.VMEM((rows, width), F32),
         pltpu.VMEM((rows, width), BF), pltpu.VMEM((PAIR, 8, width), F32), pltpu.VMEM((width, tokens), BF)],
        10_000_000_000, held,
    )


def attn_backward(scalars, pair, full, att, gsec, gfull, mod, qkv, out_weight, gates):
    tokens, width = att[0].shape
    share = out_weight.shape[0]
    rows = PAIR * tokens
    broad = whole_out((rows, width), BF)
    return call(
        attn_back_body, "attn_bwd", scalars,
        [whole(full)] + stacked(att) + stacked(gsec) + [whole(gfull), pair_of(mod, pair)]
        + [whole(v) for v in qkv] + [whole(out_weight), whole(gates)],
        [broad, whole_out((rows, 3 * share), BF), broad, whole_out((PAIR, 8, width), F32)],
        [pltpu.VMEM((3 * PAIR, 8, width), F32), pltpu.VMEM((rows, share), BF)],
        6_000_000_000,
    )


def input_backward(scalars, pair, full, mod, gqkv, qkv_weight, attn_kernel, taps, gmid, mods_in, before, slots, held):
    rows, width = full.shape
    tokens = rows // PAIR
    share = gqkv.shape[1] // 3
    tall = PAIR * (tokens + 2 * SIDE)
    slices = slices_out(slots, slots // PAIR // 2 + pair, share, tokens)
    closing = pair > 0
    mods = whole_out((PACKED, width), BF) if closing else whole_out((PAIR, 8, width), F32)
    return call(
        functools.partial(input_back_body, closing), "input_bwd", scalars,
        [whole(full), pair_of(mod, pair), whole(gqkv), whole(qkv_weight), whole(attn_kernel), whole(taps), whole(gmid),
         whole(mods_in), whole(before)],
        [whole_out((16, width), F32), mods, slices, slices],
        [pltpu.VMEM((rows, width), F32), pltpu.VMEM((rows, LANES), F32), pltpu.VMEM((tall, width), F32),
         pltpu.VMEM((tall, width), F32), pltpu.VMEM((rows, width), F32), pltpu.VMEM((rows, width), BF),
         pltpu.VMEM((PAIR, 8, width), F32), pltpu.VMEM((PACKED, width), F32), pltpu.VMEM((width, tokens), BF)],
        6_000_000_000, held,
    )


def core_swap(v):
    return lax.ppermute(v, "narrow", [(0, 1), (1, 0), (2, 3), (3, 2)])


def x_swap(v):
    return lax.ppermute(v, "narrow", [(0, 2), (2, 0), (1, 3), (3, 1)])


def sum_pair(a, b):
    return (a.astype(F32) + b.astype(F32)).astype(BF)


def slice_halves(x, keep, arrived):
    both = sum_pair(keep, arrived)
    return (
        lax.dynamic_index_in_dim(both, x, 0, keepdims=False),
        lax.dynamic_index_in_dim(both, 1 - x, 0, keepdims=False),
    )


def wide_swap(v, bit, count):
    return lax.ppermute(v, "wide", [(i, i ^ bit) for i in range(count)])


def pick(v, parts, at):
    rows = v.shape[0] // parts
    return lax.dynamic_slice_in_dim(v, at * rows, rows, 0)


def in_place(bit, own, came, axis):
    dims = own.shape[:axis] + (2,) + own.shape[axis + 1 :]
    return jnp.where(lax.broadcasted_iota(jnp.int32, dims, axis) == bit, own, came)


class WideSum:
    def __init__(self, product, at, count, back=None):
        self.count, self.dims = count, product.shape
        self.levels = count.bit_length() - 1
        self.bits = [at // (1 << k) % 2 for k in range(self.levels)]
        self.ahead = list(range(self.levels))
        self.back = list(reversed(self.ahead)) if back is None else back
        self.opened = False
        self.held = product

    def swap(self, sent, level):
        self.came = wide_swap(sent, 1 << level, self.count)

    def halve(self, held, came):
        level = self.ahead[0]
        if level == 0:
            held = pick(held, 2, self.bits[0])
        if len(self.ahead) == 1:
            return (sum_pair(held, came),)
        bit = self.bits[level + 1]
        return tuple(sum_pair(pick(held, 2, at), pick(came, 2, at)) for at in (1 - bit, bit))

    def pending(self):
        if not self.opened:
            return lambda v: pick(v, 2, 1 - self.bits[0]), (self.held,)
        if self.ahead:
            return self.halve, (self.held, self.came)
        level = self.back[0]
        return lambda a, b: in_place(self.bits[level], a, b, level), (self.held, self.came)

    def accept(self, out):
        if not self.opened:
            self.opened = True
            self.swap(out, 0)
        elif self.ahead:
            self.ahead.pop(0)
            self.held = out[-1]
            if self.ahead:
                self.swap(out[0], self.ahead[0])
            else:
                self.held = self.held.reshape((1,) * self.levels + self.held.shape)
                self.swap(self.held, self.back[0])
        else:
            self.back.pop(0)
            self.held = out
            self.swap(out, self.back[0])

    def done(self):
        return self.opened and not self.ahead and len(self.back) == 1

    def finish(self, order, shape=lambda v: v):
        level = self.back[0]
        return order(
            lambda a, b: shape(in_place(self.bits[level], a, b, level).reshape(self.dims)), self.held, self.came
        )


class Steps:
    def __init__(self, came, steps):
        self.came, self.steps = came, list(steps)

    def pending(self):
        return self.steps[0][0], self.came

    def accept(self, out):
        _, move = self.steps.pop(0)
        self.came = move(out)

    def done(self):
        return not self.steps


class Order:
    def __init__(self):
        self.last = ()

    def __call__(self, step, *inputs):
        inputs, _ = lax.optimization_barrier((inputs, self.last))
        out = step(*inputs)
        self.last = tuple(jax.tree.leaves(out)[:1])
        return out

    def advance(self, *chains):
        chains = [c for c in chains if not c.done()]
        if chains:
            work = [c.pending() for c in chains]
            outs = self(lambda *v: [w[0](*a) for w, a in zip(work, v)], *[w[1] for w in work])
            self.last = tuple(jax.tree.leaves(out)[0] for out in outs)
            for chain, out in zip(chains, outs):
                chain.accept(out)


def after(value, *others):
    return lax.optimization_barrier((value, others))[0]


def embed_times(stamps):
    halved = FREQ // 2
    freqs = jnp.exp(-math.log(10000.0) * jnp.arange(halved, dtype=F32) / halved)
    angles = stamps[:, None] * freqs[None, :]
    return jnp.concatenate([jnp.cos(angles), jnp.sin(angles)], 1)


def body(
    latents, cotangent, timesteps, time_in, time_out, ada_weight, ada_bias,
    attn_kernel, qkv_weight, out_weight, up_weight, ffn_kernel, down_weight,
):
    wide_count = lax.axis_size("wide")
    wide_at = lax.axis_index("wide")
    n = lax.axis_index("narrow")
    per_dev, tokens, share = latents.shape
    width = out_weight.shape[1]
    units = up_weight.shape[1]
    latent_total = timesteps.shape[0]
    scalars = n.astype(jnp.int32).reshape(1)

    steps, bit = [0], wide_count // 2
    while bit:
        steps, bit = steps + [k ^ bit for k in steps], bit // 2
    met = jnp.bitwise_xor(jnp.array(steps, jnp.int32), wide_at)
    stamps = timesteps.reshape(wide_count, per_dev)[met].reshape(latent_total).astype(F32)
    embedded = embed_times(stamps)
    mod, *stages = condition(embedded, time_in, time_out, ada_weight, ada_bias, per_dev, width)
    x = n // 2
    factor = 1.0 / latent_total

    def token_product(lefts, rights):
        total = None
        for a, b in zip(lefts, rights):
            part = dot_tn(a, b)
            total = part if total is None else total + part
        return (total * factor).astype(BF)

    x_own = jnp.swapaxes(latents, 1, 2)
    g_own = jnp.swapaxes(cotangent, 1, 2)
    qkv_rows = jnp.swapaxes(qkv_weight, 1, 2)
    qkv_all = qkv_rows.reshape(3 * share, width)
    order = Order()
    x_across = x_swap(x_own)
    x_across = after(x_across, mod)
    g_across = x_swap(after(g_own, x_across))
    x_parts = (x_own, core_swap(x_own), x_across, core_swap(x_across))
    g_parts = (g_own, core_swap(g_own), g_across, core_swap(g_across))

    def attend(pair):
        return lambda parts: attn_forward(scalars, pair, parts, mod, attn_kernel, qkv_rows, out_weight)

    fwd_a = order(attend(0), x_parts)
    here_a = order(sum_pair, fwd_a[6], core_swap(fwd_a[7]))
    fwd_b = order(attend(1), after(x_parts, g_across))
    att_a = order(sum_pair, here_a, x_swap(here_a))
    here_b = order(sum_pair, fwd_b[6], core_swap(fwd_b[7]))
    att_a = (att_a, core_swap(att_a))

    slots = 2 * per_dev

    def feed(pair, full, taps, held=()):
        return lambda att, parts: feed_forward(
            scalars, pair, full, att, parts, mod, up_weight, down_weight, ffn_kernel, slots, taps, held
        )

    ffn_a = order(feed(0, fwd_a[0], ffn_kernel), att_a, g_parts)
    att_b = order(sum_pair, here_b, x_swap(here_b))
    att_b = (att_b, core_swap(att_b))
    here_a = order(sum_pair, ffn_a[5], core_swap(ffn_a[6]))
    ffn_b = order(feed(1, fwd_b[0], ffn_a[8], ffn_a[9:11]), att_b, g_parts)
    sec_a = order(sum_pair, here_a, x_swap(here_a))
    sec_a = (sec_a, core_swap(sec_a))
    down_product = order(token_product, [ffn_a[2], ffn_b[2]], [ffn_a[3], ffn_b[3]])
    down_sum = WideSum(down_product, wide_at, wide_count)
    order.advance(down_sum)
    here_b = order(sum_pair, ffn_b[5], core_swap(ffn_b[6]))
    up_product = order(token_product, [ffn_a[1], ffn_b[1]], [ffn_a[4], ffn_b[4]])
    up_sum = WideSum(up_product, wide_at, wide_count)
    order.advance(up_sum)

    def attend_back(pair, fwd, ffn):
        return lambda att, sec: attn_backward(
            scalars, pair, fwd[0], att, sec, ffn[0], mod, fwd[2:5], out_weight, ffn[7]
        )

    def input_back(pair, fwd, taps, before, held):
        return lambda gqkv, gmid, mods: input_backward(
            scalars, pair, fwd[0], mod, gqkv, qkv_all, attn_kernel, taps, gmid, mods, before, slots, held
        )

    back_a = order(attend_back(0, fwd_a, ffn_a), att_a, sec_a)
    sec_b = order(sum_pair, here_b, x_swap(here_b))
    sec_b = (sec_b, core_swap(sec_b))
    order.advance(down_sum)
    back_b = order(attend_back(1, fwd_b, ffn_b), att_b, sec_b)
    order.advance(down_sum)
    attn_product = order(
        lambda grads, grouped, contexts, attended: jnp.concatenate(
            [token_product(grads, grouped), token_product(contexts, attended)], 0
        ),
        [back_a[1], back_b[1]], [fwd_a[1], fwd_b[1]], [fwd_a[5], fwd_b[5]], [back_a[0], back_b[0]],
    )
    levels = wide_count.bit_length() - 1
    attn_sum = WideSum(attn_product, wide_at, wide_count, [0] + list(range(levels - 1, 0, -1)))
    order.advance(attn_sum)
    order.advance(up_sum)
    order.advance(down_sum)
    in_a = order(input_back(0, fwd_a, attn_kernel, attn_kernel, ffn_b[9:11]), *back_a[1:4])
    order.advance(down_sum, up_sum)
    order.advance(attn_sum)
    in_b = order(input_back(1, fwd_b, in_a[0], in_a[1], in_a[2:4]), *back_b[1:4])
    order.advance(down_sum)

    rows = 6 * per_dev
    bits = [1 << k for k in reversed(range(levels))]
    moves = [lambda v, bit=bit: (v, wide_swap(v, bit, wide_count)) for bit in bits]
    join = lambda a, b: jnp.concatenate([a, b], 0)
    whole_rows = lambda a, b, c: join(sum_pair(a, b)[: rows + 9], c[:9].astype(BF))[None]
    mods = Steps(
        (in_b[1], core_swap(in_b[1])),
        [(sum_pair, lambda v: (v, x_swap(v), ffn_b[8]))]
        + [(work, move) for work, move in zip([whole_rows] + [join] * len(bits), moves)],
    )
    order.advance(up_sum)
    order.advance(mods)
    order.advance(attn_sum)
    order.advance(mods)
    order.advance(up_sum)
    while not down_sum.done():
        order.advance(down_sum)
    down_grad = down_sum.finish(order, lambda v: v.astype(F32))
    order.advance(attn_sum, mods)
    order.advance(mods)
    order.advance(up_sum)
    order.advance(attn_sum)
    made = order(functools.partial(slice_halves, x), in_b[2], core_swap(in_b[3]))
    while not all(c.done() for c in (mods, up_sum)):
        order.advance(mods)
        order.advance(up_sum)

    def unpack(held):
        gmod = held[:, :rows].reshape(latent_total, 6 * width)
        taps = jnp.sum(held[:, rows:].astype(F32), 0) * factor
        return gmod, jnp.sum(gmod.astype(F32), 0) * factor, taps[:9], taps[9:]

    gmod, ada_bias_grad, attn_taps, ffn_taps = order(lambda a, b: unpack(join(a, b)), *mods.came)
    while not attn_sum.done():
        order.advance(attn_sum)
    time_in_grad, time_out_grad, ada_weight_grad = order(
        lambda g: condition_back(g, embedded, stages, time_out, ada_weight, factor), gmod
    )
    up_grad = up_sum.finish(order, lambda v: v.astype(F32))
    finals = order(sum_pair, made[0], x_swap(made[1]))
    qkv_rows_grad, out_grad = attn_sum.finish(order, lambda v: (v[: 3 * share].astype(F32), v[3 * share :].astype(F32)))
    qkv_grad = jnp.swapaxes(qkv_rows_grad.reshape(3, share, width), 1, 2)
    final_out = jnp.swapaxes(finals[:per_dev], 1, 2)
    final_grad = jnp.swapaxes(finals[per_dev:], 1, 2)
    return (
        final_out, final_grad, time_in_grad, time_out_grad, ada_weight_grad, ada_bias_grad,
        attn_taps, qkv_grad, out_grad, up_grad, ffn_taps, down_grad,
    )


def solution(mesh):
    tokens = P("wide", None, "narrow")
    weights = (P(None, None, "narrow"), P("narrow", None), P(None, "narrow"), P(None, "narrow"), P("narrow", None))
    return jax.shard_map(
        body,
        mesh=mesh,
        in_specs=(tokens, tokens, P(), P(), P(), P(), P(), P()) + weights,
        out_specs=(tokens, tokens, P(), P(), P(), P(), P()) + weights,
        check_vma=False,
    )
```

profile of v0, /device:TPU:0, one launch (start us, length us, event | category | flops | bytes accessed | tf_op | source)
XLA Modules:
  0.0 218.5 jit_solution(1037089513071892745)
XLA Ops:
  0.6 3.0 %collective-permute-start.1 = (bf16[4,192,256]{2,1,0:T(8,128)(2,1)}, bf16[4,192,256]{2,1,0:T(8,128)(2,1)S(1)}, u32[]{:S(2)}, u32[]{:S(2)}) collective-permute-start(bf16[4,192,256]{2,1,0:T(8,128)(2,1)} %bitcast.95), channel_id=1, source_target_pairs={{0,2},{2,0},{1,3},{3,1},{4,6},{6,4},{5,7},{7,5},{8,10},{10,8},{9,1... | collective-permute-start | bytes 1179656 | tf_op jit(solution)/shard_map/ppermute | solution.py:847
  6.5 8.6 %condition.1 = (f32[4,6,768]{2,1,0:T(8,128)}, f32[32,768]{1,0:T(8,128)}, f32[32,768]{1,0:T(8,128)}, f32[32,768]{1,0:T(8,128)}, f32[32,768]{1,0:T(8,128)}) custom-call(f32[32,256]{1,0:T(8,128)} %pad_maximum_fusion.1.embedded, f32[36,128]{1,0:T(8,128)} %bitcast.103, f32[256,768]{1,0:T(8,128)} %time_in.1, f32[768,768]{1,0:T(8,128)} %time_out.3, f32[768,4608]{1,0:T(8,128)} %ada.3), custom_call_target="tpu_custom_call" | custom-call | flops 8000000000 | bytes 1000000 | tf_op jit(solution)/shard_map/condition/pallas_call | solution.py:682
  15.8 1.3 collective-permute-done.2.refs_3_
  17.8 8.0 %attn_fwd.2 = (bf16[512,768]{1,0:T(8,128)(2,1)}, bf16[512,768]{1,0:T(8,128)(2,1)}, bf16[512,192]{1,0:T(8,128)(2,1)}, bf16[512,192]{1,0:T(8,128)(2,1)}, bf16[512,...) custom-call(s32[1]{0:T(128)} %bitcast.s_ref, ...), custom_call_target="tpu_custom_call" | custom-call | flops 6000000000 | bytes 1000000 | tf_op jit(solution)/shard_map/attn_fwd/pallas_call | solution.py:563
  26.8 1.0 collective-permute-done.4
  27.9 1.1 add_convert_fusion.9
  29.8 8.0 %attn_fwd.3 = (bf16[512,768]{1,0:T(8,128)(2,1)}, bf16[512,768]{1,0:T(8,128)(2,1)}, bf16[512,192]{1,0:T(8,128)(2,1)}, bf16[512,192]{1,0:T(8,128)(2,1)}, bf16[512,...) custom-call(s32[1]{0:T(128)} %bitcast.s_ref, ...), custom_call_target="tpu_custom_call" | custom-call | flops 6000000000 | bytes 1000000 | tf_op jit(solution)/shard_map/attn_fwd/pallas_call | solution.py:563
  38.5 1.9 collective-permute-done.6
  40.6 1.1 add_convert_fusion.7
  44.1 14.5 %ffn.2 = (bf16[512,768]{1,0:T(8,128)(2,1)}, bf16[512,768]{1,0:T(8,128)(2,1)}, bf16[512,768]{1,0:T(8,128)(2,1)}, bf16[512,768]{1,0:T(8,128)(2,1)}, bf16[512,768]{...) custom-call(s32[1]{0:T(128)} %bitcast.s_ref, ...), custom_call_target="tpu_custom_call" | custom-call | flops 10000000000 | bytes 1000000 | tf_op jit(solution)/shard_map/ffn/pallas_call | solution.py:563
  59.3 1.2 collective-permute-done.12
  60.6 1.1 add_convert_fusion.5
  61.7 1.5 collective-permute-start.14
  63.9 14.8 %ffn.3 = (bf16[512,768]{1,0:T(8,128)(2,1)}, bf16[512,768]{1,0:T(8,128)(2,1)}, bf16[512,768]{1,0:T(8,128)(2,1)}, bf16[512,768]{1,0:T(8,128)(2,1)}, bf16[512,768]{...) custom-call(s32[1]{0:T(128)} %bitcast.s_ref, ...), custom_call_target="tpu_custom_call", output_to_operand_aliasing={{9}: (13, {}), {10}: (14, {})} | custom-call | flops 10000000000 | bytes 1000000 | tf_op jit(solution)/shard_map/ffn/pallas_call | solution.py:563
  82.2 1.6 collective-permute-start.18
  88.4 7.8 %attn_bwd.2 = (bf16[512,768]{1,0:T(8,128)(2,1)}, bf16[512,576]{1,0:T(8,128)(2,1)}, bf16[512,768]{1,0:T(8,128)(2,1)}, f32[2,8,768]{2,1,0:T(8,128)}) custom-call(s32[1]{0:T(128)} %bitcast.s_ref, bf16[512,768]{1,0:T(8,128)(2,1)} %get-tuple-element.213.refs_4_.refs_0_, bf16[256,768]{1,0:T(8,128)(2,1)} %copy-done.17, bf16[256,768]{1,0:T(8,128)(2,1)} %copy-done.29, ...), custom_call_target="tpu_custom_call" | custom-call | flops 6000000000 | bytes 1000000 | tf_op jit(solution)/shard_map/attn_bwd/pallas_call | solution.py:563
  96.2 1.8 add_convert_fusion.2.refs_3_
  99.7 1.6 collective-permute-start.19
  101.3 8.1 %attn_bwd.3 = (bf16[512,768]{1,0:T(8,128)(2,1)}, bf16[512,576]{1,0:T(8,128)(2,1)}, bf16[512,768]{1,0:T(8,128)(2,1)}, f32[2,8,768]{2,1,0:T(8,128)}) custom-call(s32[1]{0:T(128)} %bitcast.s_ref, bf16[512,768]{1,0:T(8,128)(2,1)} %get-tuple-element.220.refs_4_.refs_0_, bf16[256,768]{1,0:T(8,128)(2,1)} %copy-done.16, bf16[256,768]{1,0:T(8,128)(2,1)} %copy-done.27, ...), custom_call_target="tpu_custom_call" | custom-call | flops 6000000000 | bytes 1000000 | tf_op jit(solution)/shard_map/attn_bwd/pallas_call | solution.py:563
  109.5 2.7 %collective-permute-start.21 = (bf16[96,768]{1,0:T(8,128)(2,1)S(1)}, bf16[96,768]{1,0:T(8,128)(2,1)S(1)}, u32[]{:S(2)}, u32[]{:S(2)}) collective-permute-start(bf16[96,768]{1,0:T(8,128)(2,1)S(1)} %get-tuple-element.403), channel_id=1, source_target_pairs={{0,16},{4,20},{8,24},{12,28},{16,0},{20,4},{24,8},{28,12},{1,17},{... | collective-permute-start | bytes 442376 | tf_op jit(solution)/shard_map/ppermute | solution.py:863
  115.9 1.6 collective-permute-start.20
  117.5 2.0 add_convert_fusion.12
  119.5 1.0 collective-permute-start.24
  121.3 9.7 %input_bwd.2 = (f32[16,768]{1,0:T(8,128)}, f32[2,8,768]{2,1,0:T(8,128)}, bf16[2,8,192,256]{3,2,1,0:T(8,128)(2,1)}, bf16[2,8,192,256]{3,2,1,0:T(8,128)(2,1)}) custom-call(s32[1]{0:T(128)} %bitcast.s_ref, bf16[512,768]{1,0:T(8,128)(2,1)} %get-tuple-element.213.refs_4_.refs_0_, ...), custom_call_target="tpu_custom_call", output_to_operand_aliasing={{2}: (10, {}), {3}: (11, {})} | custom-call | flops 6000000000 | bytes 1000000 | tf_op jit(solution)/shard_map/input_bwd/pallas_call | solution.py:563
  131.2 2.1 collective-permute-start.28
  133.4 1.1 collective-permute-start.29
  134.8 1.1 collective-permute-start.26
  135.8 9.7 %input_bwd.3 = (f32[16,768]{1,0:T(8,128)}, bf16[40,768]{1,0:T(8,128)(2,1)}, bf16[2,8,192,256]{3,2,1,0:T(8,128)(2,1)}, bf16[2,8,192,256]{3,2,1,0:T(8,128)(2,1)}) custom-call(s32[1]{0:T(128)} %bitcast.s_ref, bf16[512,768]{1,0:T(8,128)(2,1)} %get-tuple-element.220.refs_4_.refs_0_, ...), custom_call_target="tpu_custom_call", output_to_operand_aliasing={{2}: (10, {}), {3}: (11, {})} | custom-call | flops 6000000000 | bytes 1000000 | tf_op jit(solution)/shard_map/input_bwd/pallas_call | solution.py:563
  146.9 1.4 collective-permute-start.34
  148.3 1.5 collective-permute-start.31
  149.9 1.6 collective-permute-start.30
  151.6 1.0 collective-permute-done.31
  152.7 1.7 collective-permute-start.32
  154.3 7.6 %collective-permute-done.34 = bf16[1,1,1,96,768]{4,3,2,1,0:T(8,128)(2,1)S(1)} collective-permute-done((bf16[1,1,1,96,768]{4,3,2,1,0:T(8,128)(2,1)S(1)}, bf16[1,1,1,96,768]{4,3,2,1,0:T(8,128)(2,1)S(1)}, u32[]{:S(2)}, u32[]{:S(2)}) %collective-permute-start.34) | collective-permute-done | bytes 147488 | tf_op jit(solution)/shard_map/ppermute | solution.py:863
  162.1 1.6 fusion.3
  163.7 2.4 %collective-permute-done.32 = bf16[1,42,768]{2,1,0:T(8,128)(2,1)S(1)} collective-permute-done((bf16[1,42,768]{2,1,0:T(8,128)(2,1)S(1)}, bf16[1,42,768]{2,1,0:T(8,128)(2,1)S(1)}, u32[]{:S(2)}, u32[]{:S(2)}) %collective-permute-start.32) | collective-permute-done | bytes 64544 | tf_op jit(solution)/shard_map/ppermute | solution.py:863
  166.3 1.6 collective-permute-start.35
  167.9 7.6 %collective-permute-done.37 = bf16[2,42,768]{2,1,0:T(8,128)(2,1)S(1)} collective-permute-done((bf16[2,42,768]{2,1,0:T(8,128)(2,1)S(1)}, bf16[2,42,768]{2,1,0:T(8,128)(2,1)S(1)}, u32[]{:S(2)}, u32[]{:S(2)}) %collective-permute-start.37) | collective-permute-done | bytes 129056 | tf_op jit(solution)/shard_map/ppermute | solution.py:863
  175.6 1.6 collective-permute-start.40
  178.6 1.0 dynamic-slice_bitcast_fusion
  179.6 5.9 %collective-permute-done.40 = bf16[4,42,768]{2,1,0:T(8,128)(2,1)S(1)} collective-permute-done((bf16[4,42,768]{2,1,0:T(8,128)(2,1)S(1)}, bf16[4,42,768]{2,1,0:T(8,128)(2,1)S(1)}, u32[]{:S(2)}, u32[]{:S(2)}) %collective-permute-start.40) | collective-permute-done | bytes 258080 | tf_op jit(solution)/shard_map/ppermute | solution.py:863
  185.9 7.1 %collective-permute-done.41 = bf16[2,1,1,96,768]{4,3,0,2,1:T(8,128)(2,1)S(1)} collective-permute-done((bf16[2,1,1,96,768]{4,3,0,2,1:T(8,128)(2,1)S(1)}, bf16[2,1,1,96,768]{4,3,0,2,1:T(8,128)(2,1)S(1)}, u32[]{:S(2)}, u32[]{:S(2)}) %collective-permute-start.41) | collective-permute-done | bytes 294944 | tf_op jit(solution)/shard_map/ppermute | solution.py:863
  193.2 1.5 collective-permute-start.38
  195.4 15.0 %condition_back.1 = (f32[256,768]{1,0:T(8,128)}, f32[768,768]{1,0:T(8,128)}, f32[768,4608]{1,0:T(8,128)}) custom-call(bf16[32,4608]{1,0:T(8,128)(2,1)} %copy-done, f32[32,256]{1,0:T(8,128)} %pad_maximum_fusion.1.embedded, f32[32,768]{1,0:T(8,128)} %get-tuple-element.375.inner_pre, f32[32,768]{1,0:T(8,128)} %get-tuple-element.376.inner, ...), custom_call_target="tpu_custom_call" | custom-call | flops 1 | bytes 1 | tf_op jit(solution)/shard_map/condition_back/pallas_call | solution.py:746
  210.5 2.7 %fusion.2 = f32[768,768]{1,0:T(8,128)} fusion(pred[768]{0:T(1024)(128)(4,1)S(1)} %iota.57, bf16[2,2,96,768]{3,2,1,0:T(8,128)(2,1)} %bitcast.30, bf16[2,2,96,768]{3,2,1,0:T(8,128)(2,1)S(1)} %bitcast.75), kind=kLoop, calls=%fused_computation.13 | loop fusion | flops 1179648 | bytes 3539712 | tf_op jit(solution)/shard_map/convert_element_type | solution.py:1123
  214.0 1.3 bitcast_select_fusion
  216.2 0.9 slice_bitcast_fusion
  217.2 1.3 convert_bitcast_fusion
  (198 shorter events, 31.5 us)
Async XLA Ops:
  0.6 14.5 %collective-permute-start.1 = (bf16[4,192,256]{2,1,0:T(8,128)(2,1)}, bf16[4,192,256]{2,1,0:T(8,128)(2,1)S(1)}, u32[]{:S(2)}, u32[]{:S(2)}) collective-permute-start(bf16[4,192,256]{2,1,0:T(8,128)(2,1)} %bitcast.95), channel_id=1, source_target_pairs={{0,2},{2,0},{1,3},{3,1},{4,6},{6,4},{5,7},{7,5},{8,10},{10,8},{9,1... | collective-permute-start | bytes 1179656 | tf_op jit(solution)/shard_map/ppermute | solution.py:847
  3.6 12.2 %collective-permute-start = (bf16[4,192,256]{2,1,0:T(8,128)(2,1)}, bf16[4,192,256]{2,1,0:T(8,128)(2,1)S(1)}, u32[]{:S(2)}, u32[]{:S(2)}) collective-permute-start(bf16[4,192,256]{2,1,0:T(8,128)(2,1)} %bitcast.96), channel_id=1, source_target_pairs={{0,1},{1,0},{2,3},{3,2},{4,5},{5,4},{6,7},{7,6},{8,9},{9,8},{10,11... | collective-permute-start | bytes 1179656 | tf_op jit(solution)/shard_map/ppermute | solution.py:843
  15.2 1.9 collective-permute-start.2
  15.7 11.1 %collective-permute-start.3 = (bf16[4,192,256]{2,1,0:T(8,128)(2,1)S(1)}, bf16[4,192,256]{2,1,0:T(8,128)(2,1)S(1)}, u32[]{:S(2)}, u32[]{:S(2)}) collective-permute-start(bf16[4,192,256]{2,1,0:T(8,128)(2,1)S(1)} %bitcast.101), channel_id=1, source_target_pairs={{0,2},{2,0},{1,3},{3,1},{4,6},{6,4},{5,7},{7,5},{8,10},{10,8},{9,1... | collective-permute-start | bytes 1179656 | tf_op jit(solution)/shard_map/ppermute | solution.py:847
  25.9 2.0 collective-permute-start.4
  26.8 11.6 %copy-start.28 = (bf16[4,192,256]{2,1,0:T(8,128)(2,1)}, bf16[4,192,256]{2,1,0:T(8,128)(2,1)S(1)}, u32[]{:S(2)}) copy-start(bf16[4,192,256]{2,1,0:T(8,128)(2,1)S(1)} %collective-permute-done.3.refs_2_) | copy-start | bytes 1179652
  29.0 11.5 %collective-permute-start.6 = (bf16[256,768]{1,0:T(8,128)(2,1)S(1)}, bf16[256,768]{1,0:T(8,128)(2,1)S(1)}, u32[]{:S(2)}, u32[]{:S(2)}) collective-permute-start(bf16[256,768]{1,0:T(8,128)(2,1)S(1)} %add_convert_fusion.9), channel_id=1, source_target_pairs={{0,2},{2,0},{1,3},{3,1},{4,6},{6,4},{5,7},{7,5},{8,10},{10,8},{9,1... | collective-permute-start | bytes 1179656 | tf_op jit(solution)/shard_map/ppermute | solution.py:847
  37.9 2.7 %collective-permute-start.5 = (bf16[256,768]{1,0:T(8,128)(2,1)}, bf16[256,768]{1,0:T(8,128)(2,1)S(1)}, u32[]{:S(2)}, u32[]{:S(2)}) collective-permute-start(bf16[256,768]{1,0:T(8,128)(2,1)} %get-tuple-element.222), channel_id=1, source_target_pairs={{0,1},{1,0},{2,3},{3,2},{4,5},{5,4},{6,7},{7,6},{8,9},{9,8},{10,11... | collective-permute-start | bytes 1179656 | tf_op jit(solution)/shard_map/ppermute | solution.py:843
  38.0 4.4 %collective-permute-start.9 = (bf16[4,192,256]{2,1,0:T(8,128)(2,1)S(1)}, bf16[4,192,256]{2,1,0:T(8,128)(2,1)S(1)}, u32[]{:S(2)}, u32[]{:S(2)}) collective-permute-start(bf16[4,192,256]{2,1,0:T(8,128)(2,1)S(1)} %bitcast.102), channel_id=1, source_target_pairs={{0,1},{1,0},{2,3},{3,2},{4,5},{5,4},{6,7},{7,6},{8,9},{9,8},{10,11... | collective-permute-start | bytes 1179656 | tf_op jit(solution)/shard_map/ppermute | solution.py:843
  38.5 3.9 %collective-permute-start.10 = (bf16[4,192,256]{2,1,0:T(8,128)(2,1)S(1)}, bf16[4,192,256]{2,1,0:T(8,128)(2,1)S(1)}, u32[]{:S(2)}, u32[]{:S(2)}) collective-permute-start(bf16[4,192,256]{2,1,0:T(8,128)(2,1)S(1)} %collective-permute-done.3.refs_2_), channel_id=1, source_target_pairs={{0,1},{1,0},{2,3},{3,2},{4,5},{5,4},{6,7},{7,6},{8,9},{9,8},{10,11... | collective-permute-start | bytes 1179656 | tf_op jit(solution)/shard_map/ppermute | solution.py:843
  40.5 1.9 collective-permute-start.8
  41.8 17.1 %collective-permute-start.7 = (bf16[256,768]{1,0:T(8,128)(2,1)S(1)}, bf16[256,768]{1,0:T(8,128)(2,1)S(1)}, u32[]{:S(2)}, u32[]{:S(2)}) collective-permute-start(bf16[256,768]{1,0:T(8,128)(2,1)S(1)} %add_convert_fusion.7), channel_id=1, source_target_pairs={{0,2},{2,0},{1,3},{3,1},{4,6},{6,4},{5,7},{7,5},{8,10},{10,8},{9,1... | collective-permute-start | bytes 1179656 | tf_op jit(solution)/shard_map/ppermute | solution.py:847
  58.6 2.0 collective-permute-start.12
  58.9 4.3 %collective-permute-start.11 = (bf16[256,768]{1,0:T(8,128)(2,1)S(1)}, bf16[256,768]{1,0:T(8,128)(2,1)S(1)}, u32[]{:S(2)}, u32[]{:S(2)}) collective-permute-start(bf16[256,768]{1,0:T(8,128)(2,1)S(1)} %add_convert_fusion.6.refs_5_.refs_1_), channel_id=1, source_target_pairs={{0,1},{1,0},{2,3},{3,2},{4,5},{5,4},{6,7},{7,6},{8,9},{9,8},{10,11... | collective-permute-start | bytes 1179656 | tf_op jit(solution)/shard_map/ppermute | solution.py:843
  61.7 17.1 %collective-permute-start.14 = (bf16[256,768]{1,0:T(8,128)(2,1)S(1)}, bf16[256,768]{1,0:T(8,128)(2,1)S(1)}, u32[]{:S(2)}, u32[]{:S(2)}) collective-permute-start(bf16[256,768]{1,0:T(8,128)(2,1)S(1)} %add_convert_fusion.5), channel_id=1, source_target_pairs={{0,2},{2,0},{1,3},{3,1},{4,6},{6,4},{5,7},{7,5},{8,10},{10,8},{9,1... | collective-permute-start | bytes 1179656 | tf_op jit(solution)/shard_map/ppermute | solution.py:847
  63.9 15.6 %copy-start.13 = (bf16[512,768]{1,0:T(8,128)(2,1)S(1)}, bf16[512,768]{1,0:T(8,128)(2,1)}, u32[]{:S(2)}) copy-start(bf16[512,768]{1,0:T(8,128)(2,1)} %get-tuple-element.259) | copy-start | bytes 2359300
  78.7 5.0 %collective-permute-start.13 = (bf16[256,768]{1,0:T(8,128)(2,1)}, bf16[256,768]{1,0:T(8,128)(2,1)S(1)}, u32[]{:S(2)}, u32[]{:S(2)}) collective-permute-start(bf16[256,768]{1,0:T(8,128)(2,1)} %get-tuple-element.250), channel_id=1, source_target_pairs={{0,1},{1,0},{2,3},{3,2},{4,5},{5,4},{6,7},{7,6},{8,9},{9,8},{10,11... | collective-permute-start | bytes 1179656 | tf_op jit(solution)/shard_map/ppermute | solution.py:843
  78.9 8.7 %collective-permute-start.16 = (bf16[256,768]{1,0:T(8,128)(2,1)S(1)}, bf16[256,768]{1,0:T(8,128)(2,1)S(1)}, u32[]{:S(2)}, u32[]{:S(2)}) collective-permute-start(bf16[256,768]{1,0:T(8,128)(2,1)S(1)} %add_convert_fusion.4.refs_3_), channel_id=1, source_target_pairs={{0,1},{1,0},{2,3},{3,2},{4,5},{5,4},{6,7},{7,6},{8,9},{9,8},{10,11... | collective-permute-start | bytes 1179656 | tf_op jit(solution)/shard_map/ppermute | solution.py:843
  82.2 17.3 %collective-permute-start.18 = (bf16[384,768]{1,0:T(8,128)(2,1)S(1)}, bf16[384,768]{1,0:T(8,128)(2,1)S(1)}, u32[]{:S(2)}, u32[]{:S(2)}) collective-permute-start(bf16[384,768]{1,0:T(8,128)(2,1)S(1)} %constant_dynamic-slice_fusion.2), channel_id=1, source_target_pairs={{0,4},{4,0},{8,12},{12,8},{16,20},{20,16},{24,28},{28,24},{1,5},{5... | collective-permute-start | bytes 1769480 | tf_op jit(solution)/shard_map/ppermute | solution.py:863
  83.9 12.3 %collective-permute-start.15 = (bf16[256,768]{1,0:T(8,128)(2,1)S(1)}, bf16[256,768]{1,0:T(8,128)(2,1)}, u32[]{:S(2)}, u32[]{:S(2)}) collective-permute-start(bf16[256,768]{1,0:T(8,128)(2,1)S(1)} %add_convert_fusion.3), channel_id=1, source_target_pairs={{0,2},{2,0},{1,3},{3,1},{4,6},{6,4},{5,7},{7,5},{8,10},{10,8},{9,1... | collective-permute-start | bytes 1179656 | tf_op jit(solution)/shard_map/ppermute | solution.py:847
  98.0 3.3 %collective-permute-start.17 = (bf16[256,768]{1,0:T(8,128)(2,1)}, bf16[256,768]{1,0:T(8,128)(2,1)}, u32[]{:S(2)}, u32[]{:S(2)}) collective-permute-start(bf16[256,768]{1,0:T(8,128)(2,1)} %add_convert_fusion.2.refs_3_), channel_id=1, source_target_pairs={{0,1},{1,0},{2,3},{3,2},{4,5},{5,4},{6,7},{7,6},{8,9},{9,8},{10,11... | collective-permute-start | bytes 1179656 | tf_op jit(solution)/shard_map/ppermute | solution.py:843
  98.9 18.6 %collective-permute-start.22 = (bf16[384,768]{1,0:T(8,128)(2,1)}, bf16[384,768]{1,0:T(8,128)(2,1)}, u32[]{:S(2)}, u32[]{:S(2)}) collective-permute-start(bf16[384,768]{1,0:T(8,128)(2,1)} %constant_dynamic-slice_fusion.1), channel_id=1, source_target_pairs={{0,4},{4,0},{8,12},{12,8},{16,20},{20,16},{24,28},{28,24},{1,5},{5... | collective-permute-start | bytes 1769480 | tf_op jit(solution)/shard_map/ppermute | solution.py:863
  99.7 9.8 %collective-permute-start.19 = (bf16[192,768]{1,0:T(8,128)(2,1)S(1)}, bf16[192,768]{1,0:T(8,128)(2,1)S(1)}, u32[]{:S(2)}, u32[]{:S(2)}) collective-permute-start(bf16[192,768]{1,0:T(8,128)(2,1)S(1)} %get-tuple-element.393), channel_id=1, source_target_pairs={{0,8},{4,12},{8,0},{12,4},{16,24},{20,28},{24,16},{28,20},{1,9},{5... | collective-permute-start | bytes 884744 | tf_op jit(solution)/shard_map/ppermute | solution.py:863
  101.3 10.9 %copy-start.20 = (bf16[512,192]{1,0:T(8,128)(2,1)S(1)}, bf16[512,192]{1,0:T(8,128)(2,1)}, u32[]{:S(2)}) copy-start(bf16[512,192]{1,0:T(8,128)(2,1)} %get-tuple-element.310) | copy-start | bytes 589828
  109.5 10.9 %collective-permute-start.21 = (bf16[96,768]{1,0:T(8,128)(2,1)S(1)}, bf16[96,768]{1,0:T(8,128)(2,1)S(1)}, u32[]{:S(2)}, u32[]{:S(2)}) collective-permute-start(bf16[96,768]{1,0:T(8,128)(2,1)S(1)} %get-tuple-element.403), channel_id=1, source_target_pairs={{0,16},{4,20},{8,24},{12,28},{16,0},{20,4},{24,8},{28,12},{1,17},{... | collective-permute-start | bytes 442376 | tf_op jit(solution)/shard_map/ppermute | solution.py:863
  115.9 18.6 %collective-permute-start.20 = (bf16[384,768]{1,0:T(8,128)(2,1)S(1)}, bf16[384,768]{1,0:T(8,128)(2,1)S(1)}, u32[]{:S(2)}, u32[]{:S(2)}) collective-permute-start(bf16[384,768]{1,0:T(8,128)(2,1)S(1)} %constant_dynamic-slice_fusion), channel_id=1, source_target_pairs={{0,4},{4,0},{8,12},{12,8},{16,20},{20,16},{24,28},{28,24},{1,5},{5... | collective-permute-start | bytes 1769480 | tf_op jit(solution)/shard_map/ppermute | solution.py:863
  119.5 11.7 %collective-permute-start.24 = (bf16[192,768]{1,0:T(8,128)(2,1)}, bf16[192,768]{1,0:T(8,128)(2,1)S(1)}, u32[]{:S(2)}, u32[]{:S(2)}) collective-permute-start(bf16[192,768]{1,0:T(8,128)(2,1)} %get-tuple-element.391), channel_id=1, source_target_pairs={{0,8},{4,12},{8,0},{12,4},{16,24},{20,28},{24,16},{28,20},{1,9},{5... | collective-permute-start | bytes 884744 | tf_op jit(solution)/shard_map/ppermute | solution.py:863
  120.5 10.4 %collective-permute-start.23 = (bf16[1,1,1,96,768]{4,3,2,1,0:T(8,128)(2,1)S(1)}, bf16[1,1,1,96,768]{4,3,2,1,0:T(8,128)(2,1)S(1)}, u32[]{:S(2)}, u32[]{:S(2)}) collective-permute-start(bf16[1,1,1,96,768]{4,3,2,1,0:T(8,128)(2,1)S(1)} %bitcast.82), channel_id=1, source_target_pairs={{0,16},{4,20},{8,24},{12,28},{16,0},{20,4},{24,8},{28,12},{1,17},{... | collective-permute-start | bytes 442376 | tf_op jit(solution)/shard_map/ppermute | solution.py:863
  131.2 15.6 %collective-permute-start.28 = (bf16[96,768]{1,0:T(8,128)(2,1)S(1)}, bf16[96,768]{1,0:T(8,128)(2,1)S(1)}, u32[]{:S(2)}, u32[]{:S(2)}) collective-permute-start(bf16[96,768]{1,0:T(8,128)(2,1)S(1)} %get-tuple-element.401), channel_id=1, source_target_pairs={{0,16},{4,20},{8,24},{12,28},{16,0},{20,4},{24,8},{28,12},{1,17},{... | collective-permute-start | bytes 442376 | tf_op jit(solution)/shard_map/ppermute | solution.py:863
  133.4 12.7 %collective-permute-start.29 = (bf16[1,1,2,96,768]{4,3,2,1,0:T(8,128)(2,1)S(1)}, bf16[1,1,2,96,768]{4,3,2,1,0:T(8,128)(2,1)S(1)}, u32[]{:S(2)}, u32[]{:S(2)}) collective-permute-start(bf16[1,1,2,96,768]{4,3,2,1,0:T(8,128)(2,1)S(1)} %broadcast_select_fusion.5), channel_id=1, source_target_pairs={{0,8},{4,12},{8,0},{12,4},{16,24},{20,28},{24,16},{28,20},{1,9},{5... | collective-permute-start | bytes 884744 | tf_op jit(solution)/shard_map/ppermute | solution.py:863
  134.8 15.1 %collective-permute-start.26 = (bf16[192,768]{1,0:T(8,128)(2,1)S(1)}, bf16[192,768]{1,0:T(8,128)(2,1)S(1)}, u32[]{:S(2)}, u32[]{:S(2)}) collective-permute-start(bf16[192,768]{1,0:T(8,128)(2,1)S(1)} %get-tuple-element.389), channel_id=1, source_target_pairs={{0,8},{4,12},{8,0},{12,4},{16,24},{20,28},{24,16},{28,20},{1,9},{5... | collective-permute-start | bytes 884744 | tf_op jit(solution)/shard_map/ppermute | solution.py:863
  145.6 2.7 %collective-permute-start.27 = (bf16[40,768]{1,0:T(8,128)(2,1)}, bf16[40,768]{1,0:T(8,128)(2,1)S(1)}, u32[]{:S(2)}, u32[]{:S(2)}) collective-permute-start(bf16[40,768]{1,0:T(8,128)(2,1)} %get-tuple-element.346), channel_id=1, source_target_pairs={{0,1},{1,0},{2,3},{3,2},{4,5},{5,4},{6,7},{7,6},{8,9},{9,8},{10,11... | collective-permute-start | bytes 184328 | tf_op jit(solution)/shard_map/ppermute | solution.py:843
  145.6 32.5 %collective-permute-start.25 = (bf16[2,8,192,256]{3,2,1,0:T(8,128)(2,1)}, bf16[2,8,192,256]{3,2,1,0:T(8,128)(2,1)S(1)}, u32[]{:S(2)}, u32[]{:S(2)}) collective-permute-start(bf16[2,8,192,256]{3,2,1,0:T(8,128)(2,1)} %get-tuple-element.340), channel_id=1, source_target_pairs={{0,1},{1,0},{2,3},{3,2},{4,5},{5,4},{6,7},{7,6},{8,9},{9,8},{10,11... | collective-permute-start | bytes 4718600 | tf_op jit(solution)/shard_map/ppermute | solution.py:843
  146.3 15.8 %collective-permute-start.33 = (bf16[1,2,2,96,768]{4,3,2,1,0:T(8,128)(2,1)S(1)}, bf16[1,2,2,96,768]{4,3,2,1,0:T(8,128)(2,1)S(1)}, u32[]{:S(2)}, u32[]{:S(2)}) collective-permute-start(bf16[1,2,2,96,768]{4,3,2,1,0:T(8,128)(2,1)S(1)} %broadcast_select_fusion.2), channel_id=1, source_target_pairs={{0,4},{4,0},{8,12},{12,8},{16,20},{20,16},{24,28},{28,24},{1,5},{5... | collective-permute-start | bytes 1769480 | tf_op jit(solution)/shard_map/ppermute | solution.py:863
  146.9 15.0 %collective-permute-start.34 = (bf16[1,1,1,96,768]{4,3,2,1,0:T(8,128)(2,1)S(1)}, bf16[1,1,1,96,768]{4,3,2,1,0:T(8,128)(2,1)S(1)}, u32[]{:S(2)}, u32[]{:S(2)}) collective-permute-start(bf16[1,1,1,96,768]{4,3,2,1,0:T(8,128)(2,1)S(1)} %bitcast.81), channel_id=1, source_target_pairs={{0,16},{4,20},{8,24},{12,28},{16,0},{20,4},{24,8},{28,12},{1,17},{... | collective-permute-start | bytes 442376 | tf_op jit(solution)/shard_map/ppermute | solution.py:863
  148.3 4.3 %collective-permute-start.31 = (bf16[40,768]{1,0:T(8,128)(2,1)S(1)}, bf16[40,768]{1,0:T(8,128)(2,1)S(1)}, u32[]{:S(2)}, u32[]{:S(2)}) collective-permute-start(bf16[40,768]{1,0:T(8,128)(2,1)S(1)} %add_convert_fusion.26), channel_id=1, source_target_pairs={{0,2},{2,0},{1,3},{3,1},{4,6},{6,4},{5,7},{7,5},{8,10},{10,8},{9,1... | collective-permute-start | bytes 184328 | tf_op jit(solution)/shard_map/ppermute | solution.py:847
  149.9 16.2 %collective-permute-start.30 = (bf16[96,768]{1,0:T(8,128)(2,1)S(1)}, bf16[96,768]{1,0:T(8,128)(2,1)S(1)}, u32[]{:S(2)}, u32[]{:S(2)}) collective-permute-start(bf16[96,768]{1,0:T(8,128)(2,1)S(1)} %get-tuple-element.398), channel_id=1, source_target_pairs={{0,16},{4,20},{8,24},{12,28},{16,0},{20,4},{24,8},{28,12},{1,17},{... | collective-permute-start | bytes 442376 | tf_op jit(solution)/shard_map/ppermute | solution.py:863
  152.7 13.5 %collective-permute-start.32 = (bf16[1,42,768]{2,1,0:T(8,128)(2,1)S(1)}, bf16[1,42,768]{2,1,0:T(8,128)(2,1)S(1)}, u32[]{:S(2)}, u32[]{:S(2)}) collective-permute-start(bf16[1,42,768]{2,1,0:T(8,128)(2,1)S(1)} %maximum_bitcast_fusion), channel_id=1, source_target_pairs={{0,16},{4,20},{8,24},{12,28},{16,0},{20,4},{24,8},{28,12},{1,17},{... | collective-permute-start | bytes 193544 | tf_op jit(solution)/shard_map/ppermute | solution.py:863
  162.0 15.1 %collective-permute-start.36 = (bf16[1,1,2,96,768]{4,3,2,1,0:T(8,128)(2,1)S(1)}, bf16[1,1,2,96,768]{4,3,2,1,0:T(8,128)(2,1)S(1)}, u32[]{:S(2)}, u32[]{:S(2)}) collective-permute-start(bf16[1,1,2,96,768]{4,3,2,1,0:T(8,128)(2,1)S(1)} %broadcast_select_fusion.4), channel_id=1, source_target_pairs={{0,8},{4,12},{8,0},{12,4},{16,24},{20,28},{24,16},{28,20},{1,9},{5... | collective-permute-start | bytes 884744 | tf_op jit(solution)/shard_map/ppermute | solution.py:863
  163.7 14.1 %copy-start.25 = (pred[2]{0:T(512)(128)(4,1)S(1)}, pred[2]{0:T(512)(128)(4,1)}, u32[]{:S(2)}) copy-start(pred[2]{0:T(512)(128)(4,1)} %copy-done.24) | copy-start | bytes 10
  163.7 14.4 %copy-start.3 = (bf16[2,8,192,256]{3,2,1,0:T(8,128)(2,1)S(1)}, bf16[2,8,192,256]{3,2,1,0:T(8,128)(2,1)}, u32[]{:S(2)}) copy-start(bf16[2,8,192,256]{3,2,1,0:T(8,128)(2,1)} %get-tuple-element.368) | copy-start | bytes 4718596
  166.2 9.3 %collective-permute-start.37 = (bf16[2,42,768]{2,1,0:T(8,128)(2,1)S(1)}, bf16[2,42,768]{2,1,0:T(8,128)(2,1)S(1)}, u32[]{:S(2)}, u32[]{:S(2)}) collective-permute-start(bf16[2,42,768]{2,1,0:T(8,128)(2,1)S(1)} %constant_dynamic-update-slice_fusion), channel_id=1, source_target_pairs={{0,8},{4,12},{8,0},{12,4},{16,24},{20,28},{24,16},{28,20},{1,9},{5... | collective-permute-start | bytes 387080 | tf_op jit(solution)/shard_map/ppermute | solution.py:863
  166.3 11.6 %collective-permute-start.35 = (bf16[1,1,1,96,768]{4,3,2,1,0:T(8,128)(2,1)S(1)}, bf16[1,1,1,96,768]{4,3,2,1,0:T(8,128)(2,1)S(1)}, u32[]{:S(2)}, u32[]{:S(2)}) collective-permute-start(bf16[1,1,1,96,768]{4,3,2,1,0:T(8,128)(2,1)S(1)} %bitcast.83), channel_id=1, source_target_pairs={{0,4},{4,0},{8,12},{12,8},{16,20},{20,16},{24,28},{28,24},{1,5},{5... | collective-permute-start | bytes 442376 | tf_op jit(solution)/shard_map/ppermute | solution.py:863
  175.6 9.9 %collective-permute-start.40 = (bf16[4,42,768]{2,1,0:T(8,128)(2,1)S(1)}, bf16[4,42,768]{2,1,0:T(8,128)(2,1)S(1)}, u32[]{:S(2)}, u32[]{:S(2)}) collective-permute-start(bf16[4,42,768]{2,1,0:T(8,128)(2,1)S(1)} %constant_dynamic-update-slice_fusion.2), channel_id=1, source_target_pairs={{0,4},{4,0},{8,12},{12,8},{16,20},{20,16},{24,28},{28,24},{1,5},{5... | collective-permute-start | bytes 774152 | tf_op jit(solution)/shard_map/ppermute | solution.py:863
  177.3 33.2 %collective-permute-start.39 = (bf16[1,2,2,96,768]{4,3,2,1,0:T(8,128)(2,1)S(1)}, bf16[1,2,2,96,768]{4,3,2,1,0:T(8,128)(2,1)}, u32[]{:S(2)}, u32[]{:S(2)}) collective-permute-start(bf16[1,2,2,96,768]{4,3,2,1,0:T(8,128)(2,1)S(1)} %broadcast_select_fusion.1), channel_id=1, source_target_pairs={{0,4},{4,0},{8,12},{12,8},{16,20},{20,16},{24,28},{28,24},{1,5},{5... | collective-permute-start | bytes 1769480 | tf_op jit(solution)/shard_map/ppermute | solution.py:863
  178.0 15.0 %collective-permute-start.41 = (bf16[2,1,1,96,768]{4,3,0,2,1:T(8,128)(2,1)S(1)}, bf16[2,1,1,96,768]{4,3,0,2,1:T(8,128)(2,1)S(1)}, u32[]{:S(2)}, u32[]{:S(2)}) collective-permute-start(bf16[2,1,1,96,768]{4,3,0,2,1:T(8,128)(2,1)S(1)} %broadcast_select_fusion.3), channel_id=1, source_target_pairs={{0,16},{4,20},{8,24},{12,28},{16,0},{20,4},{24,8},{28,12},{1,17},{... | collective-permute-start | bytes 884744 | tf_op jit(solution)/shard_map/ppermute | solution.py:863
  193.1 20.9 %collective-permute-start.42 = (bf16[2,1,2,96,768]{4,3,2,0,1:T(8,128)(2,1)S(1)}, bf16[2,1,2,96,768]{4,3,2,0,1:T(8,128)(2,1)}, u32[]{:S(2)}, u32[]{:S(2)}) collective-permute-start(bf16[2,1,2,96,768]{4,3,2,0,1:T(8,128)(2,1)S(1)} %broadcast_select_fusion), channel_id=1, source_target_pairs={{0,8},{4,12},{8,0},{12,4},{16,24},{20,28},{24,16},{28,20},{1,9},{5... | collective-permute-start | bytes 1769480 | tf_op jit(solution)/shard_map/ppermute | solution.py:863
  193.2 20.6 %collective-permute-start.38 = (bf16[8,192,256]{2,1,0:T(8,128)(2,1)}, bf16[8,192,256]{2,1,0:T(8,128)(2,1)S(1)}, u32[]{:S(2)}, u32[]{:S(2)}) collective-permute-start(bf16[8,192,256]{2,1,0:T(8,128)(2,1)} %get-tuple-element.394), channel_id=1, source_target_pairs={{0,2},{2,0},{1,3},{3,1},{4,6},{6,4},{5,7},{7,5},{8,10},{10,8},{9,1... | collective-permute-start | bytes 2359304 | tf_op jit(solution)/shard_map/ppermute | solution.py:847
  (31 other events, 80.4 us)
where the time goes:
time: 219 us
  Pallas kernels  104 us (47%)
  waiting for transfers between devices  37.8 us (17%)
  starting transfers between devices  36.8 us (17%)
  other arithmetic  19.8 us (9%)
  local copies, waits for them, and re-layouts  13 us (6%)
  matrix products  5.28 us (2%)
    pallas_call x8, Pallas kernels, call(): pl.pallas_call(run, name=name, out_shape=[jax.ShapeDtypeStruct(o[0], o[1]...  80.6 us
    ppermute x21, waiting for transfers between devices, wide_swap(): return lax.ppermute(v, 'wide', [(i, i ^ bit) for i in range(count)])  30.8 us
    ppermute x21, starting transfers between devices, wide_swap(): return lax.ppermute(v, 'wide', [(i, i ^ bit) for i in range(count)])  23.4 us
    pallas_call x1, Pallas kernels, condition_back(): pl.pallas_call(functools.partial(condition_back_body, factor), name='cond...  15 us
    ppermute x8, starting transfers between devices, x_swap(): return lax.ppermute(v, 'narrow', [(0, 2), (2, 0), (1, 3), (3, 1)])  9.79 us
    convert_element_type x21, other arithmetic, sum_pair(): return (a.astype(F32) + b.astype(F32)).astype(BF)  9.04 us
    pallas_call x1, Pallas kernels, condition(): pl.pallas_call(condition_body, name='condition', in_specs=[vmem, vmem, an...  8.64 us
    unnamed x75, local copies, waits for them, and re-layouts  7.38 us
  transfers between devices with their start and end apart: 43, of which 12 were waited for; matrix products, arithmetic and copies ran while one was open for 12% of the time, Pallas kernels for 48%

commit v1 on v0

--- a/solution.py
+++ b/solution.py
@@ -18,7 +18,7 @@
 HIGHEST = lax.Precision.HIGHEST
 LANES = 128
 ROWS = 128
-FEW_ROWS = 64
+FEW_ROWS = 128
 BAND = 64
 GELU_A = math.sqrt(2.0 / math.pi)
 GELU_B = 0.044715
@@ -457,18 +457,21 @@
 
     def lanes(rel, at):
         taps = taps_of(kern, at)
-
-        def bands(band, sums):
+        sums = [None] * 9
+        shift_sum, scale_sum = None, None
+        for band in range(0, tokens, BAND):
             here = pl.ds(pl.multiple_of(rel * tokens + band, BAND), BAND)
             base = pl.multiple_of(rel * tall + band, SIDE)
             total, shifted = conv_back_band(gpad, base, at, taps)
             gback[here, at] = total
-            values = [first[pl.ds(base + SIDE * r, BAND), at] for r in range(3)]
-            parts = [fold_rows(values[r] * shifted[c]) for r in range(3) for c in range(3)]
-            parts += [fold_rows(total), fold_rows(total * normed1[here, at])]
-            return [a + b for a, b in zip(sums, parts)]
-
-        *sums, shift_sum, scale_sum = band_loop(tokens, bands, [jnp.zeros((8, LANES), F32)] * 11)
+            part_a, part_b = fold_rows(total), fold_rows(total * normed1[here, at])
+            shift_sum = part_a if shift_sum is None else shift_sum + part_a
+            scale_sum = part_b if scale_sum is None else scale_sum + part_b
+            for r in range(3):
+                values = first[pl.ds(base + SIDE * r, BAND), at]
+                for c in range(3):
+                    part = fold_rows(values * shifted[c])
+                    sums[3 * r + c] = part if sums[3 * r + c] is None else sums[3 * r + c] + part
         for t in range(9):
             kgrad_out[t : t + 1, at] += jnp.sum(sums[t], 0, keepdims=True)
         lat = jnp.bitwise_xor(rel, core)
@@ -868,16 +871,16 @@
     return lax.dynamic_slice_in_dim(v, at * rows, rows, 0)
 
 
-def in_place(bit, own, came, axis):
+def in_place(second, own, came, axis):
     dims = own.shape[:axis] + (2,) + own.shape[axis + 1 :]
-    return jnp.where(lax.broadcasted_iota(jnp.int32, dims, axis) == bit, own, came)
+    chosen = lax.broadcast_in_dim(second, dims, (axis,))
+    return jnp.where(chosen, own, came)
 
 
 class WideSum:
-    def __init__(self, product, at, count, back=None):
-        self.count, self.dims = count, product.shape
+    def __init__(self, product, bits, masks, count, back=None):
+        self.count, self.dims, self.bits, self.masks = count, product.shape, bits, masks
         self.levels = count.bit_length() - 1
-        self.bits = [at // (1 << k) % 2 for k in range(self.levels)]
         self.ahead = list(range(self.levels))
         self.back = list(reversed(self.ahead)) if back is None else back
         self.opened = False
@@ -901,7 +904,7 @@
         if self.ahead:
             return self.halve, (self.held, self.came)
         level = self.back[0]
-        return lambda a, b: in_place(self.bits[level], a, b, level), (self.held, self.came)
+        return lambda a, b: in_place(self.masks[level], a, b, level), (self.held, self.came)
 
     def accept(self, out):
         if not self.opened:
@@ -923,11 +926,10 @@
     def done(self):
         return self.opened and not self.ahead and len(self.back) == 1
 
-    def finish(self, order, shape=lambda v: v):
+    def finish(self, order, dtype):
         level = self.back[0]
-        return order(
-            lambda a, b: shape(in_place(self.bits[level], a, b, level).reshape(self.dims)), self.held, self.came
-        )
+        whole_sum = order(lambda a, b: in_place(self.masks[level], a, b, level).astype(dtype), self.held, self.came)
+        return lax.optimization_barrier(whole_sum).reshape(self.dims)
 
 
 class Steps:
@@ -1023,7 +1025,10 @@
     fwd_a = order(attend(0), x_parts)
     here_a = order(sum_pair, fwd_a[6], core_swap(fwd_a[7]))
     fwd_b = order(attend(1), after(x_parts, g_across))
-    att_a = order(sum_pair, here_a, x_swap(here_a))
+    levels = wide_count.bit_length() - 1
+    places = [jnp.bitwise_and(jnp.right_shift(wide_at, k), 1) for k in range(levels)]
+    masks = [jnp.arange(2, dtype=jnp.int32) == place for place in places]
+    att_a, masks = order(lambda a, b, m: (sum_pair(a, b), m), here_a, x_swap(here_a), masks)
     here_b = order(sum_pair, fwd_b[6], core_swap(fwd_b[7]))
     att_a = (att_a, core_swap(att_a))
 
@@ -1042,11 +1047,11 @@
     sec_a = order(sum_pair, here_a, x_swap(here_a))
     sec_a = (sec_a, core_swap(sec_a))
     down_product = order(token_product, [ffn_a[2], ffn_b[2]], [ffn_a[3], ffn_b[3]])
-    down_sum = WideSum(down_product, wide_at, wide_count)
+    down_sum = WideSum(down_product, places, masks, wide_count)
     order.advance(down_sum)
     here_b = order(sum_pair, ffn_b[5], core_swap(ffn_b[6]))
     up_product = order(token_product, [ffn_a[1], ffn_b[1]], [ffn_a[4], ffn_b[4]])
-    up_sum = WideSum(up_product, wide_at, wide_count)
+    up_sum = WideSum(up_product, places, masks, wide_count)
     order.advance(up_sum)
 
     def attend_back(pair, fwd, ffn):
@@ -1071,8 +1076,7 @@
         ),
         [back_a[1], back_b[1]], [fwd_a[1], fwd_b[1]], [fwd_a[5], fwd_b[5]], [back_a[0], back_b[0]],
     )
-    levels = wide_count.bit_length() - 1
-    attn_sum = WideSum(attn_product, wide_at, wide_count, [0] + list(range(levels - 1, 0, -1)))
+    attn_sum = WideSum(attn_product, places, masks, wide_count, [0] + list(range(levels - 1, 0, -1)))
     order.advance(attn_sum)
     order.advance(up_sum)
     order.advance(down_sum)
@@ -1099,12 +1103,12 @@
     order.advance(up_sum)
     while not down_sum.done():
         order.advance(down_sum)
-    down_grad = down_sum.finish(order, lambda v: v.astype(F32))
+    down_grad = down_sum.finish(order, F32)
+    made = order(functools.partial(slice_halves, x), in_b[2], core_swap(in_b[3]))
     order.advance(attn_sum, mods)
     order.advance(mods)
     order.advance(up_sum)
     order.advance(attn_sum)
-    made = order(functools.partial(slice_halves, x), in_b[2], core_swap(in_b[3]))
     while not all(c.done() for c in (mods, up_sum)):
         order.advance(mods)
         order.advance(up_sum)
@@ -1114,15 +1118,18 @@
         taps = jnp.sum(held[:, rows:].astype(F32), 0) * factor
         return gmod, jnp.sum(gmod.astype(F32), 0) * factor, taps[:9], taps[9:]
 
-    gmod, ada_bias_grad, attn_taps, ffn_taps = order(lambda a, b: unpack(join(a, b)), *mods.came)
+    unpacked = order(lambda a, b: unpack(join(a, b)), *mods.came)
+    order.last = tuple(unpacked)
+    gmod, ada_bias_grad, attn_taps, ffn_taps = unpacked
+    finals = order(sum_pair, made[0], x_swap(made[1]))
     while not attn_sum.done():
         order.advance(attn_sum)
     time_in_grad, time_out_grad, ada_weight_grad = order(
         lambda g: condition_back(g, embedded, stages, time_out, ada_weight, factor), gmod
     )
-    up_grad = up_sum.finish(order, lambda v: v.astype(F32))
-    finals = order(sum_pair, made[0], x_swap(made[1]))
-    qkv_rows_grad, out_grad = attn_sum.finish(order, lambda v: (v[: 3 * share].astype(F32), v[3 * share :].astype(F32)))
+    up_grad = up_sum.finish(order, F32)
+    attn_grads = attn_sum.finish(order, BF)
+    qkv_rows_grad, out_grad = attn_grads[: 3 * share].astype(F32), attn_grads[3 * share :].astype(F32)
     qkv_grad = jnp.swapaxes(qkv_rows_grad.reshape(3, share, width), 1, 2)
     final_out = jnp.swapaxes(finals[:per_dev], 1, 2)
     final_grad = jnp.swapaxes(finals[per_dev:], 1, 2)

time: 219 us -> 214 us (0.977)
    pallas_call x8, Pallas kernels: 80.6 us -> 77.8 us  [call(): pl.pallas_call(run, name=name, out_shape=[jax.ShapeDtypeStruct(o[0], o[1]...]
    convert_element_type x21, other arithmetic: 9.04 us -> 11.8 us  [sum_pair(): return (a.astype(F32) + b.astype(F32)).astype(BF)]
    unnamed x75 -> x83, local copies, waits for them, and re-layouts: 7.38 us -> 7.33 us
  transfers between devices with their start and end apart: 43 -> 43, of which waited for: 12 -> 13; matrix products, arithmetic and copies ran while one was open for 12% -> 14% of each run, Pallas kernels for 48% -> 48%
where the time goes in v1:
time: 214 us
  Pallas kernels  102 us (48%)
  starting transfers between devices  36 us (17%)
  waiting for transfers between devices  35.9 us (17%)
  other arithmetic  21.6 us (10%)
  local copies, waits for them, and re-layouts  11.8 us (6%)
  matrix products  5.28 us (2%)
    pallas_call x8, Pallas kernels, call(): pl.pallas_call(run, name=name, out_shape=[jax.ShapeDtypeStruct(o[0], o[1]...  77.8 us
    ppermute x21, waiting for transfers between devices, wide_swap(): return lax.ppermute(v, 'wide', [(i, i ^ bit) for i in range(count)])  29.3 us
    ppermute x21, starting transfers between devices, wide_swap(): return lax.ppermute(v, 'wide', [(i, i ^ bit) for i in range(count)])  23 us
    pallas_call x1, Pallas kernels, condition_back(): pl.pallas_call(functools.partial(condition_back_body, factor), name='cond...  15 us
    convert_element_type x21, other arithmetic, sum_pair(): return (a.astype(F32) + b.astype(F32)).astype(BF)  11.8 us
    ppermute x8, starting transfers between devices, x_swap(): return lax.ppermute(v, 'narrow', [(0, 2), (2, 0), (1, 3), (3, 1)])  9.73 us
    pallas_call x1, Pallas kernels, condition(): pl.pallas_call(condition_body, name='condition', in_specs=[vmem, vmem, an...  8.83 us
    unnamed x83, local copies, waits for them, and re-layouts  7.33 us
  transfers between devices with their start and end apart: 43, of which 13 were waited for; matrix products, arithmetic and copies ran while one was open for 14% of the time, Pallas kernels for 48%

profile of v1, /device:TPU:0, one launch (start us, length us, event | category | flops | bytes accessed | tf_op | source)
XLA Modules:
  0.0 213.7 jit_solution(10418242919869119720)
XLA Ops:
  0.6 3.0 %collective-permute-start.1 = (bf16[4,192,256]{2,1,0:T(8,128)(2,1)}, bf16[4,192,256]{2,1,0:T(8,128)(2,1)S(1)}, u32[]{:S(2)}, u32[]{:S(2)}) collective-permute-start(bf16[4,192,256]{2,1,0:T(8,128)(2,1)} %bitcast.87), channel_id=1, source_target_pairs={{0,2},{2,0},{1,3},{3,1},{4,6},{6,4},{5,7},{7,5},{8,10},{10,8},{9,1... | collective-permute-start | bytes 1179656 | tf_op jit(solution)/shard_map/ppermute | solution.py:850
  6.5 8.8 %condition.1 = (f32[4,6,768]{2,1,0:T(8,128)}, f32[32,768]{1,0:T(8,128)}, f32[32,768]{1,0:T(8,128)}, f32[32,768]{1,0:T(8,128)}, f32[32,768]{1,0:T(8,128)}) custom-call(f32[32,256]{1,0:T(8,128)} %pad_maximum_fusion.1.embedded, f32[36,128]{1,0:T(8,128)} %bitcast.95, f32[256,768]{1,0:T(8,128)} %time_in.1, f32[768,768]{1,0:T(8,128)} %time_out.3, f32[768,4608]{1,0:T(8,128)} %ada.3), custom_call_target="tpu_custom_call" | custom-call | flops 8000000000 | bytes 1000000 | tf_op jit(solution)/shard_map/condition/pallas_call | solution.py:685
  16.0 1.3 collective-permute-done.2.refs_3_
  18.0 8.0 %attn_fwd.2 = (bf16[512,768]{1,0:T(8,128)(2,1)}, bf16[512,768]{1,0:T(8,128)(2,1)}, bf16[512,192]{1,0:T(8,128)(2,1)}, bf16[512,192]{1,0:T(8,128)(2,1)}, bf16[512,...) custom-call(s32[1]{0:T(128)} %bitcast.s_ref, ...), custom_call_target="tpu_custom_call" | custom-call | flops 6000000000 | bytes 1000000 | tf_op jit(solution)/shard_map/attn_fwd/pallas_call | solution.py:566
  27.2 0.9 collective-permute-done.4
  28.1 1.1 add_convert_fusion.9
  29.2 0.9 collective-permute-start.6
  30.1 8.1 %attn_fwd.3 = (bf16[512,768]{1,0:T(8,128)(2,1)}, bf16[512,768]{1,0:T(8,128)(2,1)}, bf16[512,192]{1,0:T(8,128)(2,1)}, bf16[512,192]{1,0:T(8,128)(2,1)}, bf16[512,...) custom-call(s32[1]{0:T(128)} %bitcast.s_ref, ...), custom_call_target="tpu_custom_call" | custom-call | flops 6000000000 | bytes 1000000 | tf_op jit(solution)/shard_map/attn_fwd/pallas_call | solution.py:566
  38.2 2.4 %collective-permute-done.6 = bf16[256,768]{1,0:T(8,128)(2,1)S(1)} collective-permute-done((bf16[256,768]{1,0:T(8,128)(2,1)S(1)}, bf16[256,768]{1,0:T(8,128)(2,1)S(1)}, u32[]{:S(2)}, u32[]{:S(2)}) %collective-permute-start.6) | collective-permute-done | bytes 393248 | tf_op jit(solution)/shard_map/ppermute | solution.py:850
  40.9 1.1 add_convert_fusion.7
  44.3 14.5 %ffn.2 = (bf16[512,768]{1,0:T(8,128)(2,1)}, bf16[512,768]{1,0:T(8,128)(2,1)}, bf16[512,768]{1,0:T(8,128)(2,1)}, bf16[512,768]{1,0:T(8,128)(2,1)}, bf16[512,768]{...) custom-call(s32[1]{0:T(128)} %bitcast.s_ref, ...), custom_call_target="tpu_custom_call" | custom-call | flops 10000000000 | bytes 1000000 | tf_op jit(solution)/shard_map/ffn/pallas_call | solution.py:566
  59.6 1.2 collective-permute-done.12
  60.8 1.1 add_convert_fusion.5
  61.9 1.5 collective-permute-start.14
  64.2 14.8 %ffn.3 = (bf16[512,768]{1,0:T(8,128)(2,1)}, bf16[512,768]{1,0:T(8,128)(2,1)}, bf16[512,768]{1,0:T(8,128)(2,1)}, bf16[512,768]{1,0:T(8,128)(2,1)}, bf16[512,768]{...) custom-call(s32[1]{0:T(128)} %bitcast.s_ref, ...), custom_call_target="tpu_custom_call", output_to_operand_aliasing={{9}: (13, {}), {10}: (14, {})} | custom-call | flops 10000000000 | bytes 1000000 | tf_op jit(solution)/shard_map/ffn/pallas_call | solution.py:566
  82.4 1.6 collective-permute-start.18
  88.6 7.8 %attn_bwd.2 = (bf16[512,768]{1,0:T(8,128)(2,1)}, bf16[512,576]{1,0:T(8,128)(2,1)}, bf16[512,768]{1,0:T(8,128)(2,1)}, f32[2,8,768]{2,1,0:T(8,128)}) custom-call(s32[1]{0:T(128)} %bitcast.s_ref, bf16[512,768]{1,0:T(8,128)(2,1)} %get-tuple-element.216.refs_4_.refs_0_, bf16[256,768]{1,0:T(8,128)(2,1)} %copy-done.17, bf16[256,768]{1,0:T(8,128)(2,1)} %copy-done.33, ...), custom_call_target="tpu_custom_call" | custom-call | flops 6000000000 | bytes 1000000 | tf_op jit(solution)/shard_map/attn_bwd/pallas_call | solution.py:566
  96.4 1.9 add_convert_fusion.2.refs_3_
  99.0 1.6 collective-permute-start.19
  100.7 8.1 %attn_bwd.3 = (bf16[512,768]{1,0:T(8,128)(2,1)}, bf16[512,576]{1,0:T(8,128)(2,1)}, bf16[512,768]{1,0:T(8,128)(2,1)}, f32[2,8,768]{2,1,0:T(8,128)}) custom-call(s32[1]{0:T(128)} %bitcast.s_ref, bf16[512,768]{1,0:T(8,128)(2,1)} %get-tuple-element.223.refs_4_.refs_0_, bf16[256,768]{1,0:T(8,128)(2,1)} %copy-done.16, bf16[256,768]{1,0:T(8,128)(2,1)} %copy-done.31, ...), custom_call_target="tpu_custom_call" | custom-call | flops 6000000000 | bytes 1000000 | tf_op jit(solution)/shard_map/attn_bwd/pallas_call | solution.py:566
  108.9 2.7 %collective-permute-start.21 = (bf16[96,768]{1,0:T(8,128)(2,1)S(1)}, bf16[96,768]{1,0:T(8,128)(2,1)S(1)}, u32[]{:S(2)}, u32[]{:S(2)}) collective-permute-start(bf16[96,768]{1,0:T(8,128)(2,1)S(1)} %get-tuple-element.409), channel_id=1, source_target_pairs={{0,16},{4,20},{8,24},{12,28},{16,0},{20,4},{24,8},{28,12},{1,17},{... | collective-permute-start | bytes 442376 | tf_op jit(solution)/shard_map/ppermute | solution.py:866
  115.3 1.6 collective-permute-start.20
  116.9 2.0 add_convert_fusion.12
  118.8 1.0 collective-permute-start.24
  120.6 8.2 %input_bwd.2 = (f32[16,768]{1,0:T(8,128)}, f32[2,8,768]{2,1,0:T(8,128)}, bf16[2,8,192,256]{3,2,1,0:T(8,128)(2,1)}, bf16[2,8,192,256]{3,2,1,0:T(8,128)(2,1)}) custom-call(s32[1]{0:T(128)} %bitcast.s_ref, bf16[512,768]{1,0:T(8,128)(2,1)} %get-tuple-element.216.refs_4_.refs_0_, ...), custom_call_target="tpu_custom_call", output_to_operand_aliasing={{2}: (10, {}), {3}: (11, {})} | custom-call | flops 6000000000 | bytes 1000000 | tf_op jit(solution)/shard_map/input_bwd/pallas_call | solution.py:566
  128.8 1.7 collective-permute-done.24
  131.3 1.4 collective-permute-start.28
  133.6 1.5 collective-permute-start.32
  135.2 8.3 %input_bwd.3 = (f32[16,768]{1,0:T(8,128)}, bf16[40,768]{1,0:T(8,128)(2,1)}, bf16[2,8,192,256]{3,2,1,0:T(8,128)(2,1)}, bf16[2,8,192,256]{3,2,1,0:T(8,128)(2,1)}) custom-call(s32[1]{0:T(128)} %bitcast.s_ref, bf16[512,768]{1,0:T(8,128)(2,1)} %get-tuple-element.223.refs_4_.refs_0_, ...), custom_call_target="tpu_custom_call", output_to_operand_aliasing={{2}: (10, {}), {3}: (11, {})} | custom-call | flops 6000000000 | bytes 1000000 | tf_op jit(solution)/shard_map/input_bwd/pallas_call | solution.py:566
  144.1 0.9 collective-permute-done.26
  145.7 1.0 add_convert_fusion.19
  146.7 1.6 collective-permute-start.29
  148.3 1.5 collective-permute-start.31
  149.9 2.3 %collective-permute-start.34 = (bf16[96,768]{1,0:T(8,128)(2,1)S(1)}, bf16[96,768]{1,0:T(8,128)(2,1)S(1)}, u32[]{:S(2)}, u32[]{:S(2)}) collective-permute-start(bf16[96,768]{1,0:T(8,128)(2,1)S(1)} %get-tuple-element.405), channel_id=1, source_target_pairs={{0,16},{4,20},{8,24},{12,28},{16,0},{20,4},{24,8},{28,12},{1,17},{... | collective-permute-start | bytes 442376 | tf_op jit(solution)/shard_map/ppermute | solution.py:866
  152.6 1.5 collective-permute-start.35
  154.1 7.4 %collective-permute-done.29 = bf16[1,1,1,96,768]{4,3,2,1,0:T(8,128)(2,1)S(1)} collective-permute-done((bf16[1,1,1,96,768]{4,3,2,1,0:T(8,128)(2,1)S(1)}, bf16[1,1,1,96,768]{4,3,2,1,0:T(8,128)(2,1)S(1)}, u32[]{:S(2)}, u32[]{:S(2)}) %collective-permute-start.29) | collective-permute-done | bytes 147488 | tf_op jit(solution)/shard_map/ppermute | solution.py:866
  161.7 1.6 select_convert_fusion.1
  164.3 1.5 collective-permute-done.35
  167.3 1.4 collective-permute-start.33
  168.7 6.4 %collective-permute-done.36 = bf16[2,42,768]{2,1,0:T(8,128)(2,1)S(1)} collective-permute-done((bf16[2,42,768]{2,1,0:T(8,128)(2,1)S(1)}, bf16[2,42,768]{2,1,0:T(8,128)(2,1)S(1)}, u32[]{:S(2)}, u32[]{:S(2)}) %collective-permute-start.36) | collective-permute-done | bytes 129056 | tf_op jit(solution)/shard_map/ppermute | solution.py:866
  176.1 1.3 collective-permute-start.42
  177.7 7.4 %collective-permute-done.37 = bf16[4,42,768]{2,1,0:T(8,128)(2,1)S(1)} collective-permute-done((bf16[4,42,768]{2,1,0:T(8,128)(2,1)S(1)}, bf16[4,42,768]{2,1,0:T(8,128)(2,1)S(1)}, u32[]{:S(2)}, u32[]{:S(2)}) %collective-permute-start.37) | collective-permute-done | bytes 258080 | tf_op jit(solution)/shard_map/ppermute | solution.py:866
  186.9 1.3 add_convert_fusion.1
  188.3 3.9 %collective-permute-done.40 = bf16[2,1,1,96,768]{4,3,0,2,1:T(8,128)(2,1)S(1)} collective-permute-done((bf16[2,1,1,96,768]{4,3,0,2,1:T(8,128)(2,1)S(1)}, bf16[2,1,1,96,768]{4,3,0,2,1:T(8,128)(2,1)S(1)}, u32[]{:S(2)}, u32[]{:S(2)}) %collective-permute-start.40) | collective-permute-done | bytes 294944 | tf_op jit(solution)/shard_map/ppermute | solution.py:866
  192.4 15.0 %condition_back.1 = (f32[256,768]{1,0:T(8,128)}, f32[768,768]{1,0:T(8,128)}, f32[768,4608]{1,0:T(8,128)}) custom-call(bf16[32,4608]{1,0:T(8,128)(2,1)} %copy-done, f32[32,256]{1,0:T(8,128)} %pad_maximum_fusion.1.embedded, f32[32,768]{1,0:T(8,128)} %get-tuple-element.383.inner_pre, f32[32,768]{1,0:T(8,128)} %get-tuple-element.384.inner, ...), custom_call_target="tpu_custom_call" | custom-call | flops 1 | bytes 1 | tf_op jit(solution)/shard_map/condition_back/pallas_call | solution.py:749
  207.5 2.8 %select_convert_fusion = f32[2,2,2,96,768]{4,3,2,1,0:T(8,128)} fusion(pred[2]{0:T(512)(128)(4,1)S(1)} %copy-done.29, bf16[2,2,96,768]{3,2,1,0:T(8,128)(2,1)} %bitcast.29, bf16[2,2,96,768]{3,2,1,0:T(8,128)(2,1)S(1)} %bitcast.68), kind=kLoop, calls=%fused_computation.11 | loop fusion | flops 1179648 | bytes 3538946 | tf_op jit(solution)/shard_map/convert_element_type | solution.py:931
  210.3 0.9 slice_bitcast_fusion
  212.3 1.4 convert_bitcast_fusion
  (201 shorter events, 32.8 us)
Async XLA Ops:
  0.6 14.7 %collective-permute-start.1 = (bf16[4,192,256]{2,1,0:T(8,128)(2,1)}, bf16[4,192,256]{2,1,0:T(8,128)(2,1)S(1)}, u32[]{:S(2)}, u32[]{:S(2)}) collective-permute-start(bf16[4,192,256]{2,1,0:T(8,128)(2,1)} %bitcast.87), channel_id=1, source_target_pairs={{0,2},{2,0},{1,3},{3,1},{4,6},{6,4},{5,7},{7,5},{8,10},{10,8},{9,1... | collective-permute-start | bytes 1179656 | tf_op jit(solution)/shard_map/ppermute | solution.py:850
  3.6 12.4 %collective-permute-start = (bf16[4,192,256]{2,1,0:T(8,128)(2,1)}, bf16[4,192,256]{2,1,0:T(8,128)(2,1)S(1)}, u32[]{:S(2)}, u32[]{:S(2)}) collective-permute-start(bf16[4,192,256]{2,1,0:T(8,128)(2,1)} %bitcast.88), channel_id=1, source_target_pairs={{0,1},{1,0},{2,3},{3,2},{4,5},{5,4},{6,7},{7,6},{8,9},{9,8},{10,11... | collective-permute-start | bytes 1179656 | tf_op jit(solution)/shard_map/ppermute | solution.py:846
  15.4 1.9 collective-permute-start.2
  15.9 11.1 %collective-permute-start.3 = (bf16[4,192,256]{2,1,0:T(8,128)(2,1)S(1)}, bf16[4,192,256]{2,1,0:T(8,128)(2,1)S(1)}, u32[]{:S(2)}, u32[]{:S(2)}) collective-permute-start(bf16[4,192,256]{2,1,0:T(8,128)(2,1)S(1)} %bitcast.93), channel_id=1, source_target_pairs={{0,2},{2,0},{1,3},{3,1},{4,6},{6,4},{5,7},{7,5},{8,10},{10,8},{9,1... | collective-permute-start | bytes 1179656 | tf_op jit(solution)/shard_map/ppermute | solution.py:850
  26.1 2.0 collective-permute-start.4
  26.5 16.1 %collective-permute-start.9 = (bf16[4,192,256]{2,1,0:T(8,128)(2,1)S(1)}, bf16[4,192,256]{2,1,0:T(8,128)(2,1)S(1)}, u32[]{:S(2)}, u32[]{:S(2)}) collective-permute-start(bf16[4,192,256]{2,1,0:T(8,128)(2,1)S(1)} %bitcast.94), channel_id=1, source_target_pairs={{0,1},{1,0},{2,3},{3,2},{4,5},{5,4},{6,7},{7,6},{8,9},{9,8},{10,11... | collective-permute-start | bytes 1179656 | tf_op jit(solution)/shard_map/ppermute | solution.py:846
  26.7 150.8 %copy-start.28 = (pred[2]{0:T(512)(128)(4,1)}, pred[2]{0:T(512)(128)(4,1)S(1)}, u32[]{:S(2)}) copy-start(pred[2]{0:T(512)(128)(4,1)S(1)} %iota_compare_fusion.2) | copy-start | bytes 10
  26.7 134.8 %copy-start.26 = (pred[2]{0:T(512)(128)(4,1)}, pred[2]{0:T(512)(128)(4,1)S(1)}, u32[]{:S(2)}) copy-start(pred[2]{0:T(512)(128)(4,1)S(1)} %get-tuple-element.318) | copy-start | bytes 10
  26.7 149.3 %copy-start.24 = (pred[2]{0:T(512)(128)(4,1)}, pred[2]{0:T(512)(128)(4,1)S(1)}, u32[]{:S(2)}) copy-start(pred[2]{0:T(512)(128)(4,1)S(1)} %get-tuple-element.346) | copy-start | bytes 10
  27.0 15.6 %collective-permute-start.10 = (bf16[4,192,256]{2,1,0:T(8,128)(2,1)S(1)}, bf16[4,192,256]{2,1,0:T(8,128)(2,1)S(1)}, u32[]{:S(2)}, u32[]{:S(2)}) collective-permute-start(bf16[4,192,256]{2,1,0:T(8,128)(2,1)S(1)} %collective-permute-done.3.refs_2_), channel_id=1, source_target_pairs={{0,1},{1,0},{2,3},{3,2},{4,5},{5,4},{6,7},{7,6},{8,9},{9,8},{10,11... | collective-permute-start | bytes 1179656 | tf_op jit(solution)/shard_map/ppermute | solution.py:846
  29.2 11.5 %collective-permute-start.6 = (bf16[256,768]{1,0:T(8,128)(2,1)S(1)}, bf16[256,768]{1,0:T(8,128)(2,1)S(1)}, u32[]{:S(2)}, u32[]{:S(2)}) collective-permute-start(bf16[256,768]{1,0:T(8,128)(2,1)S(1)} %add_convert_fusion.9), channel_id=1, source_target_pairs={{0,2},{2,0},{1,3},{3,1},{4,6},{6,4},{5,7},{7,5},{8,10},{10,8},{9,1... | collective-permute-start | bytes 1179656 | tf_op jit(solution)/shard_map/ppermute | solution.py:850
  38.1 2.7 %collective-permute-start.5 = (bf16[256,768]{1,0:T(8,128)(2,1)}, bf16[256,768]{1,0:T(8,128)(2,1)S(1)}, u32[]{:S(2)}, u32[]{:S(2)}) collective-permute-start(bf16[256,768]{1,0:T(8,128)(2,1)} %get-tuple-element.225), channel_id=1, source_target_pairs={{0,1},{1,0},{2,3},{3,2},{4,5},{5,4},{6,7},{7,6},{8,9},{9,8},{10,11... | collective-permute-start | bytes 1179656 | tf_op jit(solution)/shard_map/ppermute | solution.py:846
  40.8 1.9 collective-permute-start.8
  42.0 17.0 %collective-permute-start.7 = (bf16[256,768]{1,0:T(8,128)(2,1)S(1)}, bf16[256,768]{1,0:T(8,128)(2,1)S(1)}, u32[]{:S(2)}, u32[]{:S(2)}) collective-permute-start(bf16[256,768]{1,0:T(8,128)(2,1)S(1)} %add_convert_fusion.7), channel_id=1, source_target_pairs={{0,2},{2,0},{1,3},{3,1},{4,6},{6,4},{5,7},{7,5},{8,10},{10,8},{9,1... | collective-permute-start | bytes 1179656 | tf_op jit(solution)/shard_map/ppermute | solution.py:850
  58.8 2.0 collective-permute-start.12
  59.2 4.3 %collective-permute-start.11 = (bf16[256,768]{1,0:T(8,128)(2,1)S(1)}, bf16[256,768]{1,0:T(8,128)(2,1)S(1)}, u32[]{:S(2)}, u32[]{:S(2)}) collective-permute-start(bf16[256,768]{1,0:T(8,128)(2,1)S(1)} %add_convert_fusion.6.refs_5_.refs_1_), channel_id=1, source_target_pairs={{0,1},{1,0},{2,3},{3,2},{4,5},{5,4},{6,7},{7,6},{8,9},{9,8},{10,11... | collective-permute-start | bytes 1179656 | tf_op jit(solution)/shard_map/ppermute | solution.py:846
  61.9 17.1 %collective-permute-start.14 = (bf16[256,768]{1,0:T(8,128)(2,1)S(1)}, bf16[256,768]{1,0:T(8,128)(2,1)S(1)}, u32[]{:S(2)}, u32[]{:S(2)}) collective-permute-start(bf16[256,768]{1,0:T(8,128)(2,1)S(1)} %add_convert_fusion.5), channel_id=1, source_target_pairs={{0,2},{2,0},{1,3},{3,1},{4,6},{6,4},{5,7},{7,5},{8,10},{10,8},{9,1... | collective-permute-start | bytes 1179656 | tf_op jit(solution)/shard_map/ppermute | solution.py:850
  64.2 15.5 %copy-start.13 = (bf16[512,768]{1,0:T(8,128)(2,1)S(1)}, bf16[512,768]{1,0:T(8,128)(2,1)}, u32[]{:S(2)}) copy-start(bf16[512,768]{1,0:T(8,128)(2,1)} %get-tuple-element.262) | copy-start | bytes 2359300
  79.0 5.0 %collective-permute-start.13 = (bf16[256,768]{1,0:T(8,128)(2,1)}, bf16[256,768]{1,0:T(8,128)(2,1)S(1)}, u32[]{:S(2)}, u32[]{:S(2)}) collective-permute-start(bf16[256,768]{1,0:T(8,128)(2,1)} %get-tuple-element.253), channel_id=1, source_target_pairs={{0,1},{1,0},{2,3},{3,2},{4,5},{5,4},{6,7},{7,6},{8,9},{9,8},{10,11... | collective-permute-start | bytes 1179656 | tf_op jit(solution)/shard_map/ppermute | solution.py:846
  79.2 8.7 %collective-permute-start.16 = (bf16[256,768]{1,0:T(8,128)(2,1)S(1)}, bf16[256,768]{1,0:T(8,128)(2,1)S(1)}, u32[]{:S(2)}, u32[]{:S(2)}) collective-permute-start(bf16[256,768]{1,0:T(8,128)(2,1)S(1)} %add_convert_fusion.4.refs_3_), channel_id=1, source_target_pairs={{0,1},{1,0},{2,3},{3,2},{4,5},{5,4},{6,7},{7,6},{8,9},{9,8},{10,11... | collective-permute-start | bytes 1179656 | tf_op jit(solution)/shard_map/ppermute | solution.py:846
  82.4 16.4 %collective-permute-start.18 = (bf16[384,768]{1,0:T(8,128)(2,1)S(1)}, bf16[384,768]{1,0:T(8,128)(2,1)S(1)}, u32[]{:S(2)}, u32[]{:S(2)}) collective-permute-start(bf16[384,768]{1,0:T(8,128)(2,1)S(1)} %constant_dynamic-slice_fusion.2), channel_id=1, source_target_pairs={{0,4},{4,0},{8,12},{12,8},{16,20},{20,16},{24,28},{28,24},{1,5},{5... | collective-permute-start | bytes 1769480 | tf_op jit(solution)/shard_map/ppermute | solution.py:866
  84.1 12.3 %collective-permute-start.15 = (bf16[256,768]{1,0:T(8,128)(2,1)S(1)}, bf16[256,768]{1,0:T(8,128)(2,1)}, u32[]{:S(2)}, u32[]{:S(2)}) collective-permute-start(bf16[256,768]{1,0:T(8,128)(2,1)S(1)} %add_convert_fusion.3), channel_id=1, source_target_pairs={{0,2},{2,0},{1,3},{3,1},{4,6},{6,4},{5,7},{7,5},{8,10},{10,8},{9,1... | collective-permute-start | bytes 1179656 | tf_op jit(solution)/shard_map/ppermute | solution.py:850
  98.3 2.4 %collective-permute-start.17 = (bf16[256,768]{1,0:T(8,128)(2,1)}, bf16[256,768]{1,0:T(8,128)(2,1)}, u32[]{:S(2)}, u32[]{:S(2)}) collective-permute-start(bf16[256,768]{1,0:T(8,128)(2,1)} %add_convert_fusion.2.refs_3_), channel_id=1, source_target_pairs={{0,1},{1,0},{2,3},{3,2},{4,5},{5,4},{6,7},{7,6},{8,9},{9,8},{10,11... | collective-permute-start | bytes 1179656 | tf_op jit(solution)/shard_map/ppermute | solution.py:846
  98.3 18.6 %collective-permute-start.22 = (bf16[384,768]{1,0:T(8,128)(2,1)}, bf16[384,768]{1,0:T(8,128)(2,1)}, u32[]{:S(2)}, u32[]{:S(2)}) collective-permute-start(bf16[384,768]{1,0:T(8,128)(2,1)} %constant_dynamic-slice_fusion.1), channel_id=1, source_target_pairs={{0,4},{4,0},{8,12},{12,8},{16,20},{20,16},{24,28},{28,24},{1,5},{5... | collective-permute-start | bytes 1769480 | tf_op jit(solution)/shard_map/ppermute | solution.py:866
  99.0 9.8 %collective-permute-start.19 = (bf16[192,768]{1,0:T(8,128)(2,1)S(1)}, bf16[192,768]{1,0:T(8,128)(2,1)S(1)}, u32[]{:S(2)}, u32[]{:S(2)}) collective-permute-start(bf16[192,768]{1,0:T(8,128)(2,1)S(1)} %get-tuple-element.399), channel_id=1, source_target_pairs={{0,8},{4,12},{8,0},{12,4},{16,24},{20,28},{24,16},{28,20},{1,9},{5... | collective-permute-start | bytes 884744 | tf_op jit(solution)/shard_map/ppermute | solution.py:866
  108.9 10.9 %collective-permute-start.21 = (bf16[96,768]{1,0:T(8,128)(2,1)S(1)}, bf16[96,768]{1,0:T(8,128)(2,1)S(1)}, u32[]{:S(2)}, u32[]{:S(2)}) collective-permute-start(bf16[96,768]{1,0:T(8,128)(2,1)S(1)} %get-tuple-element.409), channel_id=1, source_target_pairs={{0,16},{4,20},{8,24},{12,28},{16,0},{20,4},{24,8},{28,12},{1,17},{... | collective-permute-start | bytes 442376 | tf_op jit(solution)/shard_map/ppermute | solution.py:866
  115.3 18.1 %collective-permute-start.20 = (bf16[384,768]{1,0:T(8,128)(2,1)S(1)}, bf16[384,768]{1,0:T(8,128)(2,1)S(1)}, u32[]{:S(2)}, u32[]{:S(2)}) collective-permute-start(bf16[384,768]{1,0:T(8,128)(2,1)S(1)} %constant_dynamic-slice_fusion), channel_id=1, source_target_pairs={{0,4},{4,0},{8,12},{12,8},{16,20},{20,16},{24,28},{28,24},{1,5},{5... | collective-permute-start | bytes 1769480 | tf_op jit(solution)/shard_map/ppermute | solution.py:866
  118.8 11.7 %collective-permute-start.24 = (bf16[192,768]{1,0:T(8,128)(2,1)}, bf16[192,768]{1,0:T(8,128)(2,1)S(1)}, u32[]{:S(2)}, u32[]{:S(2)}) collective-permute-start(bf16[192,768]{1,0:T(8,128)(2,1)} %get-tuple-element.397), channel_id=1, source_target_pairs={{0,8},{4,12},{8,0},{12,4},{16,24},{20,28},{24,16},{28,20},{1,9},{5... | collective-permute-start | bytes 884744 | tf_op jit(solution)/shard_map/ppermute | solution.py:866
  119.9 9.0 %collective-permute-start.23 = (bf16[1,1,1,96,768]{4,3,2,1,0:T(8,128)(2,1)S(1)}, bf16[1,1,1,96,768]{4,3,2,1,0:T(8,128)(2,1)S(1)}, u32[]{:S(2)}, u32[]{:S(2)}) collective-permute-start(bf16[1,1,1,96,768]{4,3,2,1,0:T(8,128)(2,1)S(1)} %bitcast.75), channel_id=1, source_target_pairs={{0,16},{4,20},{8,24},{12,28},{16,0},{20,4},{24,8},{28,12},{1,17},{... | collective-permute-start | bytes 442376 | tf_op jit(solution)/shard_map/ppermute | solution.py:866
  131.3 14.5 %collective-permute-start.28 = (bf16[96,768]{1,0:T(8,128)(2,1)}, bf16[96,768]{1,0:T(8,128)(2,1)}, u32[]{:S(2)}, u32[]{:S(2)}) collective-permute-start(bf16[96,768]{1,0:T(8,128)(2,1)} %get-tuple-element.407), channel_id=1, source_target_pairs={{0,16},{4,20},{8,24},{12,28},{16,0},{20,4},{24,8},{28,12},{1,17},{... | collective-permute-start | bytes 442376 | tf_op jit(solution)/shard_map/ppermute | solution.py:866
  132.8 12.2 %collective-permute-start.26 = (bf16[1,1,2,96,768]{4,3,2,1,0:T(8,128)(2,1)S(1)}, bf16[1,1,2,96,768]{4,3,2,1,0:T(8,128)(2,1)S(1)}, u32[]{:S(2)}, u32[]{:S(2)}) collective-permute-start(bf16[1,1,2,96,768]{4,3,2,1,0:T(8,128)(2,1)S(1)} %broadcast_select_fusion.6), channel_id=1, source_target_pairs={{0,8},{4,12},{8,0},{12,4},{16,24},{20,28},{24,16},{28,20},{1,9},{5... | collective-permute-start | bytes 884744 | tf_op jit(solution)/shard_map/ppermute | solution.py:866
  133.6 16.2 %collective-permute-start.32 = (bf16[192,768]{1,0:T(8,128)(2,1)S(1)}, bf16[192,768]{1,0:T(8,128)(2,1)S(1)}, u32[]{:S(2)}, u32[]{:S(2)}) collective-permute-start(bf16[192,768]{1,0:T(8,128)(2,1)S(1)} %get-tuple-element.395), channel_id=1, source_target_pairs={{0,8},{4,12},{8,0},{12,4},{16,24},{20,28},{24,16},{28,20},{1,9},{5... | collective-permute-start | bytes 884744 | tf_op jit(solution)/shard_map/ppermute | solution.py:866
  143.5 4.7 %collective-permute-start.30 = (bf16[40,768]{1,0:T(8,128)(2,1)}, bf16[40,768]{1,0:T(8,128)(2,1)S(1)}, u32[]{:S(2)}, u32[]{:S(2)}) collective-permute-start(bf16[40,768]{1,0:T(8,128)(2,1)} %get-tuple-element.352), channel_id=1, source_target_pairs={{0,1},{1,0},{2,3},{3,2},{4,5},{5,4},{6,7},{7,6},{8,9},{9,8},{10,11... | collective-permute-start | bytes 184328 | tf_op jit(solution)/shard_map/ppermute | solution.py:846
  143.6 19.8 %collective-permute-start.25 = (bf16[2,8,192,256]{3,2,1,0:T(8,128)(2,1)}, bf16[2,8,192,256]{3,2,1,0:T(8,128)(2,1)S(1)}, u32[]{:S(2)}, u32[]{:S(2)}) collective-permute-start(bf16[2,8,192,256]{3,2,1,0:T(8,128)(2,1)} %get-tuple-element.344), channel_id=1, source_target_pairs={{0,1},{1,0},{2,3},{3,2},{4,5},{5,4},{6,7},{7,6},{8,9},{9,8},{10,11... | collective-permute-start | bytes 4718600 | tf_op jit(solution)/shard_map/ppermute | solution.py:846
  145.1 16.6 %collective-permute-start.27 = (bf16[1,2,2,96,768]{4,3,2,1,0:T(8,128)(2,1)S(1)}, bf16[1,2,2,96,768]{4,3,2,1,0:T(8,128)(2,1)S(1)}, u32[]{:S(2)}, u32[]{:S(2)}) collective-permute-start(bf16[1,2,2,96,768]{4,3,2,1,0:T(8,128)(2,1)S(1)} %broadcast_select_fusion.3), channel_id=1, source_target_pairs={{0,4},{4,0},{8,12},{12,8},{16,20},{20,16},{24,28},{28,24},{1,5},{5... | collective-permute-start | bytes 1769480 | tf_op jit(solution)/shard_map/ppermute | solution.py:866
  146.7 14.8 %collective-permute-start.29 = (bf16[1,1,1,96,768]{4,3,2,1,0:T(8,128)(2,1)S(1)}, bf16[1,1,1,96,768]{4,3,2,1,0:T(8,128)(2,1)S(1)}, u32[]{:S(2)}, u32[]{:S(2)}) collective-permute-start(bf16[1,1,1,96,768]{4,3,2,1,0:T(8,128)(2,1)S(1)} %bitcast.73), channel_id=1, source_target_pairs={{0,16},{4,20},{8,24},{12,28},{16,0},{20,4},{24,8},{28,12},{1,17},{... | collective-permute-start | bytes 442376 | tf_op jit(solution)/shard_map/ppermute | solution.py:866
  148.3 4.3 %collective-permute-start.31 = (bf16[40,768]{1,0:T(8,128)(2,1)S(1)}, bf16[40,768]{1,0:T(8,128)(2,1)S(1)}, u32[]{:S(2)}, u32[]{:S(2)}) collective-permute-start(bf16[40,768]{1,0:T(8,128)(2,1)S(1)} %add_convert_fusion.26), channel_id=1, source_target_pairs={{0,2},{2,0},{1,3},{3,1},{4,6},{6,4},{5,7},{7,5},{8,10},{10,8},{9,1... | collective-permute-start | bytes 184328 | tf_op jit(solution)/shard_map/ppermute | solution.py:850
  149.9 15.9 %collective-permute-start.34 = (bf16[96,768]{1,0:T(8,128)(2,1)S(1)}, bf16[96,768]{1,0:T(8,128)(2,1)S(1)}, u32[]{:S(2)}, u32[]{:S(2)}) collective-permute-start(bf16[96,768]{1,0:T(8,128)(2,1)S(1)} %get-tuple-element.405), channel_id=1, source_target_pairs={{0,16},{4,20},{8,24},{12,28},{16,0},{20,4},{24,8},{28,12},{1,17},{... | collective-permute-start | bytes 442376 | tf_op jit(solution)/shard_map/ppermute | solution.py:866
  152.6 13.1 %collective-permute-start.35 = (bf16[1,42,768]{2,1,0:T(8,128)(2,1)S(1)}, bf16[1,42,768]{2,1,0:T(8,128)(2,1)S(1)}, u32[]{:S(2)}, u32[]{:S(2)}) collective-permute-start(bf16[1,42,768]{2,1,0:T(8,128)(2,1)S(1)} %maximum_bitcast_fusion), channel_id=1, source_target_pairs={{0,16},{4,20},{8,24},{12,28},{16,0},{20,4},{24,8},{28,12},{1,17},{... | collective-permute-start | bytes 193544 | tf_op jit(solution)/shard_map/ppermute | solution.py:866
  161.6 14.4 %collective-permute-start.39 = (bf16[1,1,2,96,768]{4,3,2,1,0:T(8,128)(2,1)S(1)}, bf16[1,1,2,96,768]{4,3,2,1,0:T(8,128)(2,1)S(1)}, u32[]{:S(2)}, u32[]{:S(2)}) collective-permute-start(bf16[1,1,2,96,768]{4,3,2,1,0:T(8,128)(2,1)S(1)} %broadcast_select_fusion.5), channel_id=1, source_target_pairs={{0,8},{4,12},{8,0},{12,4},{16,24},{20,28},{24,16},{28,20},{1,9},{5... | collective-permute-start | bytes 884744 | tf_op jit(solution)/shard_map/ppermute | solution.py:866
  165.8 9.3 %collective-permute-start.36 = (bf16[2,42,768]{2,1,0:T(8,128)(2,1)S(1)}, bf16[2,42,768]{2,1,0:T(8,128)(2,1)S(1)}, u32[]{:S(2)}, u32[]{:S(2)}) collective-permute-start(bf16[2,42,768]{2,1,0:T(8,128)(2,1)S(1)} %constant_dynamic-update-slice_fusion), channel_id=1, source_target_pairs={{0,8},{4,12},{8,0},{12,4},{16,24},{20,28},{24,16},{28,20},{1,9},{5... | collective-permute-start | bytes 387080 | tf_op jit(solution)/shard_map/ppermute | solution.py:866
  166.5 11.0 %collective-permute-start.38 = (bf16[1,1,1,96,768]{4,3,2,1,0:T(8,128)(2,1)S(1)}, bf16[1,1,1,96,768]{4,3,2,1,0:T(8,128)(2,1)S(1)}, u32[]{:S(2)}, u32[]{:S(2)}) collective-permute-start(bf16[1,1,1,96,768]{4,3,2,1,0:T(8,128)(2,1)S(1)} %bitcast.74), channel_id=1, source_target_pairs={{0,4},{4,0},{8,12},{12,8},{16,20},{20,16},{24,28},{28,24},{1,5},{5... | collective-permute-start | bytes 442376 | tf_op jit(solution)/shard_map/ppermute | solution.py:866
  167.3 19.7 %collective-permute-start.33 = (bf16[8,192,256]{2,1,0:T(8,128)(2,1)S(1)}, bf16[8,192,256]{2,1,0:T(8,128)(2,1)}, u32[]{:S(2)}, u32[]{:S(2)}) collective-permute-start(bf16[8,192,256]{2,1,0:T(8,128)(2,1)S(1)} %get-tuple-element.400), channel_id=1, source_target_pairs={{0,2},{2,0},{1,3},{3,1},{4,6},{6,4},{5,7},{7,5},{8,10},{10,8},{9,1... | collective-permute-start | bytes 2359304 | tf_op jit(solution)/shard_map/ppermute | solution.py:850
  175.2 9.9 %collective-permute-start.37 = (bf16[4,42,768]{2,1,0:T(8,128)(2,1)S(1)}, bf16[4,42,768]{2,1,0:T(8,128)(2,1)S(1)}, u32[]{:S(2)}, u32[]{:S(2)}) collective-permute-start(bf16[4,42,768]{2,1,0:T(8,128)(2,1)S(1)} %constant_dynamic-update-slice_fusion.2), channel_id=1, source_target_pairs={{0,4},{4,0},{8,12},{12,8},{16,20},{20,16},{24,28},{28,24},{1,5},{5... | collective-permute-start | bytes 774152 | tf_op jit(solution)/shard_map/ppermute | solution.py:866
  176.1 31.3 %collective-permute-start.42 = (bf16[1,2,2,96,768]{4,3,2,1,0:T(8,128)(2,1)S(1)}, bf16[1,2,2,96,768]{4,3,2,1,0:T(8,128)(2,1)}, u32[]{:S(2)}, u32[]{:S(2)}) collective-permute-start(bf16[1,2,2,96,768]{4,3,2,1,0:T(8,128)(2,1)S(1)} %broadcast_select_fusion.2), channel_id=1, source_target_pairs={{0,4},{4,0},{8,12},{12,8},{16,20},{20,16},{24,28},{28,24},{1,5},{5... | collective-permute-start | bytes 1769480 | tf_op jit(solution)/shard_map/ppermute | solution.py:866
  177.6 14.6 %collective-permute-start.40 = (bf16[2,1,1,96,768]{4,3,0,2,1:T(8,128)(2,1)S(1)}, bf16[2,1,1,96,768]{4,3,0,2,1:T(8,128)(2,1)S(1)}, u32[]{:S(2)}, u32[]{:S(2)}) collective-permute-start(bf16[2,1,1,96,768]{4,3,0,2,1:T(8,128)(2,1)S(1)} %broadcast_select_fusion.4), channel_id=1, source_target_pairs={{0,16},{4,20},{8,24},{12,28},{16,0},{20,4},{24,8},{28,12},{1,17},{... | collective-permute-start | bytes 884744 | tf_op jit(solution)/shard_map/ppermute | solution.py:866
  192.3 18.9 %collective-permute-start.41 = (bf16[2,1,2,96,768]{4,3,2,0,1:T(8,128)(2,1)S(1)}, bf16[2,1,2,96,768]{4,3,2,0,1:T(8,128)(2,1)S(1)}, u32[]{:S(2)}, u32[]{:S(2)}) collective-permute-start(bf16[2,1,2,96,768]{4,3,2,0,1:T(8,128)(2,1)S(1)} %broadcast_select_fusion.1), channel_id=1, source_target_pairs={{0,8},{4,12},{8,0},{12,4},{16,24},{20,28},{24,16},{28,20},{1,9},{5... | collective-permute-start | bytes 1769480 | tf_op jit(solution)/shard_map/ppermute | solution.py:866
  192.4 15.1 %copy-start.29 = (pred[2]{0:T(512)(128)(4,1)S(1)}, pred[2]{0:T(512)(128)(4,1)}, u32[]{:S(2)}) copy-start(pred[2]{0:T(512)(128)(4,1)} %copy-done.28) | copy-start | bytes 10
  (35 other events, 113.0 us)

commit v2 on v1

--- a/solution.py
+++ b/solution.py
@@ -9,9 +9,9 @@
 from jax.sharding import PartitionSpec as P
 
 HEAD_DIM = 64
-FREQ = 256
 SIDE = 16
 PAIR = 2
+PAIRS = 2
 
 BF = jnp.bfloat16
 F32 = jnp.float32
@@ -203,7 +203,7 @@
 
 def attn_kernel_body(
     flow, s_ref, xo, xc, xx, xd, mod, kern, wqkv, wout,
-    full_out, grouped_out, q_out, k_out, v_out, ctx_out, keep_out, send_out,
+    full_out, q_out, k_out, v_out, keep_out, send_out, grouped_out, ctx_out,
     held, padded,
 ):
     n = s_ref[0]
@@ -264,7 +264,7 @@
 
 def ffn_kernel_body(
     first, flow, s_ref, go, gc, gx, gd, full, att, mod, up, down, kern, kgrad_in,
-    g_out, second_out, active_out, gfed_out, ghid_out, keep_out, send_out, mods_out, kgrad_out, fkeep_out, fsend_out,
+    g_out, keep_out, send_out, mods_out, kgrad_out, active_out, gfed_out, second_out, ghid_out, fkeep_out, fsend_out,
     held, padded, slope, gpad, mid, fed, low, sums, turned,
 ):
     n = s_ref[0]
@@ -358,7 +358,7 @@
 
 def attn_back_body(
     flow, s_ref, full, att, gs, gfull, mod, q_in, k_in, v_in, wout, gates,
-    gatt_out, gqkv_out, gmid_out, mods_out,
+    gmid_out, mods_out, gatt_out, gqkv_out,
     sums, gctx,
 ):
     core = jnp.bitwise_and(s_ref[0], 1)
@@ -534,7 +534,7 @@
     n_in, n_out = len(ins), len(outs)
     places, buffer_shapes = [], []
     for array, window, into in ins:
-        dims = array.shape if window is None else (PAIR,) + array.shape[1:]
+        dims = array.shape if window is None else (window[0].size,) + array.shape[1:]
         if into is None:
             buffer_shapes.append((dims, array.dtype))
         elif into[0].start == 0:
@@ -600,6 +600,15 @@
     return (dims, dtype, None, dims)
 
 
+def pair_rows(array, pair):
+    rows = array.shape[0] // PAIRS
+    return (array, (pl.ds(rows * pair, rows),), None)
+
+
+def pair_rows_out(rows, width, pair):
+    return ((PAIRS * rows, width), BF, (pl.ds(rows * pair, rows),), (rows, width))
+
+
 def pair_of(array, pair):
     return (array, (pl.ds(PAIR * pair, PAIR),), None)
 
@@ -641,7 +650,8 @@
 
 
 def condition_body(
-    embedded, bias, time_in, time_out, ada, mod_out, inner_pre, inner, outer_pre, outer, held_in, held_out, held, sums, parts, sems,
+    steps, stamps, wide, bias, time_in, time_out, ada,
+    mod_out, embedded, inner_pre, inner, outer_pre, outer, held_in, held_out, held, sums, parts, rows_of, sems,
 ):
     depth = ada.shape[0]
     per_dev, count, width = mod_out.shape
@@ -650,6 +660,14 @@
     blocks = row_blocks(ada, held, sems.at[pl.ds(2, depth // WEIGHT_ROWS)], WEIGHT_ROWS)
     for copy in [first, second] + blocks:
         copy.start()
+    halved = embedded.shape[1] // 2
+    for r in range(embedded.shape[0]):
+        at = jnp.bitwise_xor(wide[0], steps[r // per_dev]) * per_dev + r % per_dev
+        rows_of[r : r + 1, :] = jnp.broadcast_to(stamps[at].astype(F32), (1, halved))
+    order = lax.broadcasted_iota(jnp.int32, (1, halved), 1).astype(F32)
+    angles = rows_of[...] * jnp.exp(-math.log(10000.0) * order / halved)
+    embedded[:, 0:halved] = jnp.cos(angles)
+    embedded[:, halved:] = jnp.sin(angles)
     first.wait()
     inner_pre[...] = product(embedded[...], held_in[...])
     inner[...] = silu(inner_pre[...])
@@ -676,29 +694,34 @@
             mod_out[lat, k : k + 1, :] = total[lat : lat + 1, k * width : (k + 1) * width]
 
 
-def condition(embedded, time_in, time_out, ada_weight, ada_bias, per_dev, width):
-    latent_total = embedded.shape[0]
+def condition(steps, stamps, wide, time_in, time_out, ada_weight, ada_bias, per_dev, width):
+    latent_total = stamps.shape[0]
     depth, columns = ada_weight.shape
     vmem = pl.BlockSpec(memory_space=pltpu.VMEM)
     anywhere = pl.BlockSpec(memory_space=pl.ANY)
     rows = jax.ShapeDtypeStruct((latent_total, depth), F32)
     return pl.pallas_call(
-        condition_body,
+        functools.partial(condition_body, steps),
         name="condition",
-        in_specs=[vmem, vmem, anywhere, anywhere, anywhere],
-        out_specs=[vmem] * 5,
-        out_shape=[jax.ShapeDtypeStruct((per_dev, columns // width, width), F32), rows, rows, rows, rows],
+        in_specs=[pl.BlockSpec(memory_space=pltpu.SMEM)] * 2 + [vmem, anywhere, anywhere, anywhere],
+        out_specs=[vmem] * 6,
+        out_shape=[
+            jax.ShapeDtypeStruct((per_dev, columns // width, width), F32),
+            jax.ShapeDtypeStruct((latent_total, time_in.shape[0]), F32),
+            rows, rows, rows, rows,
+        ],
         scratch_shapes=[
             pltpu.VMEM(time_in.shape, F32),
             pltpu.VMEM(time_out.shape, F32),
             pltpu.VMEM(ada_weight.shape, F32),
             pltpu.VMEM((8, columns), F32),
             pltpu.VMEM((depth // WEIGHT_ROWS, 8, WEIGHT_ROWS), F32),
+            pltpu.VMEM((latent_total, time_in.shape[0] // 2), F32),
             pltpu.SemaphoreType.DMA((2 + depth // WEIGHT_ROWS,)),
         ],
         compiler_params=pltpu.CompilerParams(vmem_limit_bytes=VMEM_LIMIT),
         cost_estimate=pl.CostEstimate(flops=8 * 10**9, bytes_accessed=10**6, transcendentals=0),
-    )(embedded, ada_bias.reshape(columns // LANES, LANES), time_in, time_out, ada_weight)
+    )(stamps, wide, ada_bias.reshape(columns // LANES, LANES), time_in, time_out, ada_weight)
 
 
 def condition_back_body(
@@ -770,7 +793,7 @@
     )(gmod, embedded, *stages, time_out, ada_weight)
 
 
-def attn_forward(scalars, pair, x_parts, mod, attn_kernel, qkv_weight, out_weight):
+def attn_forward(scalars, pair, x_parts, mod, attn_kernel, qkv_weight, out_weight, held):
     _, share, tokens = x_parts[0].shape
     width = out_weight.shape[1]
     rows = PAIR * tokens
@@ -779,9 +802,10 @@
     return call(
         attn_kernel_body, "attn_fwd", scalars,
         [pair_of(v, pair) for v in x_parts] + [pair_of(mod, pair), whole(attn_kernel), whole(qkv_weight), whole(out_weight)],
-        [whole_out((rows, width), BF), whole_out((rows, width), BF), thin, thin, thin, thin, half, half],
+        [whole_out((rows, width), BF), thin, thin, thin, half, half, pair_rows_out(rows, width, pair),
+         pair_rows_out(rows, share, pair)],
         [pltpu.VMEM((4, share, tokens), BF), pltpu.VMEM((PAIR * (tokens + 2 * SIDE), width), F32)],
-        6_000_000_000,
+        6_000_000_000, held,
     )
 
 
@@ -790,16 +814,15 @@
     width, units = up_weight.shape
     rows = PAIR * tokens
     tall = PAIR * (tokens + 2 * SIDE)
-    broad = whole_out((rows, width), BF)
-    hidden = whole_out((rows, units), BF)
     half = whole_out((tokens, width), BF)
     slices = slices_out(slots, pair, share, tokens)
     return call(
         functools.partial(ffn_kernel_body, pair == 0), "ffn", scalars,
         [pair_of(v, pair) for v in g_parts] + [whole(full)] + stacked(att)
         + [pair_of(mod, pair), whole(up_weight), whole(down_weight), whole(ffn_kernel), whole(taps)],
-        [broad, broad, hidden, broad, hidden, half, half, whole_out((PAIR, 1, width), F32), whole_out((16, units), F32),
-         slices, slices],
+        [whole_out((rows, width), BF), half, half, whole_out((PAIR, 1, width), F32), whole_out((16, units), F32),
+         whole_out((rows, units), BF), whole_out((rows, width), BF), pair_rows_out(rows, width, pair),
+         pair_rows_out(rows, units, pair), slices, slices],
         [pltpu.VMEM((4, share, tokens), BF), pltpu.VMEM((tall, units), F32), pltpu.VMEM((rows, units), F32),
          pltpu.VMEM((tall, units), F32), pltpu.VMEM((rows, width), F32), pltpu.VMEM((rows, width), F32),
          pltpu.VMEM((rows, width), BF), pltpu.VMEM((PAIR, 8, width), F32), pltpu.VMEM((width, tokens), BF)],
@@ -807,7 +830,7 @@
     )
 
 
-def attn_backward(scalars, pair, full, att, gsec, gfull, mod, qkv, out_weight, gates):
+def attn_backward(scalars, pair, full, att, gsec, gfull, mod, qkv, out_weight, gates, held):
     tokens, width = att[0].shape
     share = out_weight.shape[0]
     rows = PAIR * tokens
@@ -816,9 +839,9 @@
         attn_back_body, "attn_bwd", scalars,
         [whole(full)] + stacked(att) + stacked(gsec) + [whole(gfull), pair_of(mod, pair)]
         + [whole(v) for v in qkv] + [whole(out_weight), whole(gates)],
-        [broad, whole_out((rows, 3 * share), BF), broad, whole_out((PAIR, 8, width), F32)],
+        [broad, whole_out((PAIR, 8, width), F32), pair_rows_out(rows, width, pair), pair_rows_out(rows, 3 * share, pair)],
         [pltpu.VMEM((3 * PAIR, 8, width), F32), pltpu.VMEM((rows, share), BF)],
-        6_000_000_000,
+        6_000_000_000, held,
     )
 
 
@@ -832,7 +855,7 @@
     mods = whole_out((PACKED, width), BF) if closing else whole_out((PAIR, 8, width), F32)
     return call(
         functools.partial(input_back_body, closing), "input_bwd", scalars,
-        [whole(full), pair_of(mod, pair), whole(gqkv), whole(qkv_weight), whole(attn_kernel), whole(taps), whole(gmid),
+        [whole(full), pair_of(mod, pair), pair_rows(gqkv, pair), whole(qkv_weight), whole(attn_kernel), whole(taps), whole(gmid),
          whole(mods_in), whole(before)],
         [whole_out((16, width), F32), mods, slices, slices],
         [pltpu.VMEM((rows, width), F32), pltpu.VMEM((rows, LANES), F32), pltpu.VMEM((tall, width), F32),
@@ -971,13 +994,6 @@
     return lax.optimization_barrier((value, others))[0]
 
 
-def embed_times(stamps):
-    halved = FREQ // 2
-    freqs = jnp.exp(-math.log(10000.0) * jnp.arange(halved, dtype=F32) / halved)
-    angles = stamps[:, None] * freqs[None, :]
-    return jnp.concatenate([jnp.cos(angles), jnp.sin(angles)], 1)
-
-
 def body(
     latents, cotangent, timesteps, time_in, time_out, ada_weight, ada_bias,
     attn_kernel, qkv_weight, out_weight, up_weight, ffn_kernel, down_weight,
@@ -994,19 +1010,14 @@
     steps, bit = [0], wide_count // 2
     while bit:
         steps, bit = steps + [k ^ bit for k in steps], bit // 2
-    met = jnp.bitwise_xor(jnp.array(steps, jnp.int32), wide_at)
-    stamps = timesteps.reshape(wide_count, per_dev)[met].reshape(latent_total).astype(F32)
-    embedded = embed_times(stamps)
-    mod, *stages = condition(embedded, time_in, time_out, ada_weight, ada_bias, per_dev, width)
+    mod, embedded, *stages = condition(
+        steps, timesteps, wide_at.astype(jnp.int32).reshape(1), time_in, time_out, ada_weight, ada_bias, per_dev, width
+    )
     x = n // 2
     factor = 1.0 / latent_total
 
-    def token_product(lefts, rights):
-        total = None
-        for a, b in zip(lefts, rights):
-            part = dot_tn(a, b)
-            total = part if total is None else total + part
-        return (total * factor).astype(BF)
+    def token_products(lefts, rights):
+        return (sum(dot_tn(a, b) for a, b in zip(lefts, rights)) * factor).astype(BF)
 
     x_own = jnp.swapaxes(latents, 1, 2)
     g_own = jnp.swapaxes(cotangent, 1, 2)
@@ -1019,17 +1030,17 @@
     x_parts = (x_own, core_swap(x_own), x_across, core_swap(x_across))
     g_parts = (g_own, core_swap(g_own), g_across, core_swap(g_across))
 
-    def attend(pair):
-        return lambda parts: attn_forward(scalars, pair, parts, mod, attn_kernel, qkv_rows, out_weight)
+    def attend(pair, held=()):
+        return lambda parts: attn_forward(scalars, pair, parts, mod, attn_kernel, qkv_rows, out_weight, held)
 
     fwd_a = order(attend(0), x_parts)
-    here_a = order(sum_pair, fwd_a[6], core_swap(fwd_a[7]))
-    fwd_b = order(attend(1), after(x_parts, g_across))
+    here_a = order(sum_pair, fwd_a[4], core_swap(fwd_a[5]))
+    fwd_b = order(attend(1, fwd_a[6:8]), after(x_parts, g_across))
     levels = wide_count.bit_length() - 1
     places = [jnp.bitwise_and(jnp.right_shift(wide_at, k), 1) for k in range(levels)]
     masks = [jnp.arange(2, dtype=jnp.int32) == place for place in places]
     att_a, masks = order(lambda a, b, m: (sum_pair(a, b), m), here_a, x_swap(here_a), masks)
-    here_b = order(sum_pair, fwd_b[6], core_swap(fwd_b[7]))
+    here_b = order(sum_pair, fwd_b[4], core_swap(fwd_b[5]))
     att_a = (att_a, core_swap(att_a))
 
     slots = 2 * per_dev
@@ -1042,21 +1053,21 @@
     ffn_a = order(feed(0, fwd_a[0], ffn_kernel), att_a, g_parts)
     att_b = order(sum_pair, here_b, x_swap(here_b))
     att_b = (att_b, core_swap(att_b))
-    here_a = order(sum_pair, ffn_a[5], core_swap(ffn_a[6]))
-    ffn_b = order(feed(1, fwd_b[0], ffn_a[8], ffn_a[9:11]), att_b, g_parts)
+    here_a = order(sum_pair, ffn_a[1], core_swap(ffn_a[2]))
+    ffn_b = order(feed(1, fwd_b[0], ffn_a[4], ffn_a[7:11]), att_b, g_parts)
     sec_a = order(sum_pair, here_a, x_swap(here_a))
     sec_a = (sec_a, core_swap(sec_a))
-    down_product = order(token_product, [ffn_a[2], ffn_b[2]], [ffn_a[3], ffn_b[3]])
+    down_product = order(token_products, [ffn_a[5], ffn_b[5]], [ffn_a[6], ffn_b[6]])
     down_sum = WideSum(down_product, places, masks, wide_count)
     order.advance(down_sum)
-    here_b = order(sum_pair, ffn_b[5], core_swap(ffn_b[6]))
-    up_product = order(token_product, [ffn_a[1], ffn_b[1]], [ffn_a[4], ffn_b[4]])
+    here_b = order(sum_pair, ffn_b[1], core_swap(ffn_b[2]))
+    up_product = order(token_products, [ffn_b[7]], [ffn_b[8]])
     up_sum = WideSum(up_product, places, masks, wide_count)
     order.advance(up_sum)
 
-    def attend_back(pair, fwd, ffn):
+    def attend_back(pair, fwd, ffn, held=()):
         return lambda att, sec: attn_backward(
-            scalars, pair, fwd[0], att, sec, ffn[0], mod, fwd[2:5], out_weight, ffn[7]
+            scalars, pair, fwd[0], att, sec, ffn[0], mod, fwd[1:4], out_weight, ffn[3], held
         )
 
     def input_back(pair, fwd, taps, before, held):
@@ -1068,22 +1079,22 @@
     sec_b = order(sum_pair, here_b, x_swap(here_b))
     sec_b = (sec_b, core_swap(sec_b))
     order.advance(down_sum)
-    back_b = order(attend_back(1, fwd_b, ffn_b), att_b, sec_b)
+    back_b = order(attend_back(1, fwd_b, ffn_b, back_a[2:4]), att_b, sec_b)
     order.advance(down_sum)
     attn_product = order(
         lambda grads, grouped, contexts, attended: jnp.concatenate(
-            [token_product(grads, grouped), token_product(contexts, attended)], 0
+            [token_products([grads], [grouped]), token_products([contexts], [attended])], 0
         ),
-        [back_a[1], back_b[1]], [fwd_a[1], fwd_b[1]], [fwd_a[5], fwd_b[5]], [back_a[0], back_b[0]],
+        back_b[3], fwd_b[6], fwd_b[7], back_b[2],
     )
     attn_sum = WideSum(attn_product, places, masks, wide_count, [0] + list(range(levels - 1, 0, -1)))
     order.advance(attn_sum)
     order.advance(up_sum)
     order.advance(down_sum)
-    in_a = order(input_back(0, fwd_a, attn_kernel, attn_kernel, ffn_b[9:11]), *back_a[1:4])
+    in_a = order(input_back(0, fwd_a, attn_kernel, attn_kernel, ffn_b[9:11]), back_b[3], *back_a[:2])
     order.advance(down_sum, up_sum)
     order.advance(attn_sum)
-    in_b = order(input_back(1, fwd_b, in_a[0], in_a[1], in_a[2:4]), *back_b[1:4])
+    in_b = order(input_back(1, fwd_b, in_a[0], in_a[1], in_a[2:4]), back_b[3], *back_b[:2])
     order.advance(down_sum)
 
     rows = 6 * per_dev
@@ -1093,7 +1104,7 @@
     whole_rows = lambda a, b, c: join(sum_pair(a, b)[: rows + 9], c[:9].astype(BF))[None]
     mods = Steps(
         (in_b[1], core_swap(in_b[1])),
-        [(sum_pair, lambda v: (v, x_swap(v), ffn_b[8]))]
+        [(sum_pair, lambda v: (v, x_swap(v), ffn_b[4]))]
         + [(work, move) for work, move in zip([whole_rows] + [join] * len(bits), moves)],
     )
     order.advance(up_sum)

time: 214 us -> 212 us (level)
  local copies, waits for them, and re-layouts: 11.8 us -> 7.74 us
    unnamed x83 -> x69, local copies, waits for them, and re-layouts: 7.33 us -> 5.43 us
    dot_general x8 -> x5, matrix products: 5.28 us -> 6.18 us  [dot_tn(): lax.dot_general(a, b, (((0,), (0,)), ((), ())), preferred_element_type=F32)]
  transfers between devices with their start and end apart: 43 -> 43, of which waited for: 13 -> 13; matrix products, arithmetic and copies ran while one was open for 14% -> 13% of each run, Pallas kernels for 48% -> 48%
where the time goes in v2:
time: 212 us; the launch traced here: 211 us
  Pallas kernels  102 us (48%)
  starting transfers between devices  36.6 us (17%)
  waiting for transfers between devices  36.4 us (17%)
  other arithmetic  21.3 us (10%)
  local copies, waits for them, and re-layouts  7.74 us (4%)
  matrix products  6.18 us (3%)
    pallas_call x8, Pallas kernels, call(): pl.pallas_call(run, name=name, out_shape=[jax.ShapeDtypeStruct(o[0], o[1]...  77.8 us
    ppermute x21, waiting for transfers between devices, wide_swap(): return lax.ppermute(v, 'wide', [(i, i ^ bit) for i in range(count)])  29.5 us
    ppermute x21, starting transfers between devices, wide_swap(): return lax.ppermute(v, 'wide', [(i, i ^ bit) for i in range(count)])  22.3 us
    pallas_call x1, Pallas kernels, condition_back(): pl.pallas_call(functools.partial(condition_back_body, factor), name='cond...  15 us
    convert_element_type x21, other arithmetic, sum_pair(): return (a.astype(F32) + b.astype(F32)).astype(BF)  12.9 us
    ppermute x8, starting transfers between devices, x_swap(): return lax.ppermute(v, 'narrow', [(0, 2), (2, 0), (1, 3), (3, 1)])  11.6 us
    pallas_call x1, Pallas kernels, condition(): pl.pallas_call(functools.partial(condition_body, steps), name='condition'...  8.82 us
    dot_general x5, matrix products, dot_tn(): lax.dot_general(a, b, (((0,), (0,)), ((), ())), preferred_element_type=F32)  6.18 us
  transfers between devices with their start and end apart: 43, of which 13 were waited for; matrix products, arithmetic and copies ran while one was open for 13% of the time, Pallas kernels for 48%

profile of v2, /device:TPU:0, one launch (start us, length us, event | category | flops | bytes accessed | tf_op | source)
XLA Modules:
  0.0 211.2 jit_solution(2444841232468079627)
XLA Ops:
  0.6 3.0 %collective-permute-start.1 = (bf16[4,192,256]{2,1,0:T(8,128)(2,1)}, bf16[4,192,256]{2,1,0:T(8,128)(2,1)S(1)}, u32[]{:S(2)}, u32[]{:S(2)}) collective-permute-start(bf16[4,192,256]{2,1,0:T(8,128)(2,1)} %bitcast.82), channel_id=1, source_target_pairs={{0,2},{2,0},{1,3},{3,1},{4,6},{6,4},{5,7},{7,5},{8,10},{10,8},{9,1... | collective-permute-start | bytes 1179656 | tf_op jit(solution)/shard_map/ppermute | solution.py:873
  3.7 8.8 %condition.1 = (f32[4,6,768]{2,1,0:T(8,128)}, f32[32,256]{1,0:T(8,128)}, f32[32,768]{1,0:T(8,128)}, f32[32,768]{1,0:T(8,128)}, f32[32,768]{1,0:T(8,128)}, /*index=5*/f32[32,768]{1,0:T(8,128)}) custom-call(s32[32]{0:T(128)} %stamps.1, s32[1]{0:T(128)} %bitcast.2.wide, f32[36,128]{1,0:T(8,128)} %bitcast.90, f32[256,768]{1,0:T(8,128)} %time_in.1, ...), custom_call_target="tpu_custom_call" | custom-call | flops 8000000000 | bytes 1000000 | tf_op jit(solution)/shard_map/condition/pallas_call | solution.py:703
  13.1 1.7 collective-permute-start.3
  15.7 8.0 %attn_fwd.2 = (bf16[512,768]{1,0:T(8,128)(2,1)}, bf16[512,192]{1,0:T(8,128)(2,1)}, bf16[512,192]{1,0:T(8,128)(2,1)}, bf16[512,192]{1,0:T(8,128)(2,1)}, bf16[256,...) custom-call(s32[1]{0:T(128)} %bitcast.s_ref, ...), custom_call_target="tpu_custom_call" | custom-call | flops 6000000000 | bytes 1000000 | tf_op jit(solution)/shard_map/attn_fwd/pallas_call | solution.py:566
  24.6 1.1 collective-permute-done.4
  25.7 1.1 add_convert_fusion.9
  26.8 1.6 collective-permute-start.6
  28.4 8.1 %attn_fwd.3 = (bf16[512,768]{1,0:T(8,128)(2,1)}, bf16[512,192]{1,0:T(8,128)(2,1)}, bf16[512,192]{1,0:T(8,128)(2,1)}, bf16[512,192]{1,0:T(8,128)(2,1)}, bf16[256,...) custom-call(s32[1]{0:T(128)} %bitcast.s_ref, ...), custom_call_target="tpu_custom_call", output_to_operand_aliasing={{6}: (9, {}), {7}: (10, {})} | custom-call | flops 6000000000 | bytes 1000000 | tf_op jit(solution)/shard_map/attn_fwd/pallas_call | solution.py:566
  36.6 1.5 collective-permute-done.6
  39.6 1.4 collective-permute-start.7
  42.7 14.5 %ffn.2 = (bf16[512,768]{1,0:T(8,128)(2,1)}, bf16[256,768]{1,0:T(8,128)(2,1)}, bf16[256,768]{1,0:T(8,128)(2,1)}, f32[2,1,768]{2,1,0:T(1,128)}, f32[16,768]{1,0:T(...) custom-call(s32[1]{0:T(128)} %bitcast.s_ref, ...), custom_call_target="tpu_custom_call" | custom-call | flops 10000000000 | bytes 1000000 | tf_op jit(solution)/shard_map/ffn/pallas_call | solution.py:566
  57.9 1.2 collective-permute-done.12
  59.2 1.1 add_convert_fusion.5
  61.8 14.8 %ffn.3 = (bf16[512,768]{1,0:T(8,128)(2,1)}, bf16[256,768]{1,0:T(8,128)(2,1)}, bf16[256,768]{1,0:T(8,128)(2,1)}, f32[2,1,768]{2,1,0:T(1,128)}, f32[16,768]{1,0:T(...) custom-call(s32[1]{0:T(128)} %bitcast.s_ref, ...), custom_call_target="tpu_custom_call", output_to_operand_aliasing={{7}: (13, {}), {8}: (14, {}), {9}: (15, {}), {10}: (16, {})} | custom-call | flops 10000000000 | bytes 1000000 | tf_op jit(solution)/shard_map/ffn/pallas_call | solution.py:566
  80.0 1.6 collective-permute-start.18
  81.7 1.4 collective-permute-start.15
  83.2 1.5 multiply_convert_fusion
  85.5 7.8 %attn_bwd.2 = (bf16[512,768]{1,0:T(8,128)(2,1)}, f32[2,8,768]{2,1,0:T(8,128)}, bf16[1024,768]{1,0:T(8,128)(2,1)}, bf16[1024,576]{1,0:T(8,128)(2,1)}) custom-call(s32[1]{0:T(128)} %bitcast.s_ref, bf16[512,768]{1,0:T(8,128)(2,1)} %get-tuple-element.211.refs_4_.refs_0_, bf16[256,768]{1,0:T(8,128)(2,1)} %copy-done.7, bf16[256,768]{1,0:T(8,128)(2,1)} %copy-done.21, ...), custom_call_target="tpu_custom_call" | custom-call | flops 6000000000 | bytes 1000000 | tf_op jit(solution)/shard_map/attn_bwd/pallas_call | solution.py:566
  93.3 1.9 add_convert_fusion.2.refs_3_
  95.7 1.3 add_convert_fusion.14
  96.9 1.6 collective-permute-start.19
  98.6 8.1 %attn_bwd.3 = (bf16[512,768]{1,0:T(8,128)(2,1)}, f32[2,8,768]{2,1,0:T(8,128)}, bf16[1024,768]{1,0:T(8,128)(2,1)}, bf16[1024,576]{1,0:T(8,128)(2,1)}) custom-call(s32[1]{0:T(128)} %bitcast.s_ref, bf16[512,768]{1,0:T(8,128)(2,1)} %get-tuple-element.220.refs_4_.refs_0_, bf16[256,768]{1,0:T(8,128)(2,1)} %copy-done.6, ...), custom_call_target="tpu_custom_call", output_to_operand_aliasing={{2}: (13, {}), {3}: (14, {})} | custom-call | flops 6000000000 | bytes 1000000 | tf_op jit(solution)/shard_map/attn_bwd/pallas_call | solution.py:566
  106.8 2.7 %collective-permute-start.21 = (bf16[96,768]{1,0:T(8,128)(2,1)S(1)}, bf16[96,768]{1,0:T(8,128)(2,1)S(1)}, u32[]{:S(2)}, u32[]{:S(2)}) collective-permute-start(bf16[96,768]{1,0:T(8,128)(2,1)S(1)} %get-tuple-element.399), channel_id=1, source_target_pairs={{0,16},{4,20},{8,24},{12,28},{16,0},{20,4},{24,8},{28,12},{1,17},{... | collective-permute-start | bytes 442376 | tf_op jit(solution)/shard_map/ppermute | solution.py:889
  109.4 1.9 fusion
  111.4 1.1 multiply_convert_fusion.2
  112.7 1.6 collective-permute-start.20
  114.3 2.0 add_convert_fusion.12
  118.0 8.2 %input_bwd.2 = (f32[16,768]{1,0:T(8,128)}, f32[2,8,768]{2,1,0:T(8,128)}, bf16[2,8,192,256]{3,2,1,0:T(8,128)(2,1)}, bf16[2,8,192,256]{3,2,1,0:T(8,128)(2,1)}) custom-call(s32[1]{0:T(128)} %bitcast.s_ref, bf16[512,768]{1,0:T(8,128)(2,1)} %get-tuple-element.211.refs_4_.refs_0_, ...), custom_call_target="tpu_custom_call", output_to_operand_aliasing={{2}: (10, {}), {3}: (11, {})} | custom-call | flops 6000000000 | bytes 1000000 | tf_op jit(solution)/shard_map/input_bwd/pallas_call | solution.py:566
  126.2 1.7 collective-permute-done.24
  129.3 1.1 collective-permute-start.28
  130.4 1.3 add_convert_fusion.10
  131.7 1.9 collective-permute-start.32
  133.7 8.3 %input_bwd.3 = (f32[16,768]{1,0:T(8,128)}, bf16[40,768]{1,0:T(8,128)(2,1)}, bf16[2,8,192,256]{3,2,1,0:T(8,128)(2,1)}, bf16[2,8,192,256]{3,2,1,0:T(8,128)(2,1)}) custom-call(s32[1]{0:T(128)} %bitcast.s_ref, bf16[512,768]{1,0:T(8,128)(2,1)} %get-tuple-element.220.refs_4_.refs_0_, ...), custom_call_target="tpu_custom_call", output_to_operand_aliasing={{2}: (10, {}), {3}: (11, {})} | custom-call | flops 6000000000 | bytes 1000000 | tf_op jit(solution)/shard_map/input_bwd/pallas_call | solution.py:566
  143.3 1.5 collective-permute-start.29
  145.7 1.4 collective-permute-start.34
  147.2 2.0 collective-permute-done.31
  149.2 1.5 collective-permute-start.35
  150.8 7.4 %collective-permute-done.29 = bf16[1,1,1,96,768]{4,3,2,1,0:T(8,128)(2,1)S(1)} collective-permute-done((bf16[1,1,1,96,768]{4,3,2,1,0:T(8,128)(2,1)S(1)}, bf16[1,1,1,96,768]{4,3,2,1,0:T(8,128)(2,1)S(1)}, u32[]{:S(2)}, u32[]{:S(2)}) %collective-permute-start.29) | collective-permute-done | bytes 147488 | tf_op jit(solution)/shard_map/ppermute | solution.py:889
  158.4 1.6 select_convert_fusion.1
  161.0 1.6 collective-permute-done.35
  165.0 7.0 %collective-permute-done.36 = bf16[2,42,768]{2,1,0:T(8,128)(2,1)S(1)} collective-permute-done((bf16[2,42,768]{2,1,0:T(8,128)(2,1)S(1)}, bf16[2,42,768]{2,1,0:T(8,128)(2,1)S(1)}, u32[]{:S(2)}, u32[]{:S(2)}) %collective-permute-start.36) | collective-permute-done | bytes 129056 | tf_op jit(solution)/shard_map/ppermute | solution.py:889
  172.0 1.2 collective-permute-start.37
  174.7 7.2 %collective-permute-done.37 = bf16[4,42,768]{2,1,0:T(8,128)(2,1)S(1)} collective-permute-done((bf16[4,42,768]{2,1,0:T(8,128)(2,1)S(1)}, bf16[4,42,768]{2,1,0:T(8,128)(2,1)S(1)}, u32[]{:S(2)}, u32[]{:S(2)}) %collective-permute-start.37) | collective-permute-done | bytes 258080 | tf_op jit(solution)/shard_map/ppermute | solution.py:889
  183.8 1.3 add_convert_fusion.1
  185.1 4.6 %collective-permute-done.40 = bf16[2,1,1,96,768]{4,3,0,2,1:T(8,128)(2,1)S(1)} collective-permute-done((bf16[2,1,1,96,768]{4,3,0,2,1:T(8,128)(2,1)S(1)}, bf16[2,1,1,96,768]{4,3,0,2,1:T(8,128)(2,1)S(1)}, u32[]{:S(2)}, u32[]{:S(2)}) %collective-permute-start.40) | collective-permute-done | bytes 294944 | tf_op jit(solution)/shard_map/ppermute | solution.py:889
  189.9 15.0 %condition_back.1 = (f32[256,768]{1,0:T(8,128)}, f32[768,768]{1,0:T(8,128)}, f32[768,4608]{1,0:T(8,128)}) custom-call(bf16[32,4608]{1,0:T(8,128)(2,1)} %copy-done, f32[32,256]{1,0:T(8,128)} %get-tuple-element.372.embedded, f32[32,768]{1,0:T(8,128)} %get-tuple-element.373.inner_pre, f32[32,768]{1,0:T(8,128)} %get-tuple-element.374.inner, ...), custom_call_target="tpu_custom_call" | custom-call | flops 1 | bytes 1 | tf_op jit(solution)/shard_map/condition_back/pallas_call | solution.py:772
  205.0 2.8 %select_convert_fusion = f32[2,2,2,96,768]{4,3,2,1,0:T(8,128)} fusion(pred[2]{0:T(512)(128)(4,1)S(1)} %copy-done.17, bf16[2,2,96,768]{3,2,1,0:T(8,128)(2,1)} %bitcast.30, bf16[2,2,96,768]{3,2,1,0:T(8,128)(2,1)S(1)} %bitcast.63), kind=kLoop, calls=%fused_computation.9 | loop fusion | flops 1179648 | bytes 3538946 | tf_op jit(solution)/shard_map/convert_element_type | solution.py:954
  209.8 1.4 convert_bitcast_fusion
  (175 shorter events, 27.2 us)
Async XLA Ops:
  0.6 12.3 %collective-permute-start.1 = (bf16[4,192,256]{2,1,0:T(8,128)(2,1)}, bf16[4,192,256]{2,1,0:T(8,128)(2,1)S(1)}, u32[]{:S(2)}, u32[]{:S(2)}) collective-permute-start(bf16[4,192,256]{2,1,0:T(8,128)(2,1)} %bitcast.82), channel_id=1, source_target_pairs={{0,2},{2,0},{1,3},{3,1},{4,6},{6,4},{5,7},{7,5},{8,10},{10,8},{9,1... | collective-permute-start | bytes 1179656 | tf_op jit(solution)/shard_map/ppermute | solution.py:873
  3.6 11.1 %collective-permute-start = (bf16[4,192,256]{2,1,0:T(8,128)(2,1)}, bf16[4,192,256]{2,1,0:T(8,128)(2,1)S(1)}, u32[]{:S(2)}, u32[]{:S(2)}) collective-permute-start(bf16[4,192,256]{2,1,0:T(8,128)(2,1)} %bitcast.83), channel_id=1, source_target_pairs={{0,1},{1,0},{2,3},{3,2},{4,5},{5,4},{6,7},{7,6},{8,9},{9,8},{10,11... | collective-permute-start | bytes 1179656 | tf_op jit(solution)/shard_map/ppermute | solution.py:869
  13.0 1.8 collective-permute-start.2
  13.1 11.4 %collective-permute-start.3 = (bf16[4,192,256]{2,1,0:T(8,128)(2,1)S(1)}, bf16[4,192,256]{2,1,0:T(8,128)(2,1)S(1)}, u32[]{:S(2)}, u32[]{:S(2)}) collective-permute-start(bf16[4,192,256]{2,1,0:T(8,128)(2,1)S(1)} %bitcast.88), channel_id=1, source_target_pairs={{0,2},{2,0},{1,3},{3,1},{4,6},{6,4},{5,7},{7,5},{8,10},{10,8},{9,1... | collective-permute-start | bytes 1179656 | tf_op jit(solution)/shard_map/ppermute | solution.py:873
  23.7 2.0 collective-permute-start.4
  24.0 17.0 %collective-permute-start.9 = (bf16[4,192,256]{2,1,0:T(8,128)(2,1)S(1)}, bf16[4,192,256]{2,1,0:T(8,128)(2,1)S(1)}, u32[]{:S(2)}, u32[]{:S(2)}) collective-permute-start(bf16[4,192,256]{2,1,0:T(8,128)(2,1)S(1)} %bitcast.89), channel_id=1, source_target_pairs={{0,1},{1,0},{2,3},{3,2},{4,5},{5,4},{6,7},{7,6},{8,9},{9,8},{10,11... | collective-permute-start | bytes 1179656 | tf_op jit(solution)/shard_map/ppermute | solution.py:869
  24.3 150.0 %copy-start.16 = (pred[2]{0:T(512)(128)(4,1)}, pred[2]{0:T(512)(128)(4,1)S(1)}, u32[]{:S(2)}) copy-start(pred[2]{0:T(512)(128)(4,1)S(1)} %iota_compare_fusion.2) | copy-start | bytes 10
  24.3 133.8 %copy-start.14 = (pred[2]{0:T(512)(128)(4,1)}, pred[2]{0:T(512)(128)(4,1)S(1)}, u32[]{:S(2)}) copy-start(pred[2]{0:T(512)(128)(4,1)S(1)} %get-tuple-element.308) | copy-start | bytes 10
  24.3 148.9 %copy-start.12 = (pred[2]{0:T(512)(128)(4,1)}, pred[2]{0:T(512)(128)(4,1)S(1)}, u32[]{:S(2)}) copy-start(pred[2]{0:T(512)(128)(4,1)S(1)} %get-tuple-element.335) | copy-start | bytes 10
  24.5 16.5 %collective-permute-start.10 = (bf16[4,192,256]{2,1,0:T(8,128)(2,1)S(1)}, bf16[4,192,256]{2,1,0:T(8,128)(2,1)S(1)}, u32[]{:S(2)}, u32[]{:S(2)}) collective-permute-start(bf16[4,192,256]{2,1,0:T(8,128)(2,1)S(1)} %collective-permute-done.3.refs_2_), channel_id=1, source_target_pairs={{0,1},{1,0},{2,3},{3,2},{4,5},{5,4},{6,7},{7,6},{8,9},{9,8},{10,11... | collective-permute-start | bytes 1179656 | tf_op jit(solution)/shard_map/ppermute | solution.py:869
  26.8 11.2 %collective-permute-start.6 = (bf16[256,768]{1,0:T(8,128)(2,1)S(1)}, bf16[256,768]{1,0:T(8,128)(2,1)S(1)}, u32[]{:S(2)}, u32[]{:S(2)}) collective-permute-start(bf16[256,768]{1,0:T(8,128)(2,1)S(1)} %add_convert_fusion.9), channel_id=1, source_target_pairs={{0,2},{2,0},{1,3},{3,1},{4,6},{6,4},{5,7},{7,5},{8,10},{10,8},{9,1... | collective-permute-start | bytes 1179656 | tf_op jit(solution)/shard_map/ppermute | solution.py:873
  36.5 2.0 collective-permute-start.5
  38.2 2.8 %collective-permute-start.8 = (bf16[256,768]{1,0:T(8,128)(2,1)S(1)}, bf16[256,768]{1,0:T(8,128)(2,1)S(1)}, u32[]{:S(2)}, u32[]{:S(2)}) collective-permute-start(bf16[256,768]{1,0:T(8,128)(2,1)S(1)} %add_convert_fusion.8.refs_5_.refs_1_), channel_id=1, source_target_pairs={{0,1},{1,0},{2,3},{3,2},{4,5},{5,4},{6,7},{7,6},{8,9},{9,8},{10,11... | collective-permute-start | bytes 1179656 | tf_op jit(solution)/shard_map/ppermute | solution.py:869
  39.6 17.8 %collective-permute-start.7 = (bf16[256,768]{1,0:T(8,128)(2,1)S(1)}, bf16[256,768]{1,0:T(8,128)(2,1)S(1)}, u32[]{:S(2)}, u32[]{:S(2)}) collective-permute-start(bf16[256,768]{1,0:T(8,128)(2,1)S(1)} %add_convert_fusion.7), channel_id=1, source_target_pairs={{0,2},{2,0},{1,3},{3,1},{4,6},{6,4},{5,7},{7,5},{8,10},{10,8},{9,1... | collective-permute-start | bytes 1179656 | tf_op jit(solution)/shard_map/ppermute | solution.py:873
  57.2 2.0 collective-permute-start.12
  57.5 3.5 %collective-permute-start.11 = (bf16[256,768]{1,0:T(8,128)(2,1)S(1)}, bf16[256,768]{1,0:T(8,128)(2,1)S(1)}, u32[]{:S(2)}, u32[]{:S(2)}) collective-permute-start(bf16[256,768]{1,0:T(8,128)(2,1)S(1)} %add_convert_fusion.6.refs_5_.refs_1_), channel_id=1, source_target_pairs={{0,1},{1,0},{2,3},{3,2},{4,5},{5,4},{6,7},{7,6},{8,9},{9,8},{10,11... | collective-permute-start | bytes 1179656 | tf_op jit(solution)/shard_map/ppermute | solution.py:869
  60.3 16.4 %collective-permute-start.14 = (bf16[256,768]{1,0:T(8,128)(2,1)S(1)}, bf16[256,768]{1,0:T(8,128)(2,1)S(1)}, u32[]{:S(2)}, u32[]{:S(2)}) collective-permute-start(bf16[256,768]{1,0:T(8,128)(2,1)S(1)} %add_convert_fusion.5), channel_id=1, source_target_pairs={{0,2},{2,0},{1,3},{3,1},{4,6},{6,4},{5,7},{7,5},{8,10},{10,8},{9,1... | collective-permute-start | bytes 1179656 | tf_op jit(solution)/shard_map/ppermute | solution.py:873
  61.8 15.5 %copy-start.5 = (bf16[512,768]{1,0:T(8,128)(2,1)S(1)}, bf16[512,768]{1,0:T(8,128)(2,1)}, u32[]{:S(2)}) copy-start(bf16[512,768]{1,0:T(8,128)(2,1)} %get-tuple-element.261) | copy-start | bytes 2359300
  76.6 5.0 %collective-permute-start.13 = (bf16[256,768]{1,0:T(8,128)(2,1)}, bf16[256,768]{1,0:T(8,128)(2,1)S(1)}, u32[]{:S(2)}, u32[]{:S(2)}) collective-permute-start(bf16[256,768]{1,0:T(8,128)(2,1)} %get-tuple-element.252), channel_id=1, source_target_pairs={{0,1},{1,0},{2,3},{3,2},{4,5},{5,4},{6,7},{7,6},{8,9},{9,8},{10,11... | collective-permute-start | bytes 1179656 | tf_op jit(solution)/shard_map/ppermute | solution.py:869
  76.8 7.9 %collective-permute-start.16 = (bf16[256,768]{1,0:T(8,128)(2,1)S(1)}, bf16[256,768]{1,0:T(8,128)(2,1)S(1)}, u32[]{:S(2)}, u32[]{:S(2)}) collective-permute-start(bf16[256,768]{1,0:T(8,128)(2,1)S(1)} %add_convert_fusion.4.refs_3_), channel_id=1, source_target_pairs={{0,1},{1,0},{2,3},{3,2},{4,5},{5,4},{6,7},{7,6},{8,9},{9,8},{10,11... | collective-permute-start | bytes 1179656 | tf_op jit(solution)/shard_map/ppermute | solution.py:869
  80.0 15.6 %collective-permute-start.18 = (bf16[384,768]{1,0:T(8,128)(2,1)S(1)}, bf16[384,768]{1,0:T(8,128)(2,1)}, u32[]{:S(2)}, u32[]{:S(2)}) collective-permute-start(bf16[384,768]{1,0:T(8,128)(2,1)S(1)} %constant_dynamic-slice_fusion.2), channel_id=1, source_target_pairs={{0,4},{4,0},{8,12},{12,8},{16,20},{20,16},{24,28},{28,24},{1,5},{5... | collective-permute-start | bytes 1769480 | tf_op jit(solution)/shard_map/ppermute | solution.py:889
  81.7 11.5 %collective-permute-start.15 = (bf16[256,768]{1,0:T(8,128)(2,1)S(1)}, bf16[256,768]{1,0:T(8,128)(2,1)}, u32[]{:S(2)}, u32[]{:S(2)}) collective-permute-start(bf16[256,768]{1,0:T(8,128)(2,1)S(1)} %add_convert_fusion.3), channel_id=1, source_target_pairs={{0,2},{2,0},{1,3},{3,1},{4,6},{6,4},{5,7},{7,5},{8,10},{10,8},{9,1... | collective-permute-start | bytes 1179656 | tf_op jit(solution)/shard_map/ppermute | solution.py:873
  95.1 3.4 %collective-permute-start.17 = (bf16[256,768]{1,0:T(8,128)(2,1)}, bf16[256,768]{1,0:T(8,128)(2,1)}, u32[]{:S(2)}, u32[]{:S(2)}) collective-permute-start(bf16[256,768]{1,0:T(8,128)(2,1)} %add_convert_fusion.2.refs_3_), channel_id=1, source_target_pairs={{0,1},{1,0},{2,3},{3,2},{4,5},{5,4},{6,7},{7,6},{8,9},{9,8},{10,11... | collective-permute-start | bytes 1179656 | tf_op jit(solution)/shard_map/ppermute | solution.py:869
  95.1 19.1 %collective-permute-start.22 = (bf16[384,768]{1,0:T(8,128)(2,1)S(1)}, bf16[384,768]{1,0:T(8,128)(2,1)}, u32[]{:S(2)}, u32[]{:S(2)}) collective-permute-start(bf16[384,768]{1,0:T(8,128)(2,1)S(1)} %constant_dynamic-slice_fusion.1), channel_id=1, source_target_pairs={{0,4},{4,0},{8,12},{12,8},{16,20},{20,16},{24,28},{28,24},{1,5},{5... | collective-permute-start | bytes 1769480 | tf_op jit(solution)/shard_map/ppermute | solution.py:889
  96.9 9.7 %collective-permute-start.19 = (bf16[192,768]{1,0:T(8,128)(2,1)S(1)}, bf16[192,768]{1,0:T(8,128)(2,1)S(1)}, u32[]{:S(2)}, u32[]{:S(2)}) collective-permute-start(bf16[192,768]{1,0:T(8,128)(2,1)S(1)} %get-tuple-element.389), channel_id=1, source_target_pairs={{0,8},{4,12},{8,0},{12,4},{16,24},{20,28},{24,16},{28,20},{1,9},{5... | collective-permute-start | bytes 884744 | tf_op jit(solution)/shard_map/ppermute | solution.py:889
  106.8 10.5 %collective-permute-start.21 = (bf16[96,768]{1,0:T(8,128)(2,1)S(1)}, bf16[96,768]{1,0:T(8,128)(2,1)S(1)}, u32[]{:S(2)}, u32[]{:S(2)}) collective-permute-start(bf16[96,768]{1,0:T(8,128)(2,1)S(1)} %get-tuple-element.399), channel_id=1, source_target_pairs={{0,16},{4,20},{8,24},{12,28},{16,0},{20,4},{24,8},{28,12},{1,17},{... | collective-permute-start | bytes 442376 | tf_op jit(solution)/shard_map/ppermute | solution.py:889
  112.7 17.8 %collective-permute-start.20 = (bf16[384,768]{1,0:T(8,128)(2,1)S(1)}, bf16[384,768]{1,0:T(8,128)(2,1)}, u32[]{:S(2)}, u32[]{:S(2)}) collective-permute-start(bf16[384,768]{1,0:T(8,128)(2,1)S(1)} %constant_dynamic-slice_fusion), channel_id=1, source_target_pairs={{0,4},{4,0},{8,12},{12,8},{16,20},{20,16},{24,28},{28,24},{1,5},{5... | collective-permute-start | bytes 1769480 | tf_op jit(solution)/shard_map/ppermute | solution.py:889
  116.2 11.7 %collective-permute-start.24 = (bf16[192,768]{1,0:T(8,128)(2,1)}, bf16[192,768]{1,0:T(8,128)(2,1)S(1)}, u32[]{:S(2)}, u32[]{:S(2)}) collective-permute-start(bf16[192,768]{1,0:T(8,128)(2,1)} %get-tuple-element.387), channel_id=1, source_target_pairs={{0,8},{4,12},{8,0},{12,4},{16,24},{20,28},{24,16},{28,20},{1,9},{5... | collective-permute-start | bytes 884744 | tf_op jit(solution)/shard_map/ppermute | solution.py:889
  117.3 8.9 %collective-permute-start.23 = (bf16[1,1,1,96,768]{4,3,2,1,0:T(8,128)(2,1)S(1)}, bf16[1,1,1,96,768]{4,3,2,1,0:T(8,128)(2,1)S(1)}, u32[]{:S(2)}, u32[]{:S(2)}) collective-permute-start(bf16[1,1,1,96,768]{4,3,2,1,0:T(8,128)(2,1)S(1)} %bitcast.70), channel_id=1, source_target_pairs={{0,16},{4,20},{8,24},{12,28},{16,0},{20,4},{24,8},{28,12},{1,17},{... | collective-permute-start | bytes 442376 | tf_op jit(solution)/shard_map/ppermute | solution.py:889
  128.0 14.6 %collective-permute-start.26 = (bf16[1,1,2,96,768]{4,3,2,1,0:T(8,128)(2,1)S(1)}, bf16[1,1,2,96,768]{4,3,2,1,0:T(8,128)(2,1)S(1)}, u32[]{:S(2)}, u32[]{:S(2)}) collective-permute-start(bf16[1,1,2,96,768]{4,3,2,1,0:T(8,128)(2,1)S(1)} %broadcast_select_fusion.6), channel_id=1, source_target_pairs={{0,8},{4,12},{8,0},{12,4},{16,24},{20,28},{24,16},{28,20},{1,9},{5... | collective-permute-start | bytes 884744 | tf_op jit(solution)/shard_map/ppermute | solution.py:889
  129.3 14.0 %collective-permute-start.28 = (bf16[96,768]{1,0:T(8,128)(2,1)}, bf16[96,768]{1,0:T(8,128)(2,1)S(1)}, u32[]{:S(2)}, u32[]{:S(2)}) collective-permute-start(bf16[96,768]{1,0:T(8,128)(2,1)} %get-tuple-element.397), channel_id=1, source_target_pairs={{0,16},{4,20},{8,24},{12,28},{16,0},{20,4},{24,8},{28,12},{1,17},{... | collective-permute-start | bytes 442376 | tf_op jit(solution)/shard_map/ppermute | solution.py:889
  131.7 14.0 %collective-permute-start.32 = (bf16[192,768]{1,0:T(8,128)(2,1)S(1)}, bf16[192,768]{1,0:T(8,128)(2,1)S(1)}, u32[]{:S(2)}, u32[]{:S(2)}) collective-permute-start(bf16[192,768]{1,0:T(8,128)(2,1)S(1)} %get-tuple-element.385), channel_id=1, source_target_pairs={{0,8},{4,12},{8,0},{12,4},{16,24},{20,28},{24,16},{28,20},{1,9},{5... | collective-permute-start | bytes 884744 | tf_op jit(solution)/shard_map/ppermute | solution.py:889
  142.0 2.9 %collective-permute-start.30 = (bf16[40,768]{1,0:T(8,128)(2,1)}, bf16[40,768]{1,0:T(8,128)(2,1)S(1)}, u32[]{:S(2)}, u32[]{:S(2)}) collective-permute-start(bf16[40,768]{1,0:T(8,128)(2,1)} %get-tuple-element.341), channel_id=1, source_target_pairs={{0,1},{1,0},{2,3},{3,2},{4,5},{5,4},{6,7},{7,6},{8,9},{9,8},{10,11... | collective-permute-start | bytes 184328 | tf_op jit(solution)/shard_map/ppermute | solution.py:869
  142.1 17.9 %collective-permute-start.25 = (bf16[2,8,192,256]{3,2,1,0:T(8,128)(2,1)}, bf16[2,8,192,256]{3,2,1,0:T(8,128)(2,1)S(1)}, u32[]{:S(2)}, u32[]{:S(2)}) collective-permute-start(bf16[2,8,192,256]{3,2,1,0:T(8,128)(2,1)} %get-tuple-element.333), channel_id=1, source_target_pairs={{0,1},{1,0},{2,3},{3,2},{4,5},{5,4},{6,7},{7,6},{8,9},{9,8},{10,11... | collective-permute-start | bytes 4718600 | tf_op jit(solution)/shard_map/ppermute | solution.py:869
  142.7 15.6 %collective-permute-start.27 = (bf16[1,2,2,96,768]{4,3,2,1,0:T(8,128)(2,1)S(1)}, bf16[1,2,2,96,768]{4,3,2,1,0:T(8,128)(2,1)S(1)}, u32[]{:S(2)}, u32[]{:S(2)}) collective-permute-start(bf16[1,2,2,96,768]{4,3,2,1,0:T(8,128)(2,1)S(1)} %broadcast_select_fusion.3), channel_id=1, source_target_pairs={{0,4},{4,0},{8,12},{12,8},{16,20},{20,16},{24,28},{28,24},{1,5},{5... | collective-permute-start | bytes 1769480 | tf_op jit(solution)/shard_map/ppermute | solution.py:889
  143.3 14.8 %collective-permute-start.29 = (bf16[1,1,1,96,768]{4,3,2,1,0:T(8,128)(2,1)S(1)}, bf16[1,1,1,96,768]{4,3,2,1,0:T(8,128)(2,1)S(1)}, u32[]{:S(2)}, u32[]{:S(2)}) collective-permute-start(bf16[1,1,1,96,768]{4,3,2,1,0:T(8,128)(2,1)S(1)} %bitcast.68), channel_id=1, source_target_pairs={{0,16},{4,20},{8,24},{12,28},{16,0},{20,4},{24,8},{28,12},{1,17},{... | collective-permute-start | bytes 442376 | tf_op jit(solution)/shard_map/ppermute | solution.py:889
  144.9 4.3 %collective-permute-start.31 = (bf16[40,768]{1,0:T(8,128)(2,1)S(1)}, bf16[40,768]{1,0:T(8,128)(2,1)S(1)}, u32[]{:S(2)}, u32[]{:S(2)}) collective-permute-start(bf16[40,768]{1,0:T(8,128)(2,1)S(1)} %add_convert_fusion.26), channel_id=1, source_target_pairs={{0,2},{2,0},{1,3},{3,1},{4,6},{6,4},{5,7},{7,5},{8,10},{10,8},{9,1... | collective-permute-start | bytes 184328 | tf_op jit(solution)/shard_map/ppermute | solution.py:873
  145.7 16.9 %collective-permute-start.34 = (bf16[96,768]{1,0:T(8,128)(2,1)S(1)}, bf16[96,768]{1,0:T(8,128)(2,1)S(1)}, u32[]{:S(2)}, u32[]{:S(2)}) collective-permute-start(bf16[96,768]{1,0:T(8,128)(2,1)S(1)} %get-tuple-element.395), channel_id=1, source_target_pairs={{0,16},{4,20},{8,24},{12,28},{16,0},{20,4},{24,8},{28,12},{1,17},{... | collective-permute-start | bytes 442376 | tf_op jit(solution)/shard_map/ppermute | solution.py:889
  149.2 13.4 %collective-permute-start.35 = (bf16[1,42,768]{2,1,0:T(8,128)(2,1)S(1)}, bf16[1,42,768]{2,1,0:T(8,128)(2,1)S(1)}, u32[]{:S(2)}, u32[]{:S(2)}) collective-permute-start(bf16[1,42,768]{2,1,0:T(8,128)(2,1)S(1)} %maximum_bitcast_fusion), channel_id=1, source_target_pairs={{0,16},{4,20},{8,24},{12,28},{16,0},{20,4},{24,8},{28,12},{1,17},{... | collective-permute-start | bytes 193544 | tf_op jit(solution)/shard_map/ppermute | solution.py:889
  158.3 14.9 %collective-permute-start.39 = (bf16[1,1,2,96,768]{4,3,2,1,0:T(8,128)(2,1)S(1)}, bf16[1,1,2,96,768]{4,3,2,1,0:T(8,128)(2,1)S(1)}, u32[]{:S(2)}, u32[]{:S(2)}) collective-permute-start(bf16[1,1,2,96,768]{4,3,2,1,0:T(8,128)(2,1)S(1)} %broadcast_select_fusion.5), channel_id=1, source_target_pairs={{0,8},{4,12},{8,0},{12,4},{16,24},{20,28},{24,16},{28,20},{1,9},{5... | collective-permute-start | bytes 884744 | tf_op jit(solution)/shard_map/ppermute | solution.py:889
  162.6 9.3 %collective-permute-start.36 = (bf16[2,42,768]{2,1,0:T(8,128)(2,1)S(1)}, bf16[2,42,768]{2,1,0:T(8,128)(2,1)S(1)}, u32[]{:S(2)}, u32[]{:S(2)}) collective-permute-start(bf16[2,42,768]{2,1,0:T(8,128)(2,1)S(1)} %constant_dynamic-update-slice_fusion), channel_id=1, source_target_pairs={{0,8},{4,12},{8,0},{12,4},{16,24},{20,28},{24,16},{28,20},{1,9},{5... | collective-permute-start | bytes 387080 | tf_op jit(solution)/shard_map/ppermute | solution.py:889
  163.2 11.2 %collective-permute-start.38 = (bf16[1,1,1,96,768]{4,3,2,1,0:T(8,128)(2,1)S(1)}, bf16[1,1,1,96,768]{4,3,2,1,0:T(8,128)(2,1)S(1)}, u32[]{:S(2)}, u32[]{:S(2)}) collective-permute-start(bf16[1,1,1,96,768]{4,3,2,1,0:T(8,128)(2,1)S(1)} %bitcast.69), channel_id=1, source_target_pairs={{0,4},{4,0},{8,12},{12,8},{16,20},{20,16},{24,28},{28,24},{1,5},{5... | collective-permute-start | bytes 442376 | tf_op jit(solution)/shard_map/ppermute | solution.py:889
  164.0 19.8 %collective-permute-start.33 = (bf16[8,192,256]{2,1,0:T(8,128)(2,1)S(1)}, bf16[8,192,256]{2,1,0:T(8,128)(2,1)}, u32[]{:S(2)}, u32[]{:S(2)}) collective-permute-start(bf16[8,192,256]{2,1,0:T(8,128)(2,1)S(1)} %get-tuple-element.390), channel_id=1, source_target_pairs={{0,2},{2,0},{1,3},{3,1},{4,6},{6,4},{5,7},{7,5},{8,10},{10,8},{9,1... | collective-permute-start | bytes 2359304 | tf_op jit(solution)/shard_map/ppermute | solution.py:873
  172.0 9.9 %collective-permute-start.37 = (bf16[4,42,768]{2,1,0:T(8,128)(2,1)S(1)}, bf16[4,42,768]{2,1,0:T(8,128)(2,1)S(1)}, u32[]{:S(2)}, u32[]{:S(2)}) collective-permute-start(bf16[4,42,768]{2,1,0:T(8,128)(2,1)S(1)} %constant_dynamic-update-slice_fusion.2), channel_id=1, source_target_pairs={{0,4},{4,0},{8,12},{12,8},{16,20},{20,16},{24,28},{28,24},{1,5},{5... | collective-permute-start | bytes 774152 | tf_op jit(solution)/shard_map/ppermute | solution.py:889
  173.3 31.7 %collective-permute-start.42 = (bf16[1,2,2,96,768]{4,3,2,1,0:T(8,128)(2,1)S(1)}, bf16[1,2,2,96,768]{4,3,2,1,0:T(8,128)(2,1)}, u32[]{:S(2)}, u32[]{:S(2)}) collective-permute-start(bf16[1,2,2,96,768]{4,3,2,1,0:T(8,128)(2,1)S(1)} %broadcast_select_fusion.2), channel_id=1, source_target_pairs={{0,4},{4,0},{8,12},{12,8},{16,20},{20,16},{24,28},{28,24},{1,5},{5... | collective-permute-start | bytes 1769480 | tf_op jit(solution)/shard_map/ppermute | solution.py:889
  174.4 15.3 %collective-permute-start.40 = (bf16[2,1,1,96,768]{4,3,0,2,1:T(8,128)(2,1)S(1)}, bf16[2,1,1,96,768]{4,3,0,2,1:T(8,128)(2,1)S(1)}, u32[]{:S(2)}, u32[]{:S(2)}) collective-permute-start(bf16[2,1,1,96,768]{4,3,0,2,1:T(8,128)(2,1)S(1)} %broadcast_select_fusion.4), channel_id=1, source_target_pairs={{0,16},{4,20},{8,24},{12,28},{16,0},{20,4},{24,8},{28,12},{1,17},{... | collective-permute-start | bytes 884744 | tf_op jit(solution)/shard_map/ppermute | solution.py:889
  189.9 18.9 %collective-permute-start.41 = (bf16[2,1,2,96,768]{4,3,2,0,1:T(8,128)(2,1)S(1)}, bf16[2,1,2,96,768]{4,3,2,0,1:T(8,128)(2,1)S(1)}, u32[]{:S(2)}, u32[]{:S(2)}) collective-permute-start(bf16[2,1,2,96,768]{4,3,2,0,1:T(8,128)(2,1)S(1)} %broadcast_select_fusion.1), channel_id=1, source_target_pairs={{0,8},{4,12},{8,0},{12,4},{16,24},{20,28},{24,16},{28,20},{1,9},{5... | collective-permute-start | bytes 1769480 | tf_op jit(solution)/shard_map/ppermute | solution.py:889
  189.9 15.1 %copy-start.17 = (pred[2]{0:T(512)(128)(4,1)S(1)}, pred[2]{0:T(512)(128)(4,1)}, u32[]{:S(2)}) copy-start(pred[2]{0:T(512)(128)(4,1)} %copy-done.16) | copy-start | bytes 10
  (28 other events, 98.5 us)

commit v3 on v2

--- a/solution.py
+++ b/solution.py
@@ -1132,18 +1132,21 @@
     unpacked = order(lambda a, b: unpack(join(a, b)), *mods.came)
     order.last = tuple(unpacked)
     gmod, ada_bias_grad, attn_taps, ffn_taps = unpacked
-    finals = order(sum_pair, made[0], x_swap(made[1]))
+    final_out, final_grad = order(
+        lambda a, b: (sum_pair(a[:per_dev], b[:per_dev]), sum_pair(a[per_dev:], b[per_dev:])), made[0], x_swap(made[1])
+    )
+    order.last = (final_out, final_grad)
+    up_grad = up_sum.finish(order, F32)
     while not attn_sum.done():
         order.advance(attn_sum)
     time_in_grad, time_out_grad, ada_weight_grad = order(
         lambda g: condition_back(g, embedded, stages, time_out, ada_weight, factor), gmod
     )
-    up_grad = up_sum.finish(order, F32)
     attn_grads = attn_sum.finish(order, BF)
     qkv_rows_grad, out_grad = attn_grads[: 3 * share].astype(F32), attn_grads[3 * share :].astype(F32)
     qkv_grad = jnp.swapaxes(qkv_rows_grad.reshape(3, share, width), 1, 2)
-    final_out = jnp.swapaxes(finals[:per_dev], 1, 2)
-    final_grad = jnp.swapaxes(finals[per_dev:], 1, 2)
+    final_out = jnp.swapaxes(final_out, 1, 2)
+    final_grad = jnp.swapaxes(final_grad, 1, 2)
     return (
         final_out, final_grad, time_in_grad, time_out_grad, ada_weight_grad, ada_bias_grad,
         attn_taps, qkv_grad, out_grad, up_grad, ffn_taps, down_grad,

time: 212 us -> 215 us (1.014)
  waiting for transfers between devices: 36.4 us -> 39.7 us
    ppermute x21, waiting for transfers between devices: 29.5 us -> 32.9 us  [wide_swap(): return lax.ppermute(v, 'wide', [(i, i ^ bit) for i in range(count)])]
    unnamed x69 -> x57, local copies, waits for them, and re-layouts: 5.43 us -> 5.48 us
  transfers between devices with their start and end apart: 43 -> 43, of which waited for: 13 -> 13; matrix products, arithmetic and copies ran while one was open for 13% -> 13% of each run, Pallas kernels for 48% -> 47%
where the time goes in v3:
time: 215 us; the launch traced here: 214 us
  Pallas kernels  102 us (47%)
  waiting for transfers between devices  39.7 us (18%)
  starting transfers between devices  36.6 us (17%)
  other arithmetic  22.1 us (10%)
  local copies, waits for them, and re-layouts  6.84 us (3%)
  matrix products  6.18 us (3%)
    pallas_call x8, Pallas kernels, call(): pl.pallas_call(run, name=name, out_shape=[jax.ShapeDtypeStruct(o[0], o[1]...  77.8 us
    ppermute x21, waiting for transfers between devices, wide_swap(): return lax.ppermute(v, 'wide', [(i, i ^ bit) for i in range(count)])  32.9 us
    ppermute x21, starting transfers between devices, wide_swap(): return lax.ppermute(v, 'wide', [(i, i ^ bit) for i in range(count)])  22.3 us
    pallas_call x1, Pallas kernels, condition_back(): pl.pallas_call(functools.partial(condition_back_body, factor), name='cond...  15 us
    convert_element_type x21, other arithmetic, sum_pair(): return (a.astype(F32) + b.astype(F32)).astype(BF)  13.8 us
    ppermute x8, starting transfers between devices, x_swap(): return lax.ppermute(v, 'narrow', [(0, 2), (2, 0), (1, 3), (3, 1)])  11.6 us
    pallas_call x1, Pallas kernels, condition(): pl.pallas_call(functools.partial(condition_body, steps), name='condition'...  8.82 us
    dot_general x5, matrix products, dot_tn(): lax.dot_general(a, b, (((0,), (0,)), ((), ())), preferred_element_type=F32)  6.18 us
  transfers between devices with their start and end apart: 43, of which 13 were waited for; matrix products, arithmetic and copies ran while one was open for 13% of the time, Pallas kernels for 47%

profile of v3, /device:TPU:0, one launch (start us, length us, event | category | flops | bytes accessed | tf_op | source)
XLA Modules:
  0.0 214.5 jit_solution(1654498515437541414)
XLA Ops:
  0.6 3.0 %collective-permute-start.1 = (bf16[4,192,256]{2,1,0:T(8,128)(2,1)}, bf16[4,192,256]{2,1,0:T(8,128)(2,1)S(1)}, u32[]{:S(2)}, u32[]{:S(2)}) collective-permute-start(bf16[4,192,256]{2,1,0:T(8,128)(2,1)} %bitcast.82), channel_id=1, source_target_pairs={{0,2},{2,0},{1,3},{3,1},{4,6},{6,4},{5,7},{7,5},{8,10},{10,8},{9,1... | collective-permute-start | bytes 1179656 | tf_op jit(solution)/shard_map/ppermute | solution.py:873
  3.7 8.8 %condition.1 = (f32[4,6,768]{2,1,0:T(8,128)}, f32[32,256]{1,0:T(8,128)}, f32[32,768]{1,0:T(8,128)}, f32[32,768]{1,0:T(8,128)}, f32[32,768]{1,0:T(8,128)}, /*index=5*/f32[32,768]{1,0:T(8,128)}) custom-call(s32[32]{0:T(128)} %stamps.1, s32[1]{0:T(128)} %bitcast.2.wide, f32[36,128]{1,0:T(8,128)} %bitcast.90, f32[256,768]{1,0:T(8,128)} %time_in.1, ...), custom_call_target="tpu_custom_call" | custom-call | flops 8000000000 | bytes 1000000 | tf_op jit(solution)/shard_map/condition/pallas_call | solution.py:703
  13.1 1.7 collective-permute-start.3
  15.7 8.0 %attn_fwd.2 = (bf16[512,768]{1,0:T(8,128)(2,1)}, bf16[512,192]{1,0:T(8,128)(2,1)}, bf16[512,192]{1,0:T(8,128)(2,1)}, bf16[512,192]{1,0:T(8,128)(2,1)}, bf16[256,...) custom-call(s32[1]{0:T(128)} %bitcast.s_ref, ...), custom_call_target="tpu_custom_call" | custom-call | flops 6000000000 | bytes 1000000 | tf_op jit(solution)/shard_map/attn_fwd/pallas_call | solution.py:566
  24.6 1.2 collective-permute-done.4
  25.7 1.1 add_convert_fusion.10
  26.8 1.6 collective-permute-start.6
  28.4 8.1 %attn_fwd.3 = (bf16[512,768]{1,0:T(8,128)(2,1)}, bf16[512,192]{1,0:T(8,128)(2,1)}, bf16[512,192]{1,0:T(8,128)(2,1)}, bf16[512,192]{1,0:T(8,128)(2,1)}, bf16[256,...) custom-call(s32[1]{0:T(128)} %bitcast.s_ref, ...), custom_call_target="tpu_custom_call", output_to_operand_aliasing={{6}: (9, {}), {7}: (10, {})} | custom-call | flops 6000000000 | bytes 1000000 | tf_op jit(solution)/shard_map/attn_fwd/pallas_call | solution.py:566
  36.6 1.5 collective-permute-done.6
  39.6 1.4 collective-permute-start.7
  42.7 14.5 %ffn.2 = (bf16[512,768]{1,0:T(8,128)(2,1)}, bf16[256,768]{1,0:T(8,128)(2,1)}, bf16[256,768]{1,0:T(8,128)(2,1)}, f32[2,1,768]{2,1,0:T(1,128)}, f32[16,768]{1,0:T(...) custom-call(s32[1]{0:T(128)} %bitcast.s_ref, ...), custom_call_target="tpu_custom_call" | custom-call | flops 10000000000 | bytes 1000000 | tf_op jit(solution)/shard_map/ffn/pallas_call | solution.py:566
  58.0 1.2 collective-permute-done.12
  59.2 1.1 add_convert_fusion.6
  61.8 14.8 %ffn.3 = (bf16[512,768]{1,0:T(8,128)(2,1)}, bf16[256,768]{1,0:T(8,128)(2,1)}, bf16[256,768]{1,0:T(8,128)(2,1)}, f32[2,1,768]{2,1,0:T(1,128)}, f32[16,768]{1,0:T(...) custom-call(s32[1]{0:T(128)} %bitcast.s_ref, ...), custom_call_target="tpu_custom_call", output_to_operand_aliasing={{7}: (13, {}), {8}: (14, {}), {9}: (15, {}), {10}: (16, {})} | custom-call | flops 10000000000 | bytes 1000000 | tf_op jit(solution)/shard_map/ffn/pallas_call | solution.py:566
  80.1 1.6 collective-permute-start.18
  81.8 1.4 collective-permute-start.15
  83.2 1.5 multiply_convert_fusion
  85.6 7.8 %attn_bwd.2 = (bf16[512,768]{1,0:T(8,128)(2,1)}, f32[2,8,768]{2,1,0:T(8,128)}, bf16[1024,768]{1,0:T(8,128)(2,1)}, bf16[1024,576]{1,0:T(8,128)(2,1)}) custom-call(s32[1]{0:T(128)} %bitcast.s_ref, bf16[512,768]{1,0:T(8,128)(2,1)} %get-tuple-element.211.refs_4_.refs_0_, bf16[256,768]{1,0:T(8,128)(2,1)} %copy-done.7, bf16[256,768]{1,0:T(8,128)(2,1)} %copy-done.15, ...), custom_call_target="tpu_custom_call" | custom-call | flops 6000000000 | bytes 1000000 | tf_op jit(solution)/shard_map/attn_bwd/pallas_call | solution.py:566
  93.4 1.9 add_convert_fusion.3.refs_3_
  95.8 1.3 add_convert_fusion.15
  97.0 1.6 collective-permute-start.19
  98.7 8.1 %attn_bwd.3 = (bf16[512,768]{1,0:T(8,128)(2,1)}, f32[2,8,768]{2,1,0:T(8,128)}, bf16[1024,768]{1,0:T(8,128)(2,1)}, bf16[1024,576]{1,0:T(8,128)(2,1)}) custom-call(s32[1]{0:T(128)} %bitcast.s_ref, bf16[512,768]{1,0:T(8,128)(2,1)} %get-tuple-element.220.refs_4_.refs_0_, bf16[256,768]{1,0:T(8,128)(2,1)} %copy-done.6, ...), custom_call_target="tpu_custom_call", output_to_operand_aliasing={{2}: (13, {}), {3}: (14, {})} | custom-call | flops 6000000000 | bytes 1000000 | tf_op jit(solution)/shard_map/attn_bwd/pallas_call | solution.py:566
  106.9 2.6 %collective-permute-start.21 = (bf16[96,768]{1,0:T(8,128)(2,1)S(1)}, bf16[96,768]{1,0:T(8,128)(2,1)S(1)}, u32[]{:S(2)}, u32[]{:S(2)}) collective-permute-start(bf16[96,768]{1,0:T(8,128)(2,1)S(1)} %get-tuple-element.399), channel_id=1, source_target_pairs={{0,16},{4,20},{8,24},{12,28},{16,0},{20,4},{24,8},{28,12},{1,17},{... | collective-permute-start | bytes 442376 | tf_op jit(solution)/shard_map/ppermute | solution.py:889
  109.5 1.9 fusion
  111.5 1.1 multiply_convert_fusion.2
  112.8 1.6 collective-permute-start.20
  114.4 2.0 add_convert_fusion.13
  118.1 8.2 %input_bwd.2 = (f32[16,768]{1,0:T(8,128)}, f32[2,8,768]{2,1,0:T(8,128)}, bf16[2,8,192,256]{3,2,1,0:T(8,128)(2,1)}, bf16[2,8,192,256]{3,2,1,0:T(8,128)(2,1)}) custom-call(s32[1]{0:T(128)} %bitcast.s_ref, bf16[512,768]{1,0:T(8,128)(2,1)} %get-tuple-element.211.refs_4_.refs_0_, ...), custom_call_target="tpu_custom_call", output_to_operand_aliasing={{2}: (10, {}), {3}: (11, {})} | custom-call | flops 6000000000 | bytes 1000000 | tf_op jit(solution)/shard_map/input_bwd/pallas_call | solution.py:566
  126.3 1.7 collective-permute-done.24
  129.4 1.1 collective-permute-start.28
  130.6 1.3 add_convert_fusion.11
  131.8 1.9 collective-permute-start.32
  133.8 8.3 %input_bwd.3 = (f32[16,768]{1,0:T(8,128)}, bf16[40,768]{1,0:T(8,128)(2,1)}, bf16[2,8,192,256]{3,2,1,0:T(8,128)(2,1)}, bf16[2,8,192,256]{3,2,1,0:T(8,128)(2,1)}) custom-call(s32[1]{0:T(128)} %bitcast.s_ref, bf16[512,768]{1,0:T(8,128)(2,1)} %get-tuple-element.220.refs_4_.refs_0_, ...), custom_call_target="tpu_custom_call", output_to_operand_aliasing={{2}: (10, {}), {3}: (11, {})} | custom-call | flops 6000000000 | bytes 1000000 | tf_op jit(solution)/shard_map/input_bwd/pallas_call | solution.py:566
  143.4 1.5 collective-permute-start.29
  145.9 1.4 collective-permute-start.34
  147.3 2.0 collective-permute-done.31
  149.3 1.5 collective-permute-start.35
  150.9 7.4 %collective-permute-done.29 = bf16[1,1,1,96,768]{4,3,2,1,0:T(8,128)(2,1)S(1)} collective-permute-done((bf16[1,1,1,96,768]{4,3,2,1,0:T(8,128)(2,1)S(1)}, bf16[1,1,1,96,768]{4,3,2,1,0:T(8,128)(2,1)S(1)}, u32[]{:S(2)}, u32[]{:S(2)}) %collective-permute-start.29) | collective-permute-done | bytes 147488 | tf_op jit(solution)/shard_map/ppermute | solution.py:889
  158.5 1.6 select_convert_fusion.1
  161.1 1.6 collective-permute-done.35
  165.1 7.0 %collective-permute-done.36 = bf16[2,42,768]{2,1,0:T(8,128)(2,1)S(1)} collective-permute-done((bf16[2,42,768]{2,1,0:T(8,128)(2,1)S(1)}, bf16[2,42,768]{2,1,0:T(8,128)(2,1)S(1)}, u32[]{:S(2)}, u32[]{:S(2)}) %collective-permute-start.36) | collective-permute-done | bytes 129056 | tf_op jit(solution)/shard_map/ppermute | solution.py:889
  172.1 1.2 collective-permute-start.37
  174.9 7.2 %collective-permute-done.37 = bf16[4,42,768]{2,1,0:T(8,128)(2,1)S(1)} collective-permute-done((bf16[4,42,768]{2,1,0:T(8,128)(2,1)S(1)}, bf16[4,42,768]{2,1,0:T(8,128)(2,1)S(1)}, u32[]{:S(2)}, u32[]{:S(2)}) %collective-permute-start.37) | collective-permute-done | bytes 258080 | tf_op jit(solution)/shard_map/ppermute | solution.py:889
  183.9 2.2 %add_convert_fusion.1 = (bf16[4,192,256]{2,1,0:T(8,128)(2,1)}, bf16[4,192,256]{2,1,0:T(8,128)(2,1)}) fusion(bf16[8,192,256]{2,1,0:T(8,128)(2,1)} %collective-permute-done.33, bf16[8,192,256]{2,1,0:T(8,128)(2,1)S(1)} %get-tuple-element.367), kind=kLoop, calls=%fused_computation.11 | loop fusion | flops 1572864 | bytes 2359296 | tf_op jit(solution)/shard_map/convert_element_type | solution.py:877
  186.1 7.9 %collective-permute-done.41 = bf16[1,2,2,96,768]{4,3,2,1,0:T(8,128)(2,1)} collective-permute-done((bf16[1,2,2,96,768]{4,3,2,1,0:T(8,128)(2,1)S(1)}, bf16[1,2,2,96,768]{4,3,2,1,0:T(8,128)(2,1)}, u32[]{:S(2)}, u32[]{:S(2)}) %collective-permute-start.41) | collective-permute-done | bytes 589856 | tf_op jit(solution)/shard_map/ppermute | solution.py:889
  194.0 2.8 %select_convert_fusion = f32[2,2,2,96,768]{4,3,2,1,0:T(8,128)} fusion(pred[2]{0:T(512)(128)(4,1)S(1)} %iota_compare_fusion.2, bf16[2,2,96,768]{3,2,1,0:T(8,128)(2,1)} %bitcast.28, bf16[2,2,96,768]{3,2,1,0:T(8,128)(2,1)S(1)} %bitcast.61), kind=kLoop, calls=%fused_computation.8 | loop fusion | flops 1179648 | bytes 3538946 | tf_op jit(solution)/shard_map/convert_element_type | solution.py:954
  197.0 15.0 %condition_back.1 = (f32[256,768]{1,0:T(8,128)}, f32[768,768]{1,0:T(8,128)}, f32[768,4608]{1,0:T(8,128)}) custom-call(bf16[32,4608]{1,0:T(8,128)(2,1)} %copy-done, f32[32,256]{1,0:T(8,128)} %get-tuple-element.374.embedded, f32[32,768]{1,0:T(8,128)} %get-tuple-element.375.inner_pre, f32[32,768]{1,0:T(8,128)} %get-tuple-element.376.inner, ...), custom_call_target="tpu_custom_call" | custom-call | flops 1 | bytes 1 | tf_op jit(solution)/shard_map/condition_back/pallas_call | solution.py:772
  213.1 1.4 convert_bitcast_fusion
  (162 shorter events, 26.3 us)
Async XLA Ops:
  0.6 12.3 %collective-permute-start.1 = (bf16[4,192,256]{2,1,0:T(8,128)(2,1)}, bf16[4,192,256]{2,1,0:T(8,128)(2,1)S(1)}, u32[]{:S(2)}, u32[]{:S(2)}) collective-permute-start(bf16[4,192,256]{2,1,0:T(8,128)(2,1)} %bitcast.82), channel_id=1, source_target_pairs={{0,2},{2,0},{1,3},{3,1},{4,6},{6,4},{5,7},{7,5},{8,10},{10,8},{9,1... | collective-permute-start | bytes 1179656 | tf_op jit(solution)/shard_map/ppermute | solution.py:873
  3.6 11.1 %collective-permute-start = (bf16[4,192,256]{2,1,0:T(8,128)(2,1)}, bf16[4,192,256]{2,1,0:T(8,128)(2,1)S(1)}, u32[]{:S(2)}, u32[]{:S(2)}) collective-permute-start(bf16[4,192,256]{2,1,0:T(8,128)(2,1)} %bitcast.83), channel_id=1, source_target_pairs={{0,1},{1,0},{2,3},{3,2},{4,5},{5,4},{6,7},{7,6},{8,9},{9,8},{10,11... | collective-permute-start | bytes 1179656 | tf_op jit(solution)/shard_map/ppermute | solution.py:869
  3.7 9.4 %copy-start.12 = (bf16[4,256,192]{1,2,0:T(8,128)(2,1)S(1)}, bf16[4,256,192]{1,2,0:T(8,128)(2,1)}, u32[]{:S(2)}) copy-start(bf16[4,256,192]{1,2,0:T(8,128)(2,1)} %param.14) | copy-start | bytes 1179652
  13.0 1.8 collective-permute-start.2
  13.1 11.4 %collective-permute-start.3 = (bf16[4,192,256]{2,1,0:T(8,128)(2,1)S(1)}, bf16[4,192,256]{2,1,0:T(8,128)(2,1)S(1)}, u32[]{:S(2)}, u32[]{:S(2)}) collective-permute-start(bf16[4,192,256]{2,1,0:T(8,128)(2,1)S(1)} %bitcast.88), channel_id=1, source_target_pairs={{0,2},{2,0},{1,3},{3,1},{4,6},{6,4},{5,7},{7,5},{8,10},{10,8},{9,1... | collective-permute-start | bytes 1179656 | tf_op jit(solution)/shard_map/ppermute | solution.py:873
  23.7 2.0 collective-permute-start.4
  24.0 17.0 %collective-permute-start.9 = (bf16[4,192,256]{2,1,0:T(8,128)(2,1)S(1)}, bf16[4,192,256]{2,1,0:T(8,128)(2,1)S(1)}, u32[]{:S(2)}, u32[]{:S(2)}) collective-permute-start(bf16[4,192,256]{2,1,0:T(8,128)(2,1)S(1)} %bitcast.89), channel_id=1, source_target_pairs={{0,1},{1,0},{2,3},{3,2},{4,5},{5,4},{6,7},{7,6},{8,9},{9,8},{10,11... | collective-permute-start | bytes 1179656 | tf_op jit(solution)/shard_map/ppermute | solution.py:869
  24.5 12.0 %copy-start.14 = (bf16[4,192,256]{2,1,0:T(8,128)(2,1)}, bf16[4,192,256]{2,1,0:T(8,128)(2,1)S(1)}, u32[]{:S(2)}) copy-start(bf16[4,192,256]{2,1,0:T(8,128)(2,1)S(1)} %collective-permute-done.3.refs_2_) | copy-start | bytes 1179652
  24.5 16.5 %collective-permute-start.10 = (bf16[4,192,256]{2,1,0:T(8,128)(2,1)S(1)}, bf16[4,192,256]{2,1,0:T(8,128)(2,1)S(1)}, u32[]{:S(2)}, u32[]{:S(2)}) collective-permute-start(bf16[4,192,256]{2,1,0:T(8,128)(2,1)S(1)} %collective-permute-done.3.refs_2_), channel_id=1, source_target_pairs={{0,1},{1,0},{2,3},{3,2},{4,5},{5,4},{6,7},{7,6},{8,9},{9,8},{10,11... | collective-permute-start | bytes 1179656 | tf_op jit(solution)/shard_map/ppermute | solution.py:869
  26.8 11.2 %collective-permute-start.6 = (bf16[256,768]{1,0:T(8,128)(2,1)S(1)}, bf16[256,768]{1,0:T(8,128)(2,1)S(1)}, u32[]{:S(2)}, u32[]{:S(2)}) collective-permute-start(bf16[256,768]{1,0:T(8,128)(2,1)S(1)} %add_convert_fusion.10), channel_id=1, source_target_pairs={{0,2},{2,0},{1,3},{3,1},{4,6},{6,4},{5,7},{7,5},{8,10},{10,8},{9,1... | collective-permute-start | bytes 1179656 | tf_op jit(solution)/shard_map/ppermute | solution.py:873
  36.5 2.0 collective-permute-start.5
  38.2 2.8 %collective-permute-start.8 = (bf16[256,768]{1,0:T(8,128)(2,1)S(1)}, bf16[256,768]{1,0:T(8,128)(2,1)S(1)}, u32[]{:S(2)}, u32[]{:S(2)}) collective-permute-start(bf16[256,768]{1,0:T(8,128)(2,1)S(1)} %add_convert_fusion.9.refs_5_.refs_1_), channel_id=1, source_target_pairs={{0,1},{1,0},{2,3},{3,2},{4,5},{5,4},{6,7},{7,6},{8,9},{9,8},{10,11... | collective-permute-start | bytes 1179656 | tf_op jit(solution)/shard_map/ppermute | solution.py:869
  39.6 17.9 %collective-permute-start.7 = (bf16[256,768]{1,0:T(8,128)(2,1)S(1)}, bf16[256,768]{1,0:T(8,128)(2,1)S(1)}, u32[]{:S(2)}, u32[]{:S(2)}) collective-permute-start(bf16[256,768]{1,0:T(8,128)(2,1)S(1)} %add_convert_fusion.8), channel_id=1, source_target_pairs={{0,2},{2,0},{1,3},{3,1},{4,6},{6,4},{5,7},{7,5},{8,10},{10,8},{9,1... | collective-permute-start | bytes 1179656 | tf_op jit(solution)/shard_map/ppermute | solution.py:873
  57.2 2.0 collective-permute-start.12
  57.6 3.5 %collective-permute-start.11 = (bf16[256,768]{1,0:T(8,128)(2,1)S(1)}, bf16[256,768]{1,0:T(8,128)(2,1)S(1)}, u32[]{:S(2)}, u32[]{:S(2)}) collective-permute-start(bf16[256,768]{1,0:T(8,128)(2,1)S(1)} %add_convert_fusion.7.refs_5_.refs_1_), channel_id=1, source_target_pairs={{0,1},{1,0},{2,3},{3,2},{4,5},{5,4},{6,7},{7,6},{8,9},{9,8},{10,11... | collective-permute-start | bytes 1179656 | tf_op jit(solution)/shard_map/ppermute | solution.py:869
  60.4 16.4 %collective-permute-start.14 = (bf16[256,768]{1,0:T(8,128)(2,1)S(1)}, bf16[256,768]{1,0:T(8,128)(2,1)S(1)}, u32[]{:S(2)}, u32[]{:S(2)}) collective-permute-start(bf16[256,768]{1,0:T(8,128)(2,1)S(1)} %add_convert_fusion.6), channel_id=1, source_target_pairs={{0,2},{2,0},{1,3},{3,1},{4,6},{6,4},{5,7},{7,5},{8,10},{10,8},{9,1... | collective-permute-start | bytes 1179656 | tf_op jit(solution)/shard_map/ppermute | solution.py:873
  61.8 15.6 %copy-start.5 = (bf16[512,768]{1,0:T(8,128)(2,1)S(1)}, bf16[512,768]{1,0:T(8,128)(2,1)}, u32[]{:S(2)}) copy-start(bf16[512,768]{1,0:T(8,128)(2,1)} %get-tuple-element.261) | copy-start | bytes 2359300
  76.7 5.0 %collective-permute-start.13 = (bf16[256,768]{1,0:T(8,128)(2,1)}, bf16[256,768]{1,0:T(8,128)(2,1)S(1)}, u32[]{:S(2)}, u32[]{:S(2)}) collective-permute-start(bf16[256,768]{1,0:T(8,128)(2,1)} %get-tuple-element.252), channel_id=1, source_target_pairs={{0,1},{1,0},{2,3},{3,2},{4,5},{5,4},{6,7},{7,6},{8,9},{9,8},{10,11... | collective-permute-start | bytes 1179656 | tf_op jit(solution)/shard_map/ppermute | solution.py:869
  76.9 7.9 %collective-permute-start.16 = (bf16[256,768]{1,0:T(8,128)(2,1)S(1)}, bf16[256,768]{1,0:T(8,128)(2,1)S(1)}, u32[]{:S(2)}, u32[]{:S(2)}) collective-permute-start(bf16[256,768]{1,0:T(8,128)(2,1)S(1)} %add_convert_fusion.5.refs_3_), channel_id=1, source_target_pairs={{0,1},{1,0},{2,3},{3,2},{4,5},{5,4},{6,7},{7,6},{8,9},{9,8},{10,11... | collective-permute-start | bytes 1179656 | tf_op jit(solution)/shard_map/ppermute | solution.py:869
  80.1 15.6 %collective-permute-start.18 = (bf16[384,768]{1,0:T(8,128)(2,1)S(1)}, bf16[384,768]{1,0:T(8,128)(2,1)}, u32[]{:S(2)}, u32[]{:S(2)}) collective-permute-start(bf16[384,768]{1,0:T(8,128)(2,1)S(1)} %constant_dynamic-slice_fusion.2), channel_id=1, source_target_pairs={{0,4},{4,0},{8,12},{12,8},{16,20},{20,16},{24,28},{28,24},{1,5},{5... | collective-permute-start | bytes 1769480 | tf_op jit(solution)/shard_map/ppermute | solution.py:889
  81.8 11.6 %collective-permute-start.15 = (bf16[256,768]{1,0:T(8,128)(2,1)S(1)}, bf16[256,768]{1,0:T(8,128)(2,1)}, u32[]{:S(2)}, u32[]{:S(2)}) collective-permute-start(bf16[256,768]{1,0:T(8,128)(2,1)S(1)} %add_convert_fusion.4), channel_id=1, source_target_pairs={{0,2},{2,0},{1,3},{3,1},{4,6},{6,4},{5,7},{7,5},{8,10},{10,8},{9,1... | collective-permute-start | bytes 1179656 | tf_op jit(solution)/shard_map/ppermute | solution.py:873
  95.3 3.4 %collective-permute-start.17 = (bf16[256,768]{1,0:T(8,128)(2,1)}, bf16[256,768]{1,0:T(8,128)(2,1)}, u32[]{:S(2)}, u32[]{:S(2)}) collective-permute-start(bf16[256,768]{1,0:T(8,128)(2,1)} %add_convert_fusion.3.refs_3_), channel_id=1, source_target_pairs={{0,1},{1,0},{2,3},{3,2},{4,5},{5,4},{6,7},{7,6},{8,9},{9,8},{10,11... | collective-permute-start | bytes 1179656 | tf_op jit(solution)/shard_map/ppermute | solution.py:869
  95.3 19.1 %collective-permute-start.22 = (bf16[384,768]{1,0:T(8,128)(2,1)S(1)}, bf16[384,768]{1,0:T(8,128)(2,1)}, u32[]{:S(2)}, u32[]{:S(2)}) collective-permute-start(bf16[384,768]{1,0:T(8,128)(2,1)S(1)} %constant_dynamic-slice_fusion.1), channel_id=1, source_target_pairs={{0,4},{4,0},{8,12},{12,8},{16,20},{20,16},{24,28},{28,24},{1,5},{5... | collective-permute-start | bytes 1769480 | tf_op jit(solution)/shard_map/ppermute | solution.py:889
  97.0 9.7 %collective-permute-start.19 = (bf16[192,768]{1,0:T(8,128)(2,1)S(1)}, bf16[192,768]{1,0:T(8,128)(2,1)S(1)}, u32[]{:S(2)}, u32[]{:S(2)}) collective-permute-start(bf16[192,768]{1,0:T(8,128)(2,1)S(1)} %get-tuple-element.389), channel_id=1, source_target_pairs={{0,8},{4,12},{8,0},{12,4},{16,24},{20,28},{24,16},{28,20},{1,9},{5... | collective-permute-start | bytes 884744 | tf_op jit(solution)/shard_map/ppermute | solution.py:889
  98.7 10.9 %copy-start.22 = (bf16[1024,192]{1,0:T(8,128)(2,1)S(1)}, bf16[1024,192]{1,0:T(8,128)(2,1)}, u32[]{:S(2)}) copy-start(bf16[1024,192]{1,0:T(8,128)(2,1)} %get-tuple-element.305) | copy-start | bytes 1179652
  106.9 10.5 %collective-permute-start.21 = (bf16[96,768]{1,0:T(8,128)(2,1)S(1)}, bf16[96,768]{1,0:T(8,128)(2,1)S(1)}, u32[]{:S(2)}, u32[]{:S(2)}) collective-permute-start(bf16[96,768]{1,0:T(8,128)(2,1)S(1)} %get-tuple-element.399), channel_id=1, source_target_pairs={{0,16},{4,20},{8,24},{12,28},{16,0},{20,4},{24,8},{28,12},{1,17},{... | collective-permute-start | bytes 442376 | tf_op jit(solution)/shard_map/ppermute | solution.py:889
  112.8 17.8 %collective-permute-start.20 = (bf16[384,768]{1,0:T(8,128)(2,1)S(1)}, bf16[384,768]{1,0:T(8,128)(2,1)}, u32[]{:S(2)}, u32[]{:S(2)}) collective-permute-start(bf16[384,768]{1,0:T(8,128)(2,1)S(1)} %constant_dynamic-slice_fusion), channel_id=1, source_target_pairs={{0,4},{4,0},{8,12},{12,8},{16,20},{20,16},{24,28},{28,24},{1,5},{5... | collective-permute-start | bytes 1769480 | tf_op jit(solution)/shard_map/ppermute | solution.py:889
  116.4 11.7 %collective-permute-start.24 = (bf16[192,768]{1,0:T(8,128)(2,1)}, bf16[192,768]{1,0:T(8,128)(2,1)S(1)}, u32[]{:S(2)}, u32[]{:S(2)}) collective-permute-start(bf16[192,768]{1,0:T(8,128)(2,1)} %get-tuple-element.387), channel_id=1, source_target_pairs={{0,8},{4,12},{8,0},{12,4},{16,24},{20,28},{24,16},{28,20},{1,9},{5... | collective-permute-start | bytes 884744 | tf_op jit(solution)/shard_map/ppermute | solution.py:889
  117.4 8.9 %collective-permute-start.23 = (bf16[1,1,1,96,768]{4,3,2,1,0:T(8,128)(2,1)S(1)}, bf16[1,1,1,96,768]{4,3,2,1,0:T(8,128)(2,1)S(1)}, u32[]{:S(2)}, u32[]{:S(2)}) collective-permute-start(bf16[1,1,1,96,768]{4,3,2,1,0:T(8,128)(2,1)S(1)} %bitcast.68), channel_id=1, source_target_pairs={{0,16},{4,20},{8,24},{12,28},{16,0},{20,4},{24,8},{28,12},{1,17},{... | collective-permute-start | bytes 442376 | tf_op jit(solution)/shard_map/ppermute | solution.py:889
  128.1 14.6 %collective-permute-start.26 = (bf16[1,1,2,96,768]{4,3,2,1,0:T(8,128)(2,1)S(1)}, bf16[1,1,2,96,768]{4,3,2,1,0:T(8,128)(2,1)S(1)}, u32[]{:S(2)}, u32[]{:S(2)}) collective-permute-start(bf16[1,1,2,96,768]{4,3,2,1,0:T(8,128)(2,1)S(1)} %broadcast_select_fusion.6), channel_id=1, source_target_pairs={{0,8},{4,12},{8,0},{12,4},{16,24},{20,28},{24,16},{28,20},{1,9},{5... | collective-permute-start | bytes 884744 | tf_op jit(solution)/shard_map/ppermute | solution.py:889
  129.4 14.0 %collective-permute-start.28 = (bf16[96,768]{1,0:T(8,128)(2,1)}, bf16[96,768]{1,0:T(8,128)(2,1)S(1)}, u32[]{:S(2)}, u32[]{:S(2)}) collective-permute-start(bf16[96,768]{1,0:T(8,128)(2,1)} %get-tuple-element.397), channel_id=1, source_target_pairs={{0,16},{4,20},{8,24},{12,28},{16,0},{20,4},{24,8},{28,12},{1,17},{... | collective-permute-start | bytes 442376 | tf_op jit(solution)/shard_map/ppermute | solution.py:889
  131.8 14.0 %collective-permute-start.32 = (bf16[192,768]{1,0:T(8,128)(2,1)S(1)}, bf16[192,768]{1,0:T(8,128)(2,1)S(1)}, u32[]{:S(2)}, u32[]{:S(2)}) collective-permute-start(bf16[192,768]{1,0:T(8,128)(2,1)S(1)} %get-tuple-element.385), channel_id=1, source_target_pairs={{0,8},{4,12},{8,0},{12,4},{16,24},{20,28},{24,16},{28,20},{1,9},{5... | collective-permute-start | bytes 884744 | tf_op jit(solution)/shard_map/ppermute | solution.py:889
  142.1 2.9 %collective-permute-start.30 = (bf16[40,768]{1,0:T(8,128)(2,1)}, bf16[40,768]{1,0:T(8,128)(2,1)S(1)}, u32[]{:S(2)}, u32[]{:S(2)}) collective-permute-start(bf16[40,768]{1,0:T(8,128)(2,1)} %get-tuple-element.341), channel_id=1, source_target_pairs={{0,1},{1,0},{2,3},{3,2},{4,5},{5,4},{6,7},{7,6},{8,9},{9,8},{10,11... | collective-permute-start | bytes 184328 | tf_op jit(solution)/shard_map/ppermute | solution.py:869
  142.2 17.9 %collective-permute-start.25 = (bf16[2,8,192,256]{3,2,1,0:T(8,128)(2,1)}, bf16[2,8,192,256]{3,2,1,0:T(8,128)(2,1)S(1)}, u32[]{:S(2)}, u32[]{:S(2)}) collective-permute-start(bf16[2,8,192,256]{3,2,1,0:T(8,128)(2,1)} %get-tuple-element.333), channel_id=1, source_target_pairs={{0,1},{1,0},{2,3},{3,2},{4,5},{5,4},{6,7},{7,6},{8,9},{9,8},{10,11... | collective-permute-start | bytes 4718600 | tf_op jit(solution)/shard_map/ppermute | solution.py:869
  142.8 15.6 %collective-permute-start.27 = (bf16[1,2,2,96,768]{4,3,2,1,0:T(8,128)(2,1)S(1)}, bf16[1,2,2,96,768]{4,3,2,1,0:T(8,128)(2,1)S(1)}, u32[]{:S(2)}, u32[]{:S(2)}) collective-permute-start(bf16[1,2,2,96,768]{4,3,2,1,0:T(8,128)(2,1)S(1)} %broadcast_select_fusion.3), channel_id=1, source_target_pairs={{0,4},{4,0},{8,12},{12,8},{16,20},{20,16},{24,28},{28,24},{1,5},{5... | collective-permute-start | bytes 1769480 | tf_op jit(solution)/shard_map/ppermute | solution.py:889
  143.4 14.8 %collective-permute-start.29 = (bf16[1,1,1,96,768]{4,3,2,1,0:T(8,128)(2,1)S(1)}, bf16[1,1,1,96,768]{4,3,2,1,0:T(8,128)(2,1)S(1)}, u32[]{:S(2)}, u32[]{:S(2)}) collective-permute-start(bf16[1,1,1,96,768]{4,3,2,1,0:T(8,128)(2,1)S(1)} %bitcast.66), channel_id=1, source_target_pairs={{0,16},{4,20},{8,24},{12,28},{16,0},{20,4},{24,8},{28,12},{1,17},{... | collective-permute-start | bytes 442376 | tf_op jit(solution)/shard_map/ppermute | solution.py:889
  145.0 4.3 %collective-permute-start.31 = (bf16[40,768]{1,0:T(8,128)(2,1)S(1)}, bf16[40,768]{1,0:T(8,128)(2,1)S(1)}, u32[]{:S(2)}, u32[]{:S(2)}) collective-permute-start(bf16[40,768]{1,0:T(8,128)(2,1)S(1)} %add_convert_fusion.27), channel_id=1, source_target_pairs={{0,2},{2,0},{1,3},{3,1},{4,6},{6,4},{5,7},{7,5},{8,10},{10,8},{9,1... | collective-permute-start | bytes 184328 | tf_op jit(solution)/shard_map/ppermute | solution.py:873
  145.9 16.8 %collective-permute-start.34 = (bf16[96,768]{1,0:T(8,128)(2,1)S(1)}, bf16[96,768]{1,0:T(8,128)(2,1)S(1)}, u32[]{:S(2)}, u32[]{:S(2)}) collective-permute-start(bf16[96,768]{1,0:T(8,128)(2,1)S(1)} %get-tuple-element.395), channel_id=1, source_target_pairs={{0,16},{4,20},{8,24},{12,28},{16,0},{20,4},{24,8},{28,12},{1,17},{... | collective-permute-start | bytes 442376 | tf_op jit(solution)/shard_map/ppermute | solution.py:889
  149.3 13.4 %collective-permute-start.35 = (bf16[1,42,768]{2,1,0:T(8,128)(2,1)S(1)}, bf16[1,42,768]{2,1,0:T(8,128)(2,1)S(1)}, u32[]{:S(2)}, u32[]{:S(2)}) collective-permute-start(bf16[1,42,768]{2,1,0:T(8,128)(2,1)S(1)} %maximum_bitcast_fusion), channel_id=1, source_target_pairs={{0,16},{4,20},{8,24},{12,28},{16,0},{20,4},{24,8},{28,12},{1,17},{... | collective-permute-start | bytes 193544 | tf_op jit(solution)/shard_map/ppermute | solution.py:889
  158.4 14.9 %collective-permute-start.39 = (bf16[1,1,2,96,768]{4,3,2,1,0:T(8,128)(2,1)S(1)}, bf16[1,1,2,96,768]{4,3,2,1,0:T(8,128)(2,1)S(1)}, u32[]{:S(2)}, u32[]{:S(2)}) collective-permute-start(bf16[1,1,2,96,768]{4,3,2,1,0:T(8,128)(2,1)S(1)} %broadcast_select_fusion.5), channel_id=1, source_target_pairs={{0,8},{4,12},{8,0},{12,4},{16,24},{20,28},{24,16},{28,20},{1,9},{5... | collective-permute-start | bytes 884744 | tf_op jit(solution)/shard_map/ppermute | solution.py:889
  162.7 9.3 %collective-permute-start.36 = (bf16[2,42,768]{2,1,0:T(8,128)(2,1)S(1)}, bf16[2,42,768]{2,1,0:T(8,128)(2,1)S(1)}, u32[]{:S(2)}, u32[]{:S(2)}) collective-permute-start(bf16[2,42,768]{2,1,0:T(8,128)(2,1)S(1)} %constant_dynamic-update-slice_fusion), channel_id=1, source_target_pairs={{0,8},{4,12},{8,0},{12,4},{16,24},{20,28},{24,16},{28,20},{1,9},{5... | collective-permute-start | bytes 387080 | tf_op jit(solution)/shard_map/ppermute | solution.py:889
  163.3 11.1 %collective-permute-start.38 = (bf16[1,1,1,96,768]{4,3,2,1,0:T(8,128)(2,1)S(1)}, bf16[1,1,1,96,768]{4,3,2,1,0:T(8,128)(2,1)S(1)}, u32[]{:S(2)}, u32[]{:S(2)}) collective-permute-start(bf16[1,1,1,96,768]{4,3,2,1,0:T(8,128)(2,1)S(1)} %bitcast.67), channel_id=1, source_target_pairs={{0,4},{4,0},{8,12},{12,8},{16,20},{20,16},{24,28},{28,24},{1,5},{5... | collective-permute-start | bytes 442376 | tf_op jit(solution)/shard_map/ppermute | solution.py:889
  164.1 19.7 %collective-permute-start.33 = (bf16[8,192,256]{2,1,0:T(8,128)(2,1)S(1)}, bf16[8,192,256]{2,1,0:T(8,128)(2,1)}, u32[]{:S(2)}, u32[]{:S(2)}) collective-permute-start(bf16[8,192,256]{2,1,0:T(8,128)(2,1)S(1)} %get-tuple-element.392), channel_id=1, source_target_pairs={{0,2},{2,0},{1,3},{3,1},{4,6},{6,4},{5,7},{7,5},{8,10},{10,8},{9,1... | collective-permute-start | bytes 2359304 | tf_op jit(solution)/shard_map/ppermute | solution.py:873
  172.1 9.9 %collective-permute-start.37 = (bf16[4,42,768]{2,1,0:T(8,128)(2,1)S(1)}, bf16[4,42,768]{2,1,0:T(8,128)(2,1)S(1)}, u32[]{:S(2)}, u32[]{:S(2)}) collective-permute-start(bf16[4,42,768]{2,1,0:T(8,128)(2,1)S(1)} %constant_dynamic-update-slice_fusion.2), channel_id=1, source_target_pairs={{0,4},{4,0},{8,12},{12,8},{16,20},{20,16},{24,28},{28,24},{1,5},{5... | collective-permute-start | bytes 774152 | tf_op jit(solution)/shard_map/ppermute | solution.py:889
  173.4 20.5 %collective-permute-start.41 = (bf16[1,2,2,96,768]{4,3,2,1,0:T(8,128)(2,1)S(1)}, bf16[1,2,2,96,768]{4,3,2,1,0:T(8,128)(2,1)}, u32[]{:S(2)}, u32[]{:S(2)}) collective-permute-start(bf16[1,2,2,96,768]{4,3,2,1,0:T(8,128)(2,1)S(1)} %broadcast_select_fusion.2), channel_id=1, source_target_pairs={{0,4},{4,0},{8,12},{12,8},{16,20},{20,16},{24,28},{28,24},{1,5},{5... | collective-permute-start | bytes 1769480 | tf_op jit(solution)/shard_map/ppermute | solution.py:889
  174.5 22.2 %collective-permute-start.40 = (bf16[2,1,1,96,768]{4,3,0,2,1:T(8,128)(2,1)S(1)}, bf16[2,1,1,96,768]{4,3,0,2,1:T(8,128)(2,1)S(1)}, u32[]{:S(2)}, u32[]{:S(2)}) collective-permute-start(bf16[2,1,1,96,768]{4,3,0,2,1:T(8,128)(2,1)S(1)} %broadcast_select_fusion.4), channel_id=1, source_target_pairs={{0,16},{4,20},{8,24},{12,28},{16,0},{20,4},{24,8},{28,12},{1,17},{... | collective-permute-start | bytes 884744 | tf_op jit(solution)/shard_map/ppermute | solution.py:889
  182.5 14.3 %copy-start = (bf16[32,4608]{1,0:T(8,128)(2,1)}, bf16[32,4608]{1,0:T(8,128)(2,1)S(1)}, u32[]{:S(2)}) copy-start(bf16[32,4608]{1,0:T(8,128)(2,1)S(1)} %reshape.116.gmod) | copy-start | bytes 884740
  196.9 15.1 %collective-permute-start.42 = (bf16[2,1,2,96,768]{4,3,2,0,1:T(8,128)(2,1)S(1)}, bf16[2,1,2,96,768]{4,3,2,0,1:T(8,128)(2,1)S(1)}, u32[]{:S(2)}, u32[]{:S(2)}) collective-permute-start(bf16[2,1,2,96,768]{4,3,2,0,1:T(8,128)(2,1)S(1)} %broadcast_select_fusion.1), channel_id=1, source_target_pairs={{0,8},{4,12},{8,0},{12,4},{16,24},{20,28},{24,16},{28,20},{1,9},{5... | collective-permute-start | bytes 1769480 | tf_op jit(solution)/shard_map/ppermute | solution.py:889
  (22 other events, 50.5 us)

commit v4 on v3

--- a/solution.py
+++ b/solution.py
@@ -19,13 +19,14 @@
 LANES = 128
 ROWS = 128
 FEW_ROWS = 128
+MANY_ROWS = 256
 BAND = 64
 GELU_A = math.sqrt(2.0 / math.pi)
 GELU_B = 0.044715
 EPS = 1e-06
 VMEM_LIMIT = 60 * 1024 * 1024
 WEIGHT_ROWS = 256
-BACK_ROWS = 64
+BACK_ROWS = 128
 PACKED = 40
 
 
@@ -218,11 +219,11 @@
 
     def rows(rel, at):
         lat = jnp.bitwise_xor(rel, core)
-        normed, _ = norm_stats(full_out[pl.ds(at, ROWS), :].astype(F32))
-        here = pl.ds(pl.multiple_of(at + (2 * rel + 1) * SIDE, SIDE), ROWS)
+        normed, _ = norm_stats(full_out[pl.ds(at, MANY_ROWS), :].astype(F32))
+        here = pl.ds(pl.multiple_of(at + (2 * rel + 1) * SIDE, SIDE), MANY_ROWS)
         padded[here, :] = normed * (1.0 + mod[lat, 1:2, :]) + mod[lat, 0:1, :]
 
-    row_loop(tokens, rows)
+    row_loop(tokens, rows, MANY_ROWS)
 
     def lanes(rel, at):
         taps = taps_of(kern, at)
@@ -1136,12 +1137,12 @@
         lambda a, b: (sum_pair(a[:per_dev], b[:per_dev]), sum_pair(a[per_dev:], b[per_dev:])), made[0], x_swap(made[1])
     )
     order.last = (final_out, final_grad)
-    up_grad = up_sum.finish(order, F32)
     while not attn_sum.done():
         order.advance(attn_sum)
     time_in_grad, time_out_grad, ada_weight_grad = order(
         lambda g: condition_back(g, embedded, stages, time_out, ada_weight, factor), gmod
     )
+    up_grad = up_sum.finish(order, F32)
     attn_grads = attn_sum.finish(order, BF)
     qkv_rows_grad, out_grad = attn_grads[: 3 * share].astype(F32), attn_grads[3 * share :].astype(F32)
     qkv_grad = jnp.swapaxes(qkv_rows_grad.reshape(3, share, width), 1, 2)

time: 215 us -> 210 us (0.977)
  waiting for transfers between devices: 39.7 us -> 35.8 us
    ppermute x21, waiting for transfers between devices: 32.9 us -> 28.8 us  [wide_swap(): return lax.ppermute(v, 'wide', [(i, i ^ bit) for i in range(count)])]
  transfers between devices with their start and end apart: 43 -> 43, of which waited for: 13 -> 12; matrix products, arithmetic and copies ran while one was open for 13% -> 13% of each run, Pallas kernels for 47% -> 48%
where the time goes in v4:
time: 210 us; the launch traced here: 209 us
  Pallas kernels  100 us (48%)
  starting transfers between devices  36.7 us (17%)
  waiting for transfers between devices  35.8 us (17%)
  other arithmetic  22.2 us (11%)
  local copies, waits for them, and re-layouts  6.84 us (3%)
  matrix products  6.18 us (3%)
    pallas_call x8, Pallas kernels, call(): pl.pallas_call(run, name=name, out_shape=[jax.ShapeDtypeStruct(o[0], o[1]...  77.2 us
    ppermute x21, waiting for transfers between devices, wide_swap(): return lax.ppermute(v, 'wide', [(i, i ^ bit) for i in range(count)])  28.8 us
    ppermute x21, starting transfers between devices, wide_swap(): return lax.ppermute(v, 'wide', [(i, i ^ bit) for i in range(count)])  22.3 us
    pallas_call x1, Pallas kernels, condition_back(): pl.pallas_call(functools.partial(condition_back_body, factor), name='cond...  14.5 us
    convert_element_type x21, other arithmetic, sum_pair(): return (a.astype(F32) + b.astype(F32)).astype(BF)  13.9 us
    ppermute x8, starting transfers between devices, x_swap(): return lax.ppermute(v, 'narrow', [(0, 2), (2, 0), (1, 3), (3, 1)])  11.7 us
    pallas_call x1, Pallas kernels, condition(): pl.pallas_call(functools.partial(condition_body, steps), name='condition'...  8.82 us
    dot_general x5, matrix products, dot_tn(): lax.dot_general(a, b, (((0,), (0,)), ((), ())), preferred_element_type=F32)  6.18 us
  transfers between devices with their start and end apart: 43, of which 12 were waited for; matrix products, arithmetic and copies ran while one was open for 13% of the time, Pallas kernels for 48%

profile of v4, /device:TPU:0, one launch (start us, length us, event | category | flops | bytes accessed | tf_op | source)
XLA Modules:
  0.0 209.5 jit_solution(6784134430323028273)
XLA Ops:
  0.6 3.0 %collective-permute-start.1 = (bf16[4,192,256]{2,1,0:T(8,128)(2,1)}, bf16[4,192,256]{2,1,0:T(8,128)(2,1)S(1)}, u32[]{:S(2)}, u32[]{:S(2)}) collective-permute-start(bf16[4,192,256]{2,1,0:T(8,128)(2,1)} %bitcast.82), channel_id=1, source_target_pairs={{0,2},{2,0},{1,3},{3,1},{4,6},{6,4},{5,7},{7,5},{8,10},{10,8},{9,1... | collective-permute-start | bytes 1179656 | tf_op jit(solution)/shard_map/ppermute | solution.py:874
  3.7 8.8 %condition.1 = (f32[4,6,768]{2,1,0:T(8,128)}, f32[32,256]{1,0:T(8,128)}, f32[32,768]{1,0:T(8,128)}, f32[32,768]{1,0:T(8,128)}, f32[32,768]{1,0:T(8,128)}, /*index=5*/f32[32,768]{1,0:T(8,128)}) custom-call(s32[32]{0:T(128)} %stamps.1, s32[1]{0:T(128)} %bitcast.2.wide, f32[36,128]{1,0:T(8,128)} %bitcast.90, f32[256,768]{1,0:T(8,128)} %time_in.1, ...), custom_call_target="tpu_custom_call" | custom-call | flops 8000000000 | bytes 1000000 | tf_op jit(solution)/shard_map/condition/pallas_call | solution.py:704
  13.1 1.7 collective-permute-start.3
  15.7 7.7 %attn_fwd.2 = (bf16[512,768]{1,0:T(8,128)(2,1)}, bf16[512,192]{1,0:T(8,128)(2,1)}, bf16[512,192]{1,0:T(8,128)(2,1)}, bf16[512,192]{1,0:T(8,128)(2,1)}, bf16[256,...) custom-call(s32[1]{0:T(128)} %bitcast.s_ref, ...), custom_call_target="tpu_custom_call" | custom-call | flops 6000000000 | bytes 1000000 | tf_op jit(solution)/shard_map/attn_fwd/pallas_call | solution.py:567
  25.4 1.1 add_convert_fusion.10
  26.5 1.6 collective-permute-start.6
  28.1 7.7 %attn_fwd.3 = (bf16[512,768]{1,0:T(8,128)(2,1)}, bf16[512,192]{1,0:T(8,128)(2,1)}, bf16[512,192]{1,0:T(8,128)(2,1)}, bf16[512,192]{1,0:T(8,128)(2,1)}, bf16[256,...) custom-call(s32[1]{0:T(128)} %bitcast.s_ref, ...), custom_call_target="tpu_custom_call", output_to_operand_aliasing={{6}: (9, {}), {7}: (10, {})} | custom-call | flops 6000000000 | bytes 1000000 | tf_op jit(solution)/shard_map/attn_fwd/pallas_call | solution.py:567
  35.9 1.8 collective-permute-done.6
  38.0 1.1 add_convert_fusion.8
  39.1 1.6 collective-permute-start.7
  42.4 14.5 %ffn.2 = (bf16[512,768]{1,0:T(8,128)(2,1)}, bf16[256,768]{1,0:T(8,128)(2,1)}, bf16[256,768]{1,0:T(8,128)(2,1)}, f32[2,1,768]{2,1,0:T(1,128)}, f32[16,768]{1,0:T(...) custom-call(s32[1]{0:T(128)} %bitcast.s_ref, ...), custom_call_target="tpu_custom_call" | custom-call | flops 10000000000 | bytes 1000000 | tf_op jit(solution)/shard_map/ffn/pallas_call | solution.py:567
  57.7 1.2 collective-permute-done.12
  58.9 1.1 add_convert_fusion.6
  61.4 14.8 %ffn.3 = (bf16[512,768]{1,0:T(8,128)(2,1)}, bf16[256,768]{1,0:T(8,128)(2,1)}, bf16[256,768]{1,0:T(8,128)(2,1)}, f32[2,1,768]{2,1,0:T(1,128)}, f32[16,768]{1,0:T(...) custom-call(s32[1]{0:T(128)} %bitcast.s_ref, ...), custom_call_target="tpu_custom_call", output_to_operand_aliasing={{7}: (13, {}), {8}: (14, {}), {9}: (15, {}), {10}: (16, {})} | custom-call | flops 10000000000 | bytes 1000000 | tf_op jit(solution)/shard_map/ffn/pallas_call | solution.py:567
  79.6 1.6 collective-permute-start.18
  81.4 1.6 collective-permute-start.15
  82.9 1.5 multiply_convert_fusion
  85.3 7.8 %attn_bwd.2 = (bf16[512,768]{1,0:T(8,128)(2,1)}, f32[2,8,768]{2,1,0:T(8,128)}, bf16[1024,768]{1,0:T(8,128)(2,1)}, bf16[1024,576]{1,0:T(8,128)(2,1)}) custom-call(s32[1]{0:T(128)} %bitcast.s_ref, bf16[512,768]{1,0:T(8,128)(2,1)} %get-tuple-element.211.refs_4_.refs_0_, bf16[256,768]{1,0:T(8,128)(2,1)} %copy-done.7, bf16[256,768]{1,0:T(8,128)(2,1)} %copy-done.15, ...), custom_call_target="tpu_custom_call" | custom-call | flops 6000000000 | bytes 1000000 | tf_op jit(solution)/shard_map/attn_bwd/pallas_call | solution.py:567
  93.1 1.9 add_convert_fusion.3.refs_3_
  95.4 1.3 add_convert_fusion.15
  96.7 1.6 collective-permute-start.19
  98.4 8.1 %attn_bwd.3 = (bf16[512,768]{1,0:T(8,128)(2,1)}, f32[2,8,768]{2,1,0:T(8,128)}, bf16[1024,768]{1,0:T(8,128)(2,1)}, bf16[1024,576]{1,0:T(8,128)(2,1)}) custom-call(s32[1]{0:T(128)} %bitcast.s_ref, bf16[512,768]{1,0:T(8,128)(2,1)} %get-tuple-element.220.refs_4_.refs_0_, bf16[256,768]{1,0:T(8,128)(2,1)} %copy-done.6, ...), custom_call_target="tpu_custom_call", output_to_operand_aliasing={{2}: (13, {}), {3}: (14, {})} | custom-call | flops 6000000000 | bytes 1000000 | tf_op jit(solution)/shard_map/attn_bwd/pallas_call | solution.py:567
  106.6 2.7 %collective-permute-start.21 = (bf16[96,768]{1,0:T(8,128)(2,1)S(1)}, bf16[96,768]{1,0:T(8,128)(2,1)S(1)}, u32[]{:S(2)}, u32[]{:S(2)}) collective-permute-start(bf16[96,768]{1,0:T(8,128)(2,1)S(1)} %get-tuple-element.399), channel_id=1, source_target_pairs={{0,16},{4,20},{8,24},{12,28},{16,0},{20,4},{24,8},{28,12},{1,17},{... | collective-permute-start | bytes 442376 | tf_op jit(solution)/shard_map/ppermute | solution.py:890
  109.2 1.9 fusion
  111.2 1.1 multiply_convert_fusion.2
  112.5 1.6 collective-permute-start.20
  114.1 2.0 add_convert_fusion.13
  117.7 8.2 %input_bwd.2 = (f32[16,768]{1,0:T(8,128)}, f32[2,8,768]{2,1,0:T(8,128)}, bf16[2,8,192,256]{3,2,1,0:T(8,128)(2,1)}, bf16[2,8,192,256]{3,2,1,0:T(8,128)(2,1)}) custom-call(s32[1]{0:T(128)} %bitcast.s_ref, bf16[512,768]{1,0:T(8,128)(2,1)} %get-tuple-element.211.refs_4_.refs_0_, ...), custom_call_target="tpu_custom_call", output_to_operand_aliasing={{2}: (10, {}), {3}: (11, {})} | custom-call | flops 6000000000 | bytes 1000000 | tf_op jit(solution)/shard_map/input_bwd/pallas_call | solution.py:567
  126.0 1.7 collective-permute-done.24
  129.1 1.1 collective-permute-start.28
  130.2 1.3 add_convert_fusion.11
  131.5 1.9 collective-permute-start.32
  133.4 8.3 %input_bwd.3 = (f32[16,768]{1,0:T(8,128)}, bf16[40,768]{1,0:T(8,128)(2,1)}, bf16[2,8,192,256]{3,2,1,0:T(8,128)(2,1)}, bf16[2,8,192,256]{3,2,1,0:T(8,128)(2,1)}) custom-call(s32[1]{0:T(128)} %bitcast.s_ref, bf16[512,768]{1,0:T(8,128)(2,1)} %get-tuple-element.220.refs_4_.refs_0_, ...), custom_call_target="tpu_custom_call", output_to_operand_aliasing={{2}: (10, {}), {3}: (11, {})} | custom-call | flops 6000000000 | bytes 1000000 | tf_op jit(solution)/shard_map/input_bwd/pallas_call | solution.py:567
  143.1 1.5 collective-permute-start.29
  145.5 1.4 collective-permute-start.34
  147.0 2.0 collective-permute-done.31
  149.0 1.5 collective-permute-start.35
  150.6 7.4 %collective-permute-done.29 = bf16[1,1,1,96,768]{4,3,2,1,0:T(8,128)(2,1)S(1)} collective-permute-done((bf16[1,1,1,96,768]{4,3,2,1,0:T(8,128)(2,1)S(1)}, bf16[1,1,1,96,768]{4,3,2,1,0:T(8,128)(2,1)S(1)}, u32[]{:S(2)}, u32[]{:S(2)}) %collective-permute-start.29) | collective-permute-done | bytes 147488 | tf_op jit(solution)/shard_map/ppermute | solution.py:890
  158.2 1.6 select_convert_fusion.1
  160.7 1.6 collective-permute-done.35
  164.7 7.0 %collective-permute-done.36 = bf16[2,42,768]{2,1,0:T(8,128)(2,1)S(1)} collective-permute-done((bf16[2,42,768]{2,1,0:T(8,128)(2,1)S(1)}, bf16[2,42,768]{2,1,0:T(8,128)(2,1)S(1)}, u32[]{:S(2)}, u32[]{:S(2)}) %collective-permute-start.36) | collective-permute-done | bytes 129056 | tf_op jit(solution)/shard_map/ppermute | solution.py:890
  171.8 1.2 collective-permute-start.37
  174.5 7.2 %collective-permute-done.37 = bf16[4,42,768]{2,1,0:T(8,128)(2,1)S(1)} collective-permute-done((bf16[4,42,768]{2,1,0:T(8,128)(2,1)S(1)}, bf16[4,42,768]{2,1,0:T(8,128)(2,1)S(1)}, u32[]{:S(2)}, u32[]{:S(2)}) %collective-permute-start.37) | collective-permute-done | bytes 258080 | tf_op jit(solution)/shard_map/ppermute | solution.py:890
  183.6 2.2 %add_convert_fusion.1 = (bf16[4,192,256]{2,1,0:T(8,128)(2,1)}, bf16[4,192,256]{2,1,0:T(8,128)(2,1)}) fusion(bf16[8,192,256]{2,1,0:T(8,128)(2,1)} %collective-permute-done.33, bf16[8,192,256]{2,1,0:T(8,128)(2,1)S(1)} %get-tuple-element.367), kind=kLoop, calls=%fused_computation.11 | loop fusion | flops 1572864 | bytes 2359296 | tf_op jit(solution)/shard_map/convert_element_type | solution.py:878
  185.8 3.8 %collective-permute-done.40 = bf16[2,1,1,96,768]{4,3,0,2,1:T(8,128)(2,1)S(1)} collective-permute-done((bf16[2,1,1,96,768]{4,3,0,2,1:T(8,128)(2,1)S(1)}, bf16[2,1,1,96,768]{4,3,0,2,1:T(8,128)(2,1)S(1)}, u32[]{:S(2)}, u32[]{:S(2)}) %collective-permute-start.40) | collective-permute-done | bytes 294944 | tf_op jit(solution)/shard_map/ppermute | solution.py:890
  189.7 14.5 %condition_back.1 = (f32[256,768]{1,0:T(8,128)}, f32[768,768]{1,0:T(8,128)}, f32[768,4608]{1,0:T(8,128)}) custom-call(bf16[32,4608]{1,0:T(8,128)(2,1)} %copy-done, f32[32,256]{1,0:T(8,128)} %get-tuple-element.372.embedded, f32[32,768]{1,0:T(8,128)} %get-tuple-element.373.inner_pre, f32[32,768]{1,0:T(8,128)} %get-tuple-element.374.inner, ...), custom_call_target="tpu_custom_call" | custom-call | flops 1 | bytes 1 | tf_op jit(solution)/shard_map/condition_back/pallas_call | solution.py:773
  204.2 2.8 %select_convert_fusion = f32[2,2,2,96,768]{4,3,2,1,0:T(8,128)} fusion(pred[2]{0:T(512)(128)(4,1)S(1)} %iota_compare_fusion.2, bf16[2,2,96,768]{3,2,1,0:T(8,128)(2,1)} %bitcast.30, bf16[2,2,96,768]{3,2,1,0:T(8,128)(2,1)S(1)} %bitcast.60), kind=kLoop, calls=%fused_computation.8 | loop fusion | flops 1179648 | bytes 3538946 | tf_op jit(solution)/shard_map/convert_element_type | solution.py:955
  208.1 1.4 convert_bitcast_fusion
  (162 shorter events, 26.0 us)
Async XLA Ops:
  0.6 12.3 %collective-permute-start.1 = (bf16[4,192,256]{2,1,0:T(8,128)(2,1)}, bf16[4,192,256]{2,1,0:T(8,128)(2,1)S(1)}, u32[]{:S(2)}, u32[]{:S(2)}) collective-permute-start(bf16[4,192,256]{2,1,0:T(8,128)(2,1)} %bitcast.82), channel_id=1, source_target_pairs={{0,2},{2,0},{1,3},{3,1},{4,6},{6,4},{5,7},{7,5},{8,10},{10,8},{9,1... | collective-permute-start | bytes 1179656 | tf_op jit(solution)/shard_map/ppermute | solution.py:874
  3.6 11.1 %collective-permute-start = (bf16[4,192,256]{2,1,0:T(8,128)(2,1)}, bf16[4,192,256]{2,1,0:T(8,128)(2,1)S(1)}, u32[]{:S(2)}, u32[]{:S(2)}) collective-permute-start(bf16[4,192,256]{2,1,0:T(8,128)(2,1)} %bitcast.83), channel_id=1, source_target_pairs={{0,1},{1,0},{2,3},{3,2},{4,5},{5,4},{6,7},{7,6},{8,9},{9,8},{10,11... | collective-permute-start | bytes 1179656 | tf_op jit(solution)/shard_map/ppermute | solution.py:870
  3.7 9.4 %copy-start.12 = (bf16[4,256,192]{1,2,0:T(8,128)(2,1)S(1)}, bf16[4,256,192]{1,2,0:T(8,128)(2,1)}, u32[]{:S(2)}) copy-start(bf16[4,256,192]{1,2,0:T(8,128)(2,1)} %param.14) | copy-start | bytes 1179652
  13.0 1.8 collective-permute-start.2
  13.1 11.4 %collective-permute-start.3 = (bf16[4,192,256]{2,1,0:T(8,128)(2,1)S(1)}, bf16[4,192,256]{2,1,0:T(8,128)(2,1)S(1)}, u32[]{:S(2)}, u32[]{:S(2)}) collective-permute-start(bf16[4,192,256]{2,1,0:T(8,128)(2,1)S(1)} %bitcast.88), channel_id=1, source_target_pairs={{0,2},{2,0},{1,3},{3,1},{4,6},{6,4},{5,7},{7,5},{8,10},{10,8},{9,1... | collective-permute-start | bytes 1179656 | tf_op jit(solution)/shard_map/ppermute | solution.py:874
  23.4 2.0 collective-permute-start.4
  23.6 17.0 %collective-permute-start.9 = (bf16[4,192,256]{2,1,0:T(8,128)(2,1)S(1)}, bf16[4,192,256]{2,1,0:T(8,128)(2,1)S(1)}, u32[]{:S(2)}, u32[]{:S(2)}) collective-permute-start(bf16[4,192,256]{2,1,0:T(8,128)(2,1)S(1)} %bitcast.89), channel_id=1, source_target_pairs={{0,1},{1,0},{2,3},{3,2},{4,5},{5,4},{6,7},{7,6},{8,9},{9,8},{10,11... | collective-permute-start | bytes 1179656 | tf_op jit(solution)/shard_map/ppermute | solution.py:870
  24.5 11.3 %copy-start.14 = (bf16[4,192,256]{2,1,0:T(8,128)(2,1)}, bf16[4,192,256]{2,1,0:T(8,128)(2,1)S(1)}, u32[]{:S(2)}) copy-start(bf16[4,192,256]{2,1,0:T(8,128)(2,1)S(1)} %collective-permute-done.3.refs_2_) | copy-start | bytes 1179652
  24.5 16.1 %collective-permute-start.10 = (bf16[4,192,256]{2,1,0:T(8,128)(2,1)S(1)}, bf16[4,192,256]{2,1,0:T(8,128)(2,1)S(1)}, u32[]{:S(2)}, u32[]{:S(2)}) collective-permute-start(bf16[4,192,256]{2,1,0:T(8,128)(2,1)S(1)} %collective-permute-done.3.refs_2_), channel_id=1, source_target_pairs={{0,1},{1,0},{2,3},{3,2},{4,5},{5,4},{6,7},{7,6},{8,9},{9,8},{10,11... | collective-permute-start | bytes 1179656 | tf_op jit(solution)/shard_map/ppermute | solution.py:870
  26.5 11.2 %collective-permute-start.6 = (bf16[256,768]{1,0:T(8,128)(2,1)S(1)}, bf16[256,768]{1,0:T(8,128)(2,1)S(1)}, u32[]{:S(2)}, u32[]{:S(2)}) collective-permute-start(bf16[256,768]{1,0:T(8,128)(2,1)S(1)} %add_convert_fusion.10), channel_id=1, source_target_pairs={{0,2},{2,0},{1,3},{3,1},{4,6},{6,4},{5,7},{7,5},{8,10},{10,8},{9,1... | collective-permute-start | bytes 1179656 | tf_op jit(solution)/shard_map/ppermute | solution.py:874
  35.8 2.1 %collective-permute-start.5 = (bf16[256,768]{1,0:T(8,128)(2,1)}, bf16[256,768]{1,0:T(8,128)(2,1)S(1)}, u32[]{:S(2)}, u32[]{:S(2)}) collective-permute-start(bf16[256,768]{1,0:T(8,128)(2,1)} %get-tuple-element.222), channel_id=1, source_target_pairs={{0,1},{1,0},{2,3},{3,2},{4,5},{5,4},{6,7},{7,6},{8,9},{9,8},{10,11... | collective-permute-start | bytes 1179656 | tf_op jit(solution)/shard_map/ppermute | solution.py:870
  37.9 2.8 %collective-permute-start.8 = (bf16[256,768]{1,0:T(8,128)(2,1)S(1)}, bf16[256,768]{1,0:T(8,128)(2,1)S(1)}, u32[]{:S(2)}, u32[]{:S(2)}) collective-permute-start(bf16[256,768]{1,0:T(8,128)(2,1)S(1)} %add_convert_fusion.9.refs_5_.refs_1_), channel_id=1, source_target_pairs={{0,1},{1,0},{2,3},{3,2},{4,5},{5,4},{6,7},{7,6},{8,9},{9,8},{10,11... | collective-permute-start | bytes 1179656 | tf_op jit(solution)/shard_map/ppermute | solution.py:870
  39.1 18.0 %collective-permute-start.7 = (bf16[256,768]{1,0:T(8,128)(2,1)S(1)}, bf16[256,768]{1,0:T(8,128)(2,1)S(1)}, u32[]{:S(2)}, u32[]{:S(2)}) collective-permute-start(bf16[256,768]{1,0:T(8,128)(2,1)S(1)} %add_convert_fusion.8), channel_id=1, source_target_pairs={{0,2},{2,0},{1,3},{3,1},{4,6},{6,4},{5,7},{7,5},{8,10},{10,8},{9,1... | collective-permute-start | bytes 1179656 | tf_op jit(solution)/shard_map/ppermute | solution.py:874
  56.9 2.0 collective-permute-start.12
  57.3 3.4 %collective-permute-start.11 = (bf16[256,768]{1,0:T(8,128)(2,1)S(1)}, bf16[256,768]{1,0:T(8,128)(2,1)S(1)}, u32[]{:S(2)}, u32[]{:S(2)}) collective-permute-start(bf16[256,768]{1,0:T(8,128)(2,1)S(1)} %add_convert_fusion.7.refs_5_.refs_1_), channel_id=1, source_target_pairs={{0,1},{1,0},{2,3},{3,2},{4,5},{5,4},{6,7},{7,6},{8,9},{9,8},{10,11... | collective-permute-start | bytes 1179656 | tf_op jit(solution)/shard_map/ppermute | solution.py:870
  60.0 16.3 %collective-permute-start.14 = (bf16[256,768]{1,0:T(8,128)(2,1)S(1)}, bf16[256,768]{1,0:T(8,128)(2,1)S(1)}, u32[]{:S(2)}, u32[]{:S(2)}) collective-permute-start(bf16[256,768]{1,0:T(8,128)(2,1)S(1)} %add_convert_fusion.6), channel_id=1, source_target_pairs={{0,2},{2,0},{1,3},{3,1},{4,6},{6,4},{5,7},{7,5},{8,10},{10,8},{9,1... | collective-permute-start | bytes 1179656 | tf_op jit(solution)/shard_map/ppermute | solution.py:874
  61.4 15.6 %copy-start.5 = (bf16[512,768]{1,0:T(8,128)(2,1)S(1)}, bf16[512,768]{1,0:T(8,128)(2,1)}, u32[]{:S(2)}) copy-start(bf16[512,768]{1,0:T(8,128)(2,1)} %get-tuple-element.261) | copy-start | bytes 2359300
  76.2 5.0 %collective-permute-start.13 = (bf16[256,768]{1,0:T(8,128)(2,1)}, bf16[256,768]{1,0:T(8,128)(2,1)S(1)}, u32[]{:S(2)}, u32[]{:S(2)}) collective-permute-start(bf16[256,768]{1,0:T(8,128)(2,1)} %get-tuple-element.252), channel_id=1, source_target_pairs={{0,1},{1,0},{2,3},{3,2},{4,5},{5,4},{6,7},{7,6},{8,9},{9,8},{10,11... | collective-permute-start | bytes 1179656 | tf_op jit(solution)/shard_map/ppermute | solution.py:870
  76.4 8.1 %collective-permute-start.16 = (bf16[256,768]{1,0:T(8,128)(2,1)S(1)}, bf16[256,768]{1,0:T(8,128)(2,1)S(1)}, u32[]{:S(2)}, u32[]{:S(2)}) collective-permute-start(bf16[256,768]{1,0:T(8,128)(2,1)S(1)} %add_convert_fusion.5.refs_3_), channel_id=1, source_target_pairs={{0,1},{1,0},{2,3},{3,2},{4,5},{5,4},{6,7},{7,6},{8,9},{9,8},{10,11... | collective-permute-start | bytes 1179656 | tf_op jit(solution)/shard_map/ppermute | solution.py:870
  79.6 15.8 %collective-permute-start.18 = (bf16[384,768]{1,0:T(8,128)(2,1)S(1)}, bf16[384,768]{1,0:T(8,128)(2,1)}, u32[]{:S(2)}, u32[]{:S(2)}) collective-permute-start(bf16[384,768]{1,0:T(8,128)(2,1)S(1)} %constant_dynamic-slice_fusion.2), channel_id=1, source_target_pairs={{0,4},{4,0},{8,12},{12,8},{16,20},{20,16},{24,28},{28,24},{1,5},{5... | collective-permute-start | bytes 1769480 | tf_op jit(solution)/shard_map/ppermute | solution.py:890
  81.4 11.7 %collective-permute-start.15 = (bf16[256,768]{1,0:T(8,128)(2,1)S(1)}, bf16[256,768]{1,0:T(8,128)(2,1)}, u32[]{:S(2)}, u32[]{:S(2)}) collective-permute-start(bf16[256,768]{1,0:T(8,128)(2,1)S(1)} %add_convert_fusion.4), channel_id=1, source_target_pairs={{0,2},{2,0},{1,3},{3,1},{4,6},{6,4},{5,7},{7,5},{8,10},{10,8},{9,1... | collective-permute-start | bytes 1179656 | tf_op jit(solution)/shard_map/ppermute | solution.py:874
  94.9 3.4 %collective-permute-start.17 = (bf16[256,768]{1,0:T(8,128)(2,1)}, bf16[256,768]{1,0:T(8,128)(2,1)}, u32[]{:S(2)}, u32[]{:S(2)}) collective-permute-start(bf16[256,768]{1,0:T(8,128)(2,1)} %add_convert_fusion.3.refs_3_), channel_id=1, source_target_pairs={{0,1},{1,0},{2,3},{3,2},{4,5},{5,4},{6,7},{7,6},{8,9},{9,8},{10,11... | collective-permute-start | bytes 1179656 | tf_op jit(solution)/shard_map/ppermute | solution.py:870
  94.9 19.1 %collective-permute-start.22 = (bf16[384,768]{1,0:T(8,128)(2,1)S(1)}, bf16[384,768]{1,0:T(8,128)(2,1)}, u32[]{:S(2)}, u32[]{:S(2)}) collective-permute-start(bf16[384,768]{1,0:T(8,128)(2,1)S(1)} %constant_dynamic-slice_fusion.1), channel_id=1, source_target_pairs={{0,4},{4,0},{8,12},{12,8},{16,20},{20,16},{24,28},{28,24},{1,5},{5... | collective-permute-start | bytes 1769480 | tf_op jit(solution)/shard_map/ppermute | solution.py:890
  96.7 9.7 %collective-permute-start.19 = (bf16[192,768]{1,0:T(8,128)(2,1)S(1)}, bf16[192,768]{1,0:T(8,128)(2,1)S(1)}, u32[]{:S(2)}, u32[]{:S(2)}) collective-permute-start(bf16[192,768]{1,0:T(8,128)(2,1)S(1)} %get-tuple-element.389), channel_id=1, source_target_pairs={{0,8},{4,12},{8,0},{12,4},{16,24},{20,28},{24,16},{28,20},{1,9},{5... | collective-permute-start | bytes 884744 | tf_op jit(solution)/shard_map/ppermute | solution.py:890
  98.4 10.9 %copy-start.22 = (bf16[1024,192]{1,0:T(8,128)(2,1)S(1)}, bf16[1024,192]{1,0:T(8,128)(2,1)}, u32[]{:S(2)}) copy-start(bf16[1024,192]{1,0:T(8,128)(2,1)} %get-tuple-element.305) | copy-start | bytes 1179652
  106.6 10.5 %collective-permute-start.21 = (bf16[96,768]{1,0:T(8,128)(2,1)S(1)}, bf16[96,768]{1,0:T(8,128)(2,1)S(1)}, u32[]{:S(2)}, u32[]{:S(2)}) collective-permute-start(bf16[96,768]{1,0:T(8,128)(2,1)S(1)} %get-tuple-element.399), channel_id=1, source_target_pairs={{0,16},{4,20},{8,24},{12,28},{16,0},{20,4},{24,8},{28,12},{1,17},{... | collective-permute-start | bytes 442376 | tf_op jit(solution)/shard_map/ppermute | solution.py:890
  112.5 17.8 %collective-permute-start.20 = (bf16[384,768]{1,0:T(8,128)(2,1)S(1)}, bf16[384,768]{1,0:T(8,128)(2,1)}, u32[]{:S(2)}, u32[]{:S(2)}) collective-permute-start(bf16[384,768]{1,0:T(8,128)(2,1)S(1)} %constant_dynamic-slice_fusion), channel_id=1, source_target_pairs={{0,4},{4,0},{8,12},{12,8},{16,20},{20,16},{24,28},{28,24},{1,5},{5... | collective-permute-start | bytes 1769480 | tf_op jit(solution)/shard_map/ppermute | solution.py:890
  116.0 11.7 %collective-permute-start.24 = (bf16[192,768]{1,0:T(8,128)(2,1)}, bf16[192,768]{1,0:T(8,128)(2,1)S(1)}, u32[]{:S(2)}, u32[]{:S(2)}) collective-permute-start(bf16[192,768]{1,0:T(8,128)(2,1)} %get-tuple-element.387), channel_id=1, source_target_pairs={{0,8},{4,12},{8,0},{12,4},{16,24},{20,28},{24,16},{28,20},{1,9},{5... | collective-permute-start | bytes 884744 | tf_op jit(solution)/shard_map/ppermute | solution.py:890
  117.1 8.9 %collective-permute-start.23 = (bf16[1,1,1,96,768]{4,3,2,1,0:T(8,128)(2,1)S(1)}, bf16[1,1,1,96,768]{4,3,2,1,0:T(8,128)(2,1)S(1)}, u32[]{:S(2)}, u32[]{:S(2)}) collective-permute-start(bf16[1,1,1,96,768]{4,3,2,1,0:T(8,128)(2,1)S(1)} %bitcast.68), channel_id=1, source_target_pairs={{0,16},{4,20},{8,24},{12,28},{16,0},{20,4},{24,8},{28,12},{1,17},{... | collective-permute-start | bytes 442376 | tf_op jit(solution)/shard_map/ppermute | solution.py:890
  127.8 14.6 %collective-permute-start.26 = (bf16[1,1,2,96,768]{4,3,2,1,0:T(8,128)(2,1)S(1)}, bf16[1,1,2,96,768]{4,3,2,1,0:T(8,128)(2,1)S(1)}, u32[]{:S(2)}, u32[]{:S(2)}) collective-permute-start(bf16[1,1,2,96,768]{4,3,2,1,0:T(8,128)(2,1)S(1)} %broadcast_select_fusion.6), channel_id=1, source_target_pairs={{0,8},{4,12},{8,0},{12,4},{16,24},{20,28},{24,16},{28,20},{1,9},{5... | collective-permute-start | bytes 884744 | tf_op jit(solution)/shard_map/ppermute | solution.py:890
  129.1 14.0 %collective-permute-start.28 = (bf16[96,768]{1,0:T(8,128)(2,1)}, bf16[96,768]{1,0:T(8,128)(2,1)S(1)}, u32[]{:S(2)}, u32[]{:S(2)}) collective-permute-start(bf16[96,768]{1,0:T(8,128)(2,1)} %get-tuple-element.397), channel_id=1, source_target_pairs={{0,16},{4,20},{8,24},{12,28},{16,0},{20,4},{24,8},{28,12},{1,17},{... | collective-permute-start | bytes 442376 | tf_op jit(solution)/shard_map/ppermute | solution.py:890
  131.5 13.9 %collective-permute-start.32 = (bf16[192,768]{1,0:T(8,128)(2,1)S(1)}, bf16[192,768]{1,0:T(8,128)(2,1)S(1)}, u32[]{:S(2)}, u32[]{:S(2)}) collective-permute-start(bf16[192,768]{1,0:T(8,128)(2,1)S(1)} %get-tuple-element.385), channel_id=1, source_target_pairs={{0,8},{4,12},{8,0},{12,4},{16,24},{20,28},{24,16},{28,20},{1,9},{5... | collective-permute-start | bytes 884744 | tf_op jit(solution)/shard_map/ppermute | solution.py:890
  141.8 2.9 %collective-permute-start.30 = (bf16[40,768]{1,0:T(8,128)(2,1)}, bf16[40,768]{1,0:T(8,128)(2,1)S(1)}, u32[]{:S(2)}, u32[]{:S(2)}) collective-permute-start(bf16[40,768]{1,0:T(8,128)(2,1)} %get-tuple-element.341), channel_id=1, source_target_pairs={{0,1},{1,0},{2,3},{3,2},{4,5},{5,4},{6,7},{7,6},{8,9},{9,8},{10,11... | collective-permute-start | bytes 184328 | tf_op jit(solution)/shard_map/ppermute | solution.py:870
  141.9 17.9 %collective-permute-start.25 = (bf16[2,8,192,256]{3,2,1,0:T(8,128)(2,1)}, bf16[2,8,192,256]{3,2,1,0:T(8,128)(2,1)S(1)}, u32[]{:S(2)}, u32[]{:S(2)}) collective-permute-start(bf16[2,8,192,256]{3,2,1,0:T(8,128)(2,1)} %get-tuple-element.333), channel_id=1, source_target_pairs={{0,1},{1,0},{2,3},{3,2},{4,5},{5,4},{6,7},{7,6},{8,9},{9,8},{10,11... | collective-permute-start | bytes 4718600 | tf_op jit(solution)/shard_map/ppermute | solution.py:870
  142.5 15.6 %collective-permute-start.27 = (bf16[1,2,2,96,768]{4,3,2,1,0:T(8,128)(2,1)S(1)}, bf16[1,2,2,96,768]{4,3,2,1,0:T(8,128)(2,1)S(1)}, u32[]{:S(2)}, u32[]{:S(2)}) collective-permute-start(bf16[1,2,2,96,768]{4,3,2,1,0:T(8,128)(2,1)S(1)} %broadcast_select_fusion.3), channel_id=1, source_target_pairs={{0,4},{4,0},{8,12},{12,8},{16,20},{20,16},{24,28},{28,24},{1,5},{5... | collective-permute-start | bytes 1769480 | tf_op jit(solution)/shard_map/ppermute | solution.py:890
  143.1 14.8 %collective-permute-start.29 = (bf16[1,1,1,96,768]{4,3,2,1,0:T(8,128)(2,1)S(1)}, bf16[1,1,1,96,768]{4,3,2,1,0:T(8,128)(2,1)S(1)}, u32[]{:S(2)}, u32[]{:S(2)}) collective-permute-start(bf16[1,1,1,96,768]{4,3,2,1,0:T(8,128)(2,1)S(1)} %bitcast.66), channel_id=1, source_target_pairs={{0,16},{4,20},{8,24},{12,28},{16,0},{20,4},{24,8},{28,12},{1,17},{... | collective-permute-start | bytes 442376 | tf_op jit(solution)/shard_map/ppermute | solution.py:890
  144.7 4.3 %collective-permute-start.31 = (bf16[40,768]{1,0:T(8,128)(2,1)S(1)}, bf16[40,768]{1,0:T(8,128)(2,1)S(1)}, u32[]{:S(2)}, u32[]{:S(2)}) collective-permute-start(bf16[40,768]{1,0:T(8,128)(2,1)S(1)} %add_convert_fusion.27), channel_id=1, source_target_pairs={{0,2},{2,0},{1,3},{3,1},{4,6},{6,4},{5,7},{7,5},{8,10},{10,8},{9,1... | collective-permute-start | bytes 184328 | tf_op jit(solution)/shard_map/ppermute | solution.py:874
  145.5 16.8 %collective-permute-start.34 = (bf16[96,768]{1,0:T(8,128)(2,1)S(1)}, bf16[96,768]{1,0:T(8,128)(2,1)S(1)}, u32[]{:S(2)}, u32[]{:S(2)}) collective-permute-start(bf16[96,768]{1,0:T(8,128)(2,1)S(1)} %get-tuple-element.395), channel_id=1, source_target_pairs={{0,16},{4,20},{8,24},{12,28},{16,0},{20,4},{24,8},{28,12},{1,17},{... | collective-permute-start | bytes 442376 | tf_op jit(solution)/shard_map/ppermute | solution.py:890
  149.0 13.4 %collective-permute-start.35 = (bf16[1,42,768]{2,1,0:T(8,128)(2,1)S(1)}, bf16[1,42,768]{2,1,0:T(8,128)(2,1)S(1)}, u32[]{:S(2)}, u32[]{:S(2)}) collective-permute-start(bf16[1,42,768]{2,1,0:T(8,128)(2,1)S(1)} %maximum_bitcast_fusion), channel_id=1, source_target_pairs={{0,16},{4,20},{8,24},{12,28},{16,0},{20,4},{24,8},{28,12},{1,17},{... | collective-permute-start | bytes 193544 | tf_op jit(solution)/shard_map/ppermute | solution.py:890
  158.1 14.9 %collective-permute-start.39 = (bf16[1,1,2,96,768]{4,3,2,1,0:T(8,128)(2,1)S(1)}, bf16[1,1,2,96,768]{4,3,2,1,0:T(8,128)(2,1)S(1)}, u32[]{:S(2)}, u32[]{:S(2)}) collective-permute-start(bf16[1,1,2,96,768]{4,3,2,1,0:T(8,128)(2,1)S(1)} %broadcast_select_fusion.5), channel_id=1, source_target_pairs={{0,8},{4,12},{8,0},{12,4},{16,24},{20,28},{24,16},{28,20},{1,9},{5... | collective-permute-start | bytes 884744 | tf_op jit(solution)/shard_map/ppermute | solution.py:890
  162.4 9.3 %collective-permute-start.36 = (bf16[2,42,768]{2,1,0:T(8,128)(2,1)S(1)}, bf16[2,42,768]{2,1,0:T(8,128)(2,1)S(1)}, u32[]{:S(2)}, u32[]{:S(2)}) collective-permute-start(bf16[2,42,768]{2,1,0:T(8,128)(2,1)S(1)} %constant_dynamic-update-slice_fusion), channel_id=1, source_target_pairs={{0,8},{4,12},{8,0},{12,4},{16,24},{20,28},{24,16},{28,20},{1,9},{5... | collective-permute-start | bytes 387080 | tf_op jit(solution)/shard_map/ppermute | solution.py:890
  162.9 11.2 %collective-permute-start.38 = (bf16[1,1,1,96,768]{4,3,2,1,0:T(8,128)(2,1)S(1)}, bf16[1,1,1,96,768]{4,3,2,1,0:T(8,128)(2,1)S(1)}, u32[]{:S(2)}, u32[]{:S(2)}) collective-permute-start(bf16[1,1,1,96,768]{4,3,2,1,0:T(8,128)(2,1)S(1)} %bitcast.67), channel_id=1, source_target_pairs={{0,4},{4,0},{8,12},{12,8},{16,20},{20,16},{24,28},{28,24},{1,5},{5... | collective-permute-start | bytes 442376 | tf_op jit(solution)/shard_map/ppermute | solution.py:890
  163.8 19.8 %collective-permute-start.33 = (bf16[8,192,256]{2,1,0:T(8,128)(2,1)S(1)}, bf16[8,192,256]{2,1,0:T(8,128)(2,1)}, u32[]{:S(2)}, u32[]{:S(2)}) collective-permute-start(bf16[8,192,256]{2,1,0:T(8,128)(2,1)S(1)} %get-tuple-element.392), channel_id=1, source_target_pairs={{0,2},{2,0},{1,3},{3,1},{4,6},{6,4},{5,7},{7,5},{8,10},{10,8},{9,1... | collective-permute-start | bytes 2359304 | tf_op jit(solution)/shard_map/ppermute | solution.py:874
  171.8 9.9 %collective-permute-start.37 = (bf16[4,42,768]{2,1,0:T(8,128)(2,1)S(1)}, bf16[4,42,768]{2,1,0:T(8,128)(2,1)S(1)}, u32[]{:S(2)}, u32[]{:S(2)}) collective-permute-start(bf16[4,42,768]{2,1,0:T(8,128)(2,1)S(1)} %constant_dynamic-update-slice_fusion.2), channel_id=1, source_target_pairs={{0,4},{4,0},{8,12},{12,8},{16,20},{20,16},{24,28},{28,24},{1,5},{5... | collective-permute-start | bytes 774152 | tf_op jit(solution)/shard_map/ppermute | solution.py:890
  173.1 31.1 %collective-permute-start.42 = (bf16[1,2,2,96,768]{4,3,2,1,0:T(8,128)(2,1)S(1)}, bf16[1,2,2,96,768]{4,3,2,1,0:T(8,128)(2,1)}, u32[]{:S(2)}, u32[]{:S(2)}) collective-permute-start(bf16[1,2,2,96,768]{4,3,2,1,0:T(8,128)(2,1)S(1)} %broadcast_select_fusion.2), channel_id=1, source_target_pairs={{0,4},{4,0},{8,12},{12,8},{16,20},{20,16},{24,28},{28,24},{1,5},{5... | collective-permute-start | bytes 1769480 | tf_op jit(solution)/shard_map/ppermute | solution.py:890
  174.2 15.3 %collective-permute-start.40 = (bf16[2,1,1,96,768]{4,3,0,2,1:T(8,128)(2,1)S(1)}, bf16[2,1,1,96,768]{4,3,0,2,1:T(8,128)(2,1)S(1)}, u32[]{:S(2)}, u32[]{:S(2)}) collective-permute-start(bf16[2,1,1,96,768]{4,3,0,2,1:T(8,128)(2,1)S(1)} %broadcast_select_fusion.4), channel_id=1, source_target_pairs={{0,16},{4,20},{8,24},{12,28},{16,0},{20,4},{24,8},{28,12},{1,17},{... | collective-permute-start | bytes 884744 | tf_op jit(solution)/shard_map/ppermute | solution.py:890
  182.2 7.5 %copy-start = (bf16[32,4608]{1,0:T(8,128)(2,1)}, bf16[32,4608]{1,0:T(8,128)(2,1)S(1)}, u32[]{:S(2)}) copy-start(bf16[32,4608]{1,0:T(8,128)(2,1)S(1)} %reshape.116.gmod) | copy-start | bytes 884740
  189.6 17.4 %collective-permute-start.41 = (bf16[2,1,2,96,768]{4,3,2,0,1:T(8,128)(2,1)S(1)}, bf16[2,1,2,96,768]{4,3,2,0,1:T(8,128)(2,1)S(1)}, u32[]{:S(2)}, u32[]{:S(2)}) collective-permute-start(bf16[2,1,2,96,768]{4,3,2,0,1:T(8,128)(2,1)S(1)} %broadcast_select_fusion.1), channel_id=1, source_target_pairs={{0,8},{4,12},{8,0},{12,4},{16,24},{20,28},{24,16},{28,20},{1,9},{5... | collective-permute-start | bytes 1769480 | tf_op jit(solution)/shard_map/ppermute | solution.py:890
  (22 other events, 50.7 us)

commit v5 on v4

--- a/solution.py
+++ b/solution.py
@@ -1118,27 +1118,24 @@
     down_grad = down_sum.finish(order, F32)
     made = order(functools.partial(slice_halves, x), in_b[2], core_swap(in_b[3]))
     order.advance(attn_sum, mods)
-    order.advance(mods)
-    order.advance(up_sum)
     order.advance(attn_sum)
     while not all(c.done() for c in (mods, up_sum)):
-        order.advance(mods)
-        order.advance(up_sum)
+        order.advance(mods, up_sum)
 
     def unpack(held):
         gmod = held[:, :rows].reshape(latent_total, 6 * width)
         taps = jnp.sum(held[:, rows:].astype(F32), 0) * factor
         return gmod, jnp.sum(gmod.astype(F32), 0) * factor, taps[:9], taps[9:]
 
-    unpacked = order(lambda a, b: unpack(join(a, b)), *mods.came)
-    order.last = tuple(unpacked)
-    gmod, ada_bias_grad, attn_taps, ffn_taps = unpacked
     final_out, final_grad = order(
         lambda a, b: (sum_pair(a[:per_dev], b[:per_dev]), sum_pair(a[per_dev:], b[per_dev:])), made[0], x_swap(made[1])
     )
     order.last = (final_out, final_grad)
     while not attn_sum.done():
         order.advance(attn_sum)
+    unpacked = order(lambda a, b: unpack(join(a, b)), *mods.came)
+    order.last = tuple(unpacked)
+    gmod, ada_bias_grad, attn_taps, ffn_taps = unpacked
     time_in_grad, time_out_grad, ada_weight_grad = order(
         lambda g: condition_back(g, embedded, stages, time_out, ada_weight, factor), gmod
     )

time: 210 us -> 205 us (0.976)
  waiting for transfers between devices: 35.8 us -> 32.6 us
  other arithmetic: 22.2 us -> 19.9 us
    ppermute x21, waiting for transfers between devices: 28.8 us -> 17.1 us  [wide_swap(): return lax.ppermute(v, 'wide', [(i, i ^ bit) for i in range(count)])]
    ppermute x8, waiting for transfers between devices: 4.87 us -> 13.4 us  [x_swap(): return lax.ppermute(v, 'narrow', [(0, 2), (2, 0), (1, 3), (3, 1)])]
  transfers between devices with their start and end apart: 43 -> 43, of which waited for: 12 -> 12; matrix products, arithmetic and copies ran while one was open for 13% -> 12% of each run, Pallas kernels for 48% -> 49%
where the time goes in v5:
time: 205 us; the launch traced here: 204 us
  Pallas kernels  100 us (49%)
  starting transfers between devices  37.1 us (18%)
  waiting for transfers between devices  32.6 us (16%)
  other arithmetic  19.9 us (10%)
  local copies, waits for them, and re-layouts  6.83 us (3%)
  matrix products  6.18 us (3%)
    pallas_call x8, Pallas kernels, call(): pl.pallas_call(run, name=name, out_shape=[jax.ShapeDtypeStruct(o[0], o[1]...  77.2 us
    ppermute x21, starting transfers between devices, wide_swap(): return lax.ppermute(v, 'wide', [(i, i ^ bit) for i in range(count)])  22.8 us
    ppermute x21, waiting for transfers between devices, wide_swap(): return lax.ppermute(v, 'wide', [(i, i ^ bit) for i in range(count)])  17.1 us
    pallas_call x1, Pallas kernels, condition_back(): pl.pallas_call(functools.partial(condition_back_body, factor), name='cond...  14.5 us
    ppermute x8, waiting for transfers between devices, x_swap(): return lax.ppermute(v, 'narrow', [(0, 2), (2, 0), (1, 3), (3, 1)])  13.4 us
    convert_element_type x21, other arithmetic, sum_pair(): return (a.astype(F32) + b.astype(F32)).astype(BF)  12.8 us
    ppermute x8, starting transfers between devices, x_swap(): return lax.ppermute(v, 'narrow', [(0, 2), (2, 0), (1, 3), (3, 1)])  11.6 us
    pallas_call x1, Pallas kernels, condition(): pl.pallas_call(functools.partial(condition_body, steps), name='condition'...  8.82 us
  transfers between devices with their start and end apart: 43, of which 12 were waited for; matrix products, arithmetic and copies ran while one was open for 12% of the time, Pallas kernels for 49%

profile of v5, /device:TPU:0, one launch (start us, length us, event | category | flops | bytes accessed | tf_op | source)
XLA Modules:
  0.0 204.5 jit_solution(5720721594561296958)
XLA Ops:
  0.6 3.0 %collective-permute-start.1 = (bf16[4,192,256]{2,1,0:T(8,128)(2,1)}, bf16[4,192,256]{2,1,0:T(8,128)(2,1)S(1)}, u32[]{:S(2)}, u32[]{:S(2)}) collective-permute-start(bf16[4,192,256]{2,1,0:T(8,128)(2,1)} %bitcast.83), channel_id=1, source_target_pairs={{0,2},{2,0},{1,3},{3,1},{4,6},{6,4},{5,7},{7,5},{8,10},{10,8},{9,1... | collective-permute-start | bytes 1179656 | tf_op jit(solution)/shard_map/ppermute | solution.py:874
  3.7 8.8 %condition.1 = (f32[4,6,768]{2,1,0:T(8,128)}, f32[32,256]{1,0:T(8,128)}, f32[32,768]{1,0:T(8,128)}, f32[32,768]{1,0:T(8,128)}, f32[32,768]{1,0:T(8,128)}, /*index=5*/f32[32,768]{1,0:T(8,128)}) custom-call(s32[32]{0:T(128)} %stamps.1, s32[1]{0:T(128)} %bitcast.2.wide, f32[36,128]{1,0:T(8,128)} %bitcast.91, f32[256,768]{1,0:T(8,128)} %time_in.1, ...), custom_call_target="tpu_custom_call" | custom-call | flops 8000000000 | bytes 1000000 | tf_op jit(solution)/shard_map/condition/pallas_call | solution.py:704
  13.1 1.7 collective-permute-start.3
  15.7 7.7 %attn_fwd.2 = (bf16[512,768]{1,0:T(8,128)(2,1)}, bf16[512,192]{1,0:T(8,128)(2,1)}, bf16[512,192]{1,0:T(8,128)(2,1)}, bf16[512,192]{1,0:T(8,128)(2,1)}, bf16[256,...) custom-call(s32[1]{0:T(128)} %bitcast.s_ref, ...), custom_call_target="tpu_custom_call" | custom-call | flops 6000000000 | bytes 1000000 | tf_op jit(solution)/shard_map/attn_fwd/pallas_call | solution.py:567
  25.4 1.1 add_convert_fusion.10
  26.5 1.6 collective-permute-start.6
  28.1 7.7 %attn_fwd.3 = (bf16[512,768]{1,0:T(8,128)(2,1)}, bf16[512,192]{1,0:T(8,128)(2,1)}, bf16[512,192]{1,0:T(8,128)(2,1)}, bf16[512,192]{1,0:T(8,128)(2,1)}, bf16[256,...) custom-call(s32[1]{0:T(128)} %bitcast.s_ref, ...), custom_call_target="tpu_custom_call", output_to_operand_aliasing={{6}: (9, {}), {7}: (10, {})} | custom-call | flops 6000000000 | bytes 1000000 | tf_op jit(solution)/shard_map/attn_fwd/pallas_call | solution.py:567
  35.9 1.8 collective-permute-done.6
  38.0 1.1 add_convert_fusion.8
  39.1 1.6 collective-permute-start.7
  42.4 14.5 %ffn.2 = (bf16[512,768]{1,0:T(8,128)(2,1)}, bf16[256,768]{1,0:T(8,128)(2,1)}, bf16[256,768]{1,0:T(8,128)(2,1)}, f32[2,1,768]{2,1,0:T(1,128)}, f32[16,768]{1,0:T(...) custom-call(s32[1]{0:T(128)} %bitcast.s_ref, ...), custom_call_target="tpu_custom_call" | custom-call | flops 10000000000 | bytes 1000000 | tf_op jit(solution)/shard_map/ffn/pallas_call | solution.py:567
  57.7 1.2 collective-permute-done.12
  58.9 1.1 add_convert_fusion.6
  61.4 14.8 %ffn.3 = (bf16[512,768]{1,0:T(8,128)(2,1)}, bf16[256,768]{1,0:T(8,128)(2,1)}, bf16[256,768]{1,0:T(8,128)(2,1)}, f32[2,1,768]{2,1,0:T(1,128)}, f32[16,768]{1,0:T(...) custom-call(s32[1]{0:T(128)} %bitcast.s_ref, ...), custom_call_target="tpu_custom_call", output_to_operand_aliasing={{7}: (13, {}), {8}: (14, {}), {9}: (15, {}), {10}: (16, {})} | custom-call | flops 10000000000 | bytes 1000000 | tf_op jit(solution)/shard_map/ffn/pallas_call | solution.py:567
  79.6 1.6 collective-permute-start.18
  81.4 1.6 collective-permute-start.15
  82.9 1.5 multiply_convert_fusion
  85.3 7.8 %attn_bwd.2 = (bf16[512,768]{1,0:T(8,128)(2,1)}, f32[2,8,768]{2,1,0:T(8,128)}, bf16[1024,768]{1,0:T(8,128)(2,1)}, bf16[1024,576]{1,0:T(8,128)(2,1)}) custom-call(s32[1]{0:T(128)} %bitcast.s_ref, bf16[512,768]{1,0:T(8,128)(2,1)} %get-tuple-element.211.refs_4_.refs_0_, bf16[256,768]{1,0:T(8,128)(2,1)} %copy-done.7, bf16[256,768]{1,0:T(8,128)(2,1)} %copy-done.15, ...), custom_call_target="tpu_custom_call" | custom-call | flops 6000000000 | bytes 1000000 | tf_op jit(solution)/shard_map/attn_bwd/pallas_call | solution.py:567
  93.1 1.9 add_convert_fusion.3.refs_3_
  95.4 1.3 add_convert_fusion.15
  96.7 1.6 collective-permute-start.19
  98.4 8.1 %attn_bwd.3 = (bf16[512,768]{1,0:T(8,128)(2,1)}, f32[2,8,768]{2,1,0:T(8,128)}, bf16[1024,768]{1,0:T(8,128)(2,1)}, bf16[1024,576]{1,0:T(8,128)(2,1)}) custom-call(s32[1]{0:T(128)} %bitcast.s_ref, bf16[512,768]{1,0:T(8,128)(2,1)} %get-tuple-element.220.refs_4_.refs_0_, bf16[256,768]{1,0:T(8,128)(2,1)} %copy-done.6, ...), custom_call_target="tpu_custom_call", output_to_operand_aliasing={{2}: (13, {}), {3}: (14, {})} | custom-call | flops 6000000000 | bytes 1000000 | tf_op jit(solution)/shard_map/attn_bwd/pallas_call | solution.py:567
  106.6 2.7 %collective-permute-start.21 = (bf16[96,768]{1,0:T(8,128)(2,1)S(1)}, bf16[96,768]{1,0:T(8,128)(2,1)S(1)}, u32[]{:S(2)}, u32[]{:S(2)}) collective-permute-start(bf16[96,768]{1,0:T(8,128)(2,1)S(1)} %get-tuple-element.399), channel_id=1, source_target_pairs={{0,16},{4,20},{8,24},{12,28},{16,0},{20,4},{24,8},{28,12},{1,17},{... | collective-permute-start | bytes 442376 | tf_op jit(solution)/shard_map/ppermute | solution.py:890
  109.2 1.9 fusion
  111.2 1.1 multiply_convert_fusion.2
  112.5 1.6 collective-permute-start.20
  114.1 2.0 add_convert_fusion.13
  117.7 8.2 %input_bwd.2 = (f32[16,768]{1,0:T(8,128)}, f32[2,8,768]{2,1,0:T(8,128)}, bf16[2,8,192,256]{3,2,1,0:T(8,128)(2,1)}, bf16[2,8,192,256]{3,2,1,0:T(8,128)(2,1)}) custom-call(s32[1]{0:T(128)} %bitcast.s_ref, bf16[512,768]{1,0:T(8,128)(2,1)} %get-tuple-element.211.refs_4_.refs_0_, ...), custom_call_target="tpu_custom_call", output_to_operand_aliasing={{2}: (10, {}), {3}: (11, {})} | custom-call | flops 6000000000 | bytes 1000000 | tf_op jit(solution)/shard_map/input_bwd/pallas_call | solution.py:567
  126.0 1.7 collective-permute-done.24
  129.1 1.1 collective-permute-start.28
  130.2 1.3 add_convert_fusion.11
  131.5 1.9 collective-permute-start.32
  133.4 8.3 %input_bwd.3 = (f32[16,768]{1,0:T(8,128)}, bf16[40,768]{1,0:T(8,128)(2,1)}, bf16[2,8,192,256]{3,2,1,0:T(8,128)(2,1)}, bf16[2,8,192,256]{3,2,1,0:T(8,128)(2,1)}) custom-call(s32[1]{0:T(128)} %bitcast.s_ref, bf16[512,768]{1,0:T(8,128)(2,1)} %get-tuple-element.220.refs_4_.refs_0_, ...), custom_call_target="tpu_custom_call", output_to_operand_aliasing={{2}: (10, {}), {3}: (11, {})} | custom-call | flops 6000000000 | bytes 1000000 | tf_op jit(solution)/shard_map/input_bwd/pallas_call | solution.py:567
  143.1 1.5 collective-permute-start.29
  145.5 1.4 collective-permute-start.34
  147.0 2.0 collective-permute-done.31
  149.0 1.5 collective-permute-start.35
  150.6 7.4 %collective-permute-done.29 = bf16[1,1,1,96,768]{4,3,2,1,0:T(8,128)(2,1)S(1)} collective-permute-done((bf16[1,1,1,96,768]{4,3,2,1,0:T(8,128)(2,1)S(1)}, bf16[1,1,1,96,768]{4,3,2,1,0:T(8,128)(2,1)S(1)}, u32[]{:S(2)}, u32[]{:S(2)}) %collective-permute-start.29) | collective-permute-done | bytes 147488 | tf_op jit(solution)/shard_map/ppermute | solution.py:890
  158.2 1.6 select_convert_fusion.1
  160.8 1.6 collective-permute-done.35
  162.4 1.2 collective-permute-start.38
  164.7 3.2 %collective-permute-done.38 = bf16[1,1,1,96,768]{4,3,2,1,0:T(8,128)(2,1)S(1)} collective-permute-done((bf16[1,1,1,96,768]{4,3,2,1,0:T(8,128)(2,1)S(1)}, bf16[1,1,1,96,768]{4,3,2,1,0:T(8,128)(2,1)S(1)}, u32[]{:S(2)}, u32[]{:S(2)}) %collective-permute-start.38) | collective-permute-done | bytes 147488 | tf_op jit(solution)/shard_map/ppermute | solution.py:890
  168.8 3.1 %collective-permute-done.36 = bf16[2,42,768]{2,1,0:T(8,128)(2,1)S(1)} collective-permute-done((bf16[2,42,768]{2,1,0:T(8,128)(2,1)S(1)}, bf16[2,42,768]{2,1,0:T(8,128)(2,1)S(1)}, u32[]{:S(2)}, u32[]{:S(2)}) %collective-permute-start.36) | collective-permute-done | bytes 129056 | tf_op jit(solution)/shard_map/ppermute | solution.py:890
  171.9 1.2 collective-permute-start.39
  174.2 8.6 %collective-permute-done.33 = bf16[8,192,256]{2,1,0:T(8,128)(2,1)S(1)} collective-permute-done((bf16[8,192,256]{2,1,0:T(8,128)(2,1)S(1)}, bf16[8,192,256]{2,1,0:T(8,128)(2,1)S(1)}, u32[]{:S(2)}, u32[]{:S(2)}) %collective-permute-start.33) | collective-permute-done | bytes 786464 | tf_op jit(solution)/shard_map/ppermute | solution.py:874
  185.9 14.5 %condition_back.1 = (f32[256,768]{1,0:T(8,128)}, f32[768,768]{1,0:T(8,128)}, f32[768,4608]{1,0:T(8,128)}) custom-call(bf16[32,4608]{1,0:T(8,128)(2,1)} %copy-done, f32[32,256]{1,0:T(8,128)} %get-tuple-element.372.embedded, f32[32,768]{1,0:T(8,128)} %get-tuple-element.373.inner_pre, f32[32,768]{1,0:T(8,128)} %get-tuple-element.374.inner, ...), custom_call_target="tpu_custom_call" | custom-call | flops 1 | bytes 1 | tf_op jit(solution)/shard_map/condition_back/pallas_call | solution.py:773
  200.4 1.6 select_convert_fusion
  203.1 1.4 convert_bitcast_fusion
  (162 shorter events, 26.3 us)
Async XLA Ops:
  0.6 12.3 %collective-permute-start.1 = (bf16[4,192,256]{2,1,0:T(8,128)(2,1)}, bf16[4,192,256]{2,1,0:T(8,128)(2,1)S(1)}, u32[]{:S(2)}, u32[]{:S(2)}) collective-permute-start(bf16[4,192,256]{2,1,0:T(8,128)(2,1)} %bitcast.83), channel_id=1, source_target_pairs={{0,2},{2,0},{1,3},{3,1},{4,6},{6,4},{5,7},{7,5},{8,10},{10,8},{9,1... | collective-permute-start | bytes 1179656 | tf_op jit(solution)/shard_map/ppermute | solution.py:874
  3.6 11.1 %collective-permute-start = (bf16[4,192,256]{2,1,0:T(8,128)(2,1)}, bf16[4,192,256]{2,1,0:T(8,128)(2,1)S(1)}, u32[]{:S(2)}, u32[]{:S(2)}) collective-permute-start(bf16[4,192,256]{2,1,0:T(8,128)(2,1)} %bitcast.84), channel_id=1, source_target_pairs={{0,1},{1,0},{2,3},{3,2},{4,5},{5,4},{6,7},{7,6},{8,9},{9,8},{10,11... | collective-permute-start | bytes 1179656 | tf_op jit(solution)/shard_map/ppermute | solution.py:870
  3.7 9.4 %copy-start.12 = (bf16[4,256,192]{1,2,0:T(8,128)(2,1)S(1)}, bf16[4,256,192]{1,2,0:T(8,128)(2,1)}, u32[]{:S(2)}) copy-start(bf16[4,256,192]{1,2,0:T(8,128)(2,1)} %param.14) | copy-start | bytes 1179652
  13.0 1.8 collective-permute-start.2
  13.1 11.4 %collective-permute-start.3 = (bf16[4,192,256]{2,1,0:T(8,128)(2,1)S(1)}, bf16[4,192,256]{2,1,0:T(8,128)(2,1)S(1)}, u32[]{:S(2)}, u32[]{:S(2)}) collective-permute-start(bf16[4,192,256]{2,1,0:T(8,128)(2,1)S(1)} %bitcast.89), channel_id=1, source_target_pairs={{0,2},{2,0},{1,3},{3,1},{4,6},{6,4},{5,7},{7,5},{8,10},{10,8},{9,1... | collective-permute-start | bytes 1179656 | tf_op jit(solution)/shard_map/ppermute | solution.py:874
  23.4 2.0 collective-permute-start.4
  23.6 17.0 %collective-permute-start.9 = (bf16[4,192,256]{2,1,0:T(8,128)(2,1)S(1)}, bf16[4,192,256]{2,1,0:T(8,128)(2,1)S(1)}, u32[]{:S(2)}, u32[]{:S(2)}) collective-permute-start(bf16[4,192,256]{2,1,0:T(8,128)(2,1)S(1)} %bitcast.90), channel_id=1, source_target_pairs={{0,1},{1,0},{2,3},{3,2},{4,5},{5,4},{6,7},{7,6},{8,9},{9,8},{10,11... | collective-permute-start | bytes 1179656 | tf_op jit(solution)/shard_map/ppermute | solution.py:870
  24.5 11.3 %copy-start.14 = (bf16[4,192,256]{2,1,0:T(8,128)(2,1)}, bf16[4,192,256]{2,1,0:T(8,128)(2,1)S(1)}, u32[]{:S(2)}) copy-start(bf16[4,192,256]{2,1,0:T(8,128)(2,1)S(1)} %collective-permute-done.3.refs_2_) | copy-start | bytes 1179652
  24.5 16.1 %collective-permute-start.10 = (bf16[4,192,256]{2,1,0:T(8,128)(2,1)S(1)}, bf16[4,192,256]{2,1,0:T(8,128)(2,1)S(1)}, u32[]{:S(2)}, u32[]{:S(2)}) collective-permute-start(bf16[4,192,256]{2,1,0:T(8,128)(2,1)S(1)} %collective-permute-done.3.refs_2_), channel_id=1, source_target_pairs={{0,1},{1,0},{2,3},{3,2},{4,5},{5,4},{6,7},{7,6},{8,9},{9,8},{10,11... | collective-permute-start | bytes 1179656 | tf_op jit(solution)/shard_map/ppermute | solution.py:870
  26.5 11.2 %collective-permute-start.6 = (bf16[256,768]{1,0:T(8,128)(2,1)S(1)}, bf16[256,768]{1,0:T(8,128)(2,1)S(1)}, u32[]{:S(2)}, u32[]{:S(2)}) collective-permute-start(bf16[256,768]{1,0:T(8,128)(2,1)S(1)} %add_convert_fusion.10), channel_id=1, source_target_pairs={{0,2},{2,0},{1,3},{3,1},{4,6},{6,4},{5,7},{7,5},{8,10},{10,8},{9,1... | collective-permute-start | bytes 1179656 | tf_op jit(solution)/shard_map/ppermute | solution.py:874
  35.8 2.1 %collective-permute-start.5 = (bf16[256,768]{1,0:T(8,128)(2,1)}, bf16[256,768]{1,0:T(8,128)(2,1)S(1)}, u32[]{:S(2)}, u32[]{:S(2)}) collective-permute-start(bf16[256,768]{1,0:T(8,128)(2,1)} %get-tuple-element.222), channel_id=1, source_target_pairs={{0,1},{1,0},{2,3},{3,2},{4,5},{5,4},{6,7},{7,6},{8,9},{9,8},{10,11... | collective-permute-start | bytes 1179656 | tf_op jit(solution)/shard_map/ppermute | solution.py:870
  37.9 2.8 %collective-permute-start.8 = (bf16[256,768]{1,0:T(8,128)(2,1)S(1)}, bf16[256,768]{1,0:T(8,128)(2,1)S(1)}, u32[]{:S(2)}, u32[]{:S(2)}) collective-permute-start(bf16[256,768]{1,0:T(8,128)(2,1)S(1)} %add_convert_fusion.9.refs_5_.refs_1_), channel_id=1, source_target_pairs={{0,1},{1,0},{2,3},{3,2},{4,5},{5,4},{6,7},{7,6},{8,9},{9,8},{10,11... | collective-permute-start | bytes 1179656 | tf_op jit(solution)/shard_map/ppermute | solution.py:870
  39.1 18.0 %collective-permute-start.7 = (bf16[256,768]{1,0:T(8,128)(2,1)S(1)}, bf16[256,768]{1,0:T(8,128)(2,1)S(1)}, u32[]{:S(2)}, u32[]{:S(2)}) collective-permute-start(bf16[256,768]{1,0:T(8,128)(2,1)S(1)} %add_convert_fusion.8), channel_id=1, source_target_pairs={{0,2},{2,0},{1,3},{3,1},{4,6},{6,4},{5,7},{7,5},{8,10},{10,8},{9,1... | collective-permute-start | bytes 1179656 | tf_op jit(solution)/shard_map/ppermute | solution.py:874
  56.9 2.0 collective-permute-start.12
  57.3 3.4 %collective-permute-start.11 = (bf16[256,768]{1,0:T(8,128)(2,1)S(1)}, bf16[256,768]{1,0:T(8,128)(2,1)S(1)}, u32[]{:S(2)}, u32[]{:S(2)}) collective-permute-start(bf16[256,768]{1,0:T(8,128)(2,1)S(1)} %add_convert_fusion.7.refs_5_.refs_1_), channel_id=1, source_target_pairs={{0,1},{1,0},{2,3},{3,2},{4,5},{5,4},{6,7},{7,6},{8,9},{9,8},{10,11... | collective-permute-start | bytes 1179656 | tf_op jit(solution)/shard_map/ppermute | solution.py:870
  60.0 16.3 %collective-permute-start.14 = (bf16[256,768]{1,0:T(8,128)(2,1)S(1)}, bf16[256,768]{1,0:T(8,128)(2,1)S(1)}, u32[]{:S(2)}, u32[]{:S(2)}) collective-permute-start(bf16[256,768]{1,0:T(8,128)(2,1)S(1)} %add_convert_fusion.6), channel_id=1, source_target_pairs={{0,2},{2,0},{1,3},{3,1},{4,6},{6,4},{5,7},{7,5},{8,10},{10,8},{9,1... | collective-permute-start | bytes 1179656 | tf_op jit(solution)/shard_map/ppermute | solution.py:874
  61.4 15.6 %copy-start.5 = (bf16[512,768]{1,0:T(8,128)(2,1)S(1)}, bf16[512,768]{1,0:T(8,128)(2,1)}, u32[]{:S(2)}) copy-start(bf16[512,768]{1,0:T(8,128)(2,1)} %get-tuple-element.261) | copy-start | bytes 2359300
  76.2 5.0 %collective-permute-start.13 = (bf16[256,768]{1,0:T(8,128)(2,1)}, bf16[256,768]{1,0:T(8,128)(2,1)S(1)}, u32[]{:S(2)}, u32[]{:S(2)}) collective-permute-start(bf16[256,768]{1,0:T(8,128)(2,1)} %get-tuple-element.252), channel_id=1, source_target_pairs={{0,1},{1,0},{2,3},{3,2},{4,5},{5,4},{6,7},{7,6},{8,9},{9,8},{10,11... | collective-permute-start | bytes 1179656 | tf_op jit(solution)/shard_map/ppermute | solution.py:870
  76.4 8.1 %collective-permute-start.16 = (bf16[256,768]{1,0:T(8,128)(2,1)S(1)}, bf16[256,768]{1,0:T(8,128)(2,1)S(1)}, u32[]{:S(2)}, u32[]{:S(2)}) collective-permute-start(bf16[256,768]{1,0:T(8,128)(2,1)S(1)} %add_convert_fusion.5.refs_3_), channel_id=1, source_target_pairs={{0,1},{1,0},{2,3},{3,2},{4,5},{5,4},{6,7},{7,6},{8,9},{9,8},{10,11... | collective-permute-start | bytes 1179656 | tf_op jit(solution)/shard_map/ppermute | solution.py:870
  79.6 15.8 %collective-permute-start.18 = (bf16[384,768]{1,0:T(8,128)(2,1)S(1)}, bf16[384,768]{1,0:T(8,128)(2,1)}, u32[]{:S(2)}, u32[]{:S(2)}) collective-permute-start(bf16[384,768]{1,0:T(8,128)(2,1)S(1)} %constant_dynamic-slice_fusion.2), channel_id=1, source_target_pairs={{0,4},{4,0},{8,12},{12,8},{16,20},{20,16},{24,28},{28,24},{1,5},{5... | collective-permute-start | bytes 1769480 | tf_op jit(solution)/shard_map/ppermute | solution.py:890
  81.4 11.7 %collective-permute-start.15 = (bf16[256,768]{1,0:T(8,128)(2,1)S(1)}, bf16[256,768]{1,0:T(8,128)(2,1)}, u32[]{:S(2)}, u32[]{:S(2)}) collective-permute-start(bf16[256,768]{1,0:T(8,128)(2,1)S(1)} %add_convert_fusion.4), channel_id=1, source_target_pairs={{0,2},{2,0},{1,3},{3,1},{4,6},{6,4},{5,7},{7,5},{8,10},{10,8},{9,1... | collective-permute-start | bytes 1179656 | tf_op jit(solution)/shard_map/ppermute | solution.py:874
  94.9 3.4 %collective-permute-start.17 = (bf16[256,768]{1,0:T(8,128)(2,1)}, bf16[256,768]{1,0:T(8,128)(2,1)}, u32[]{:S(2)}, u32[]{:S(2)}) collective-permute-start(bf16[256,768]{1,0:T(8,128)(2,1)} %add_convert_fusion.3.refs_3_), channel_id=1, source_target_pairs={{0,1},{1,0},{2,3},{3,2},{4,5},{5,4},{6,7},{7,6},{8,9},{9,8},{10,11... | collective-permute-start | bytes 1179656 | tf_op jit(solution)/shard_map/ppermute | solution.py:870
  94.9 19.1 %collective-permute-start.22 = (bf16[384,768]{1,0:T(8,128)(2,1)S(1)}, bf16[384,768]{1,0:T(8,128)(2,1)}, u32[]{:S(2)}, u32[]{:S(2)}) collective-permute-start(bf16[384,768]{1,0:T(8,128)(2,1)S(1)} %constant_dynamic-slice_fusion.1), channel_id=1, source_target_pairs={{0,4},{4,0},{8,12},{12,8},{16,20},{20,16},{24,28},{28,24},{1,5},{5... | collective-permute-start | bytes 1769480 | tf_op jit(solution)/shard_map/ppermute | solution.py:890
  96.7 9.7 %collective-permute-start.19 = (bf16[192,768]{1,0:T(8,128)(2,1)S(1)}, bf16[192,768]{1,0:T(8,128)(2,1)S(1)}, u32[]{:S(2)}, u32[]{:S(2)}) collective-permute-start(bf16[192,768]{1,0:T(8,128)(2,1)S(1)} %get-tuple-element.389), channel_id=1, source_target_pairs={{0,8},{4,12},{8,0},{12,4},{16,24},{20,28},{24,16},{28,20},{1,9},{5... | collective-permute-start | bytes 884744 | tf_op jit(solution)/shard_map/ppermute | solution.py:890
  98.4 10.9 %copy-start.22 = (bf16[1024,192]{1,0:T(8,128)(2,1)S(1)}, bf16[1024,192]{1,0:T(8,128)(2,1)}, u32[]{:S(2)}) copy-start(bf16[1024,192]{1,0:T(8,128)(2,1)} %get-tuple-element.305) | copy-start | bytes 1179652
  106.6 10.5 %collective-permute-start.21 = (bf16[96,768]{1,0:T(8,128)(2,1)S(1)}, bf16[96,768]{1,0:T(8,128)(2,1)S(1)}, u32[]{:S(2)}, u32[]{:S(2)}) collective-permute-start(bf16[96,768]{1,0:T(8,128)(2,1)S(1)} %get-tuple-element.399), channel_id=1, source_target_pairs={{0,16},{4,20},{8,24},{12,28},{16,0},{20,4},{24,8},{28,12},{1,17},{... | collective-permute-start | bytes 442376 | tf_op jit(solution)/shard_map/ppermute | solution.py:890
  112.5 17.8 %collective-permute-start.20 = (bf16[384,768]{1,0:T(8,128)(2,1)S(1)}, bf16[384,768]{1,0:T(8,128)(2,1)}, u32[]{:S(2)}, u32[]{:S(2)}) collective-permute-start(bf16[384,768]{1,0:T(8,128)(2,1)S(1)} %constant_dynamic-slice_fusion), channel_id=1, source_target_pairs={{0,4},{4,0},{8,12},{12,8},{16,20},{20,16},{24,28},{28,24},{1,5},{5... | collective-permute-start | bytes 1769480 | tf_op jit(solution)/shard_map/ppermute | solution.py:890
  116.0 11.7 %collective-permute-start.24 = (bf16[192,768]{1,0:T(8,128)(2,1)}, bf16[192,768]{1,0:T(8,128)(2,1)S(1)}, u32[]{:S(2)}, u32[]{:S(2)}) collective-permute-start(bf16[192,768]{1,0:T(8,128)(2,1)} %get-tuple-element.387), channel_id=1, source_target_pairs={{0,8},{4,12},{8,0},{12,4},{16,24},{20,28},{24,16},{28,20},{1,9},{5... | collective-permute-start | bytes 884744 | tf_op jit(solution)/shard_map/ppermute | solution.py:890
  117.1 8.9 %collective-permute-start.23 = (bf16[1,1,1,96,768]{4,3,2,1,0:T(8,128)(2,1)S(1)}, bf16[1,1,1,96,768]{4,3,2,1,0:T(8,128)(2,1)S(1)}, u32[]{:S(2)}, u32[]{:S(2)}) collective-permute-start(bf16[1,1,1,96,768]{4,3,2,1,0:T(8,128)(2,1)S(1)} %bitcast.67), channel_id=1, source_target_pairs={{0,16},{4,20},{8,24},{12,28},{16,0},{20,4},{24,8},{28,12},{1,17},{... | collective-permute-start | bytes 442376 | tf_op jit(solution)/shard_map/ppermute | solution.py:890
  127.8 14.6 %collective-permute-start.26 = (bf16[1,1,2,96,768]{4,3,2,1,0:T(8,128)(2,1)S(1)}, bf16[1,1,2,96,768]{4,3,2,1,0:T(8,128)(2,1)S(1)}, u32[]{:S(2)}, u32[]{:S(2)}) collective-permute-start(bf16[1,1,2,96,768]{4,3,2,1,0:T(8,128)(2,1)S(1)} %broadcast_select_fusion.6), channel_id=1, source_target_pairs={{0,8},{4,12},{8,0},{12,4},{16,24},{20,28},{24,16},{28,20},{1,9},{5... | collective-permute-start | bytes 884744 | tf_op jit(solution)/shard_map/ppermute | solution.py:890
  129.1 14.0 %collective-permute-start.28 = (bf16[96,768]{1,0:T(8,128)(2,1)}, bf16[96,768]{1,0:T(8,128)(2,1)S(1)}, u32[]{:S(2)}, u32[]{:S(2)}) collective-permute-start(bf16[96,768]{1,0:T(8,128)(2,1)} %get-tuple-element.397), channel_id=1, source_target_pairs={{0,16},{4,20},{8,24},{12,28},{16,0},{20,4},{24,8},{28,12},{1,17},{... | collective-permute-start | bytes 442376 | tf_op jit(solution)/shard_map/ppermute | solution.py:890
  131.5 13.9 %collective-permute-start.32 = (bf16[192,768]{1,0:T(8,128)(2,1)S(1)}, bf16[192,768]{1,0:T(8,128)(2,1)S(1)}, u32[]{:S(2)}, u32[]{:S(2)}) collective-permute-start(bf16[192,768]{1,0:T(8,128)(2,1)S(1)} %get-tuple-element.385), channel_id=1, source_target_pairs={{0,8},{4,12},{8,0},{12,4},{16,24},{20,28},{24,16},{28,20},{1,9},{5... | collective-permute-start | bytes 884744 | tf_op jit(solution)/shard_map/ppermute | solution.py:890
  141.8 7.2 %copy-start.11 = (f32[16,768]{1,0:T(8,128)S(1)}, f32[16,768]{1,0:T(8,128)}, u32[]{:S(2)}) copy-start(f32[16,768]{1,0:T(8,128)} %get-tuple-element.348) | copy-start | bytes 147460
  141.8 2.9 %collective-permute-start.30 = (bf16[40,768]{1,0:T(8,128)(2,1)}, bf16[40,768]{1,0:T(8,128)(2,1)S(1)}, u32[]{:S(2)}, u32[]{:S(2)}) collective-permute-start(bf16[40,768]{1,0:T(8,128)(2,1)} %get-tuple-element.341), channel_id=1, source_target_pairs={{0,1},{1,0},{2,3},{3,2},{4,5},{5,4},{6,7},{7,6},{8,9},{9,8},{10,11... | collective-permute-start | bytes 184328 | tf_op jit(solution)/shard_map/ppermute | solution.py:870
  141.9 17.9 %collective-permute-start.25 = (bf16[2,8,192,256]{3,2,1,0:T(8,128)(2,1)}, bf16[2,8,192,256]{3,2,1,0:T(8,128)(2,1)S(1)}, u32[]{:S(2)}, u32[]{:S(2)}) collective-permute-start(bf16[2,8,192,256]{3,2,1,0:T(8,128)(2,1)} %get-tuple-element.333), channel_id=1, source_target_pairs={{0,1},{1,0},{2,3},{3,2},{4,5},{5,4},{6,7},{7,6},{8,9},{9,8},{10,11... | collective-permute-start | bytes 4718600 | tf_op jit(solution)/shard_map/ppermute | solution.py:870
  142.5 15.6 %collective-permute-start.27 = (bf16[1,2,2,96,768]{4,3,2,1,0:T(8,128)(2,1)S(1)}, bf16[1,2,2,96,768]{4,3,2,1,0:T(8,128)(2,1)S(1)}, u32[]{:S(2)}, u32[]{:S(2)}) collective-permute-start(bf16[1,2,2,96,768]{4,3,2,1,0:T(8,128)(2,1)S(1)} %broadcast_select_fusion.3), channel_id=1, source_target_pairs={{0,4},{4,0},{8,12},{12,8},{16,20},{20,16},{24,28},{28,24},{1,5},{5... | collective-permute-start | bytes 1769480 | tf_op jit(solution)/shard_map/ppermute | solution.py:890
  143.1 14.8 %collective-permute-start.29 = (bf16[1,1,1,96,768]{4,3,2,1,0:T(8,128)(2,1)S(1)}, bf16[1,1,1,96,768]{4,3,2,1,0:T(8,128)(2,1)S(1)}, u32[]{:S(2)}, u32[]{:S(2)}) collective-permute-start(bf16[1,1,1,96,768]{4,3,2,1,0:T(8,128)(2,1)S(1)} %bitcast.66), channel_id=1, source_target_pairs={{0,16},{4,20},{8,24},{12,28},{16,0},{20,4},{24,8},{28,12},{1,17},{... | collective-permute-start | bytes 442376 | tf_op jit(solution)/shard_map/ppermute | solution.py:890
  144.7 4.3 %collective-permute-start.31 = (bf16[40,768]{1,0:T(8,128)(2,1)S(1)}, bf16[40,768]{1,0:T(8,128)(2,1)S(1)}, u32[]{:S(2)}, u32[]{:S(2)}) collective-permute-start(bf16[40,768]{1,0:T(8,128)(2,1)S(1)} %add_convert_fusion.27), channel_id=1, source_target_pairs={{0,2},{2,0},{1,3},{3,1},{4,6},{6,4},{5,7},{7,5},{8,10},{10,8},{9,1... | collective-permute-start | bytes 184328 | tf_op jit(solution)/shard_map/ppermute | solution.py:874
  145.5 16.8 %collective-permute-start.34 = (bf16[96,768]{1,0:T(8,128)(2,1)S(1)}, bf16[96,768]{1,0:T(8,128)(2,1)S(1)}, u32[]{:S(2)}, u32[]{:S(2)}) collective-permute-start(bf16[96,768]{1,0:T(8,128)(2,1)S(1)} %get-tuple-element.395), channel_id=1, source_target_pairs={{0,16},{4,20},{8,24},{12,28},{16,0},{20,4},{24,8},{28,12},{1,17},{... | collective-permute-start | bytes 442376 | tf_op jit(solution)/shard_map/ppermute | solution.py:890
  149.0 13.4 %collective-permute-start.35 = (bf16[1,42,768]{2,1,0:T(8,128)(2,1)S(1)}, bf16[1,42,768]{2,1,0:T(8,128)(2,1)S(1)}, u32[]{:S(2)}, u32[]{:S(2)}) collective-permute-start(bf16[1,42,768]{2,1,0:T(8,128)(2,1)S(1)} %maximum_bitcast_fusion), channel_id=1, source_target_pairs={{0,16},{4,20},{8,24},{12,28},{16,0},{20,4},{24,8},{28,12},{1,17},{... | collective-permute-start | bytes 193544 | tf_op jit(solution)/shard_map/ppermute | solution.py:890
  158.1 10.8 %collective-permute-start.37 = (bf16[1,1,2,96,768]{4,3,2,1,0:T(8,128)(2,1)S(1)}, bf16[1,1,2,96,768]{4,3,2,1,0:T(8,128)(2,1)S(1)}, u32[]{:S(2)}, u32[]{:S(2)}) collective-permute-start(bf16[1,1,2,96,768]{4,3,2,1,0:T(8,128)(2,1)S(1)} %broadcast_select_fusion.5), channel_id=1, source_target_pairs={{0,8},{4,12},{8,0},{12,4},{16,24},{20,28},{24,16},{28,20},{1,9},{5... | collective-permute-start | bytes 884744 | tf_op jit(solution)/shard_map/ppermute | solution.py:890
  162.4 5.5 %collective-permute-start.38 = (bf16[1,1,1,96,768]{4,3,2,1,0:T(8,128)(2,1)S(1)}, bf16[1,1,1,96,768]{4,3,2,1,0:T(8,128)(2,1)S(1)}, u32[]{:S(2)}, u32[]{:S(2)}) collective-permute-start(bf16[1,1,1,96,768]{4,3,2,1,0:T(8,128)(2,1)S(1)} %bitcast.68), channel_id=1, source_target_pairs={{0,4},{4,0},{8,12},{12,8},{16,20},{20,16},{24,28},{28,24},{1,5},{5... | collective-permute-start | bytes 442376 | tf_op jit(solution)/shard_map/ppermute | solution.py:890
  163.6 19.1 %collective-permute-start.33 = (bf16[8,192,256]{2,1,0:T(8,128)(2,1)S(1)}, bf16[8,192,256]{2,1,0:T(8,128)(2,1)S(1)}, u32[]{:S(2)}, u32[]{:S(2)}) collective-permute-start(bf16[8,192,256]{2,1,0:T(8,128)(2,1)S(1)} %get-tuple-element.392), channel_id=1, source_target_pairs={{0,2},{2,0},{1,3},{3,1},{4,6},{6,4},{5,7},{7,5},{8,10},{10,8},{9,1... | collective-permute-start | bytes 2359304 | tf_op jit(solution)/shard_map/ppermute | solution.py:874
  164.5 7.4 %collective-permute-start.36 = (bf16[2,42,768]{2,1,0:T(8,128)(2,1)S(1)}, bf16[2,42,768]{2,1,0:T(8,128)(2,1)S(1)}, u32[]{:S(2)}, u32[]{:S(2)}) collective-permute-start(bf16[2,42,768]{2,1,0:T(8,128)(2,1)S(1)} %constant_dynamic-update-slice_fusion), channel_id=1, source_target_pairs={{0,8},{4,12},{8,0},{12,4},{16,24},{20,28},{24,16},{28,20},{1,9},{5... | collective-permute-start | bytes 387080 | tf_op jit(solution)/shard_map/ppermute | solution.py:890
  168.0 15.9 %collective-permute-start.40 = (bf16[2,1,1,96,768]{4,3,0,2,1:T(8,128)(2,1)S(1)}, bf16[2,1,1,96,768]{4,3,0,2,1:T(8,128)(2,1)S(1)}, u32[]{:S(2)}, u32[]{:S(2)}) collective-permute-start(bf16[2,1,1,96,768]{4,3,0,2,1:T(8,128)(2,1)S(1)} %broadcast_select_fusion.4), channel_id=1, source_target_pairs={{0,16},{4,20},{8,24},{12,28},{16,0},{20,4},{24,8},{28,12},{1,17},{... | collective-permute-start | bytes 884744 | tf_op jit(solution)/shard_map/ppermute | solution.py:890
  171.9 12.2 %collective-permute-start.39 = (bf16[4,42,768]{2,1,0:T(8,128)(2,1)S(1)}, bf16[4,42,768]{2,1,0:T(8,128)(2,1)S(1)}, u32[]{:S(2)}, u32[]{:S(2)}) collective-permute-start(bf16[4,42,768]{2,1,0:T(8,128)(2,1)S(1)} %constant_dynamic-update-slice_fusion.2), channel_id=1, source_target_pairs={{0,4},{4,0},{8,12},{12,8},{16,20},{20,16},{24,28},{28,24},{1,5},{5... | collective-permute-start | bytes 774152 | tf_op jit(solution)/shard_map/ppermute | solution.py:890
  173.2 27.2 %collective-permute-start.42 = (bf16[1,2,2,96,768]{4,3,2,1,0:T(8,128)(2,1)S(1)}, bf16[1,2,2,96,768]{4,3,2,1,0:T(8,128)(2,1)S(1)}, u32[]{:S(2)}, u32[]{:S(2)}) collective-permute-start(bf16[1,2,2,96,768]{4,3,2,1,0:T(8,128)(2,1)S(1)} %broadcast_select_fusion.2), channel_id=1, source_target_pairs={{0,4},{4,0},{8,12},{12,8},{16,20},{20,16},{24,28},{28,24},{1,5},{5... | collective-permute-start | bytes 1769480 | tf_op jit(solution)/shard_map/ppermute | solution.py:890
  184.0 18.0 %collective-permute-start.41 = (bf16[2,1,2,96,768]{4,3,2,0,1:T(8,128)(2,1)S(1)}, bf16[2,1,2,96,768]{4,3,2,0,1:T(8,128)(2,1)S(1)}, u32[]{:S(2)}, u32[]{:S(2)}) collective-permute-start(bf16[2,1,2,96,768]{4,3,2,0,1:T(8,128)(2,1)S(1)} %broadcast_select_fusion.1), channel_id=1, source_target_pairs={{0,8},{4,12},{8,0},{12,4},{16,24},{20,28},{24,16},{28,20},{1,9},{5... | collective-permute-start | bytes 1769480 | tf_op jit(solution)/shard_map/ppermute | solution.py:890
  (22 other events, 44.9 us)

commit v6 on v5

--- a/solution.py
+++ b/solution.py
@@ -1131,11 +1131,10 @@
         lambda a, b: (sum_pair(a[:per_dev], b[:per_dev]), sum_pair(a[per_dev:], b[per_dev:])), made[0], x_swap(made[1])
     )
     order.last = (final_out, final_grad)
+    unpacked = order(lambda a, b: unpack(join(a, b)), *mods.came)
+    gmod, ada_bias_grad, attn_taps, ffn_taps = unpacked
     while not attn_sum.done():
         order.advance(attn_sum)
-    unpacked = order(lambda a, b: unpack(join(a, b)), *mods.came)
-    order.last = tuple(unpacked)
-    gmod, ada_bias_grad, attn_taps, ffn_taps = unpacked
     time_in_grad, time_out_grad, ada_weight_grad = order(
         lambda g: condition_back(g, embedded, stages, time_out, ada_weight, factor), gmod
     )

time: 205 us -> 205 us (level)
  waiting for transfers between devices: 32.6 us -> 30 us
    ppermute x8, waiting for transfers between devices: 13.4 us -> 10.9 us  [x_swap(): return lax.ppermute(v, 'narrow', [(0, 2), (2, 0), (1, 3), (3, 1)])]
    ppermute x21, starting transfers between devices: 22.8 us -> 25.3 us  [wide_swap(): return lax.ppermute(v, 'wide', [(i, i ^ bit) for i in range(count)])]
  transfers between devices with their start and end apart: 43 -> 43, of which waited for: 12 -> 14; matrix products, arithmetic and copies ran while one was open for 12% -> 13% of each run, Pallas kernels for 49% -> 49%
where the time goes in v6:
time: 205 us; the launch traced here: 204 us
  Pallas kernels  101 us (49%)
  starting transfers between devices  39 us (19%)
  waiting for transfers between devices  30 us (15%)
  other arithmetic  19.9 us (10%)
  local copies, waits for them, and re-layouts  7.55 us (4%)
  matrix products  6.18 us (3%)
    pallas_call x8, Pallas kernels, call(): pl.pallas_call(run, name=name, out_shape=[jax.ShapeDtypeStruct(o[0], o[1]...  77.2 us
    ppermute x21, starting transfers between devices, wide_swap(): return lax.ppermute(v, 'wide', [(i, i ^ bit) for i in range(count)])  25.3 us
    ppermute x21, waiting for transfers between devices, wide_swap(): return lax.ppermute(v, 'wide', [(i, i ^ bit) for i in range(count)])  16 us
    pallas_call x1, Pallas kernels, condition_back(): pl.pallas_call(functools.partial(condition_back_body, factor), name='cond...  14.5 us
    convert_element_type x21, other arithmetic, sum_pair(): return (a.astype(F32) + b.astype(F32)).astype(BF)  12.8 us
    ppermute x8, waiting for transfers between devices, x_swap(): return lax.ppermute(v, 'narrow', [(0, 2), (2, 0), (1, 3), (3, 1)])  10.9 us
    ppermute x8, starting transfers between devices, x_swap(): return lax.ppermute(v, 'narrow', [(0, 2), (2, 0), (1, 3), (3, 1)])  10.6 us
    pallas_call x1, Pallas kernels, condition(): pl.pallas_call(functools.partial(condition_body, steps), name='condition'...  8.82 us
  transfers between devices with their start and end apart: 43, of which 14 were waited for; matrix products, arithmetic and copies ran while one was open for 13% of the time, Pallas kernels for 49%

profile of v6, /device:TPU:0, one launch (start us, length us, event | category | flops | bytes accessed | tf_op | source)
XLA Modules:
  0.0 204.4 jit_solution(286210285600411782)
XLA Ops:
  1.2 2.6 %collective-permute-start.1 = (bf16[4,192,256]{2,1,0:T(8,128)(2,1)}, bf16[4,192,256]{2,1,0:T(8,128)(2,1)S(1)}, u32[]{:S(2)}, u32[]{:S(2)}) collective-permute-start(bf16[4,192,256]{2,1,0:T(8,128)(2,1)} %bitcast.84), channel_id=1, source_target_pairs={{0,2},{2,0},{1,3},{3,1},{4,6},{6,4},{5,7},{7,5},{8,10},{10,8},{9,1... | collective-permute-start | bytes 1179656 | tf_op jit(solution)/shard_map/ppermute | solution.py:874
  3.7 8.8 %condition.1 = (f32[4,6,768]{2,1,0:T(8,128)}, f32[32,256]{1,0:T(8,128)}, f32[32,768]{1,0:T(8,128)}, f32[32,768]{1,0:T(8,128)}, f32[32,768]{1,0:T(8,128)}, /*index=5*/f32[32,768]{1,0:T(8,128)}) custom-call(s32[32]{0:T(128)} %stamps.1, s32[1]{0:T(128)} %bitcast.2.wide, f32[36,128]{1,0:T(8,128)} %bitcast.91, f32[256,768]{1,0:T(8,128)} %time_in.1, ...), custom_call_target="tpu_custom_call" | custom-call | flops 8000000000 | bytes 1000000 | tf_op jit(solution)/shard_map/condition/pallas_call | solution.py:704
  13.7 1.8 collective-permute-start.3
  16.4 7.7 %attn_fwd.2 = (bf16[512,768]{1,0:T(8,128)(2,1)}, bf16[512,192]{1,0:T(8,128)(2,1)}, bf16[512,192]{1,0:T(8,128)(2,1)}, bf16[512,192]{1,0:T(8,128)(2,1)}, bf16[256,...) custom-call(s32[1]{0:T(128)} %bitcast.s_ref, ...), custom_call_target="tpu_custom_call" | custom-call | flops 6000000000 | bytes 1000000 | tf_op jit(solution)/shard_map/attn_fwd/pallas_call | solution.py:567
  27.2 1.6 collective-permute-start.6
  28.8 7.7 %attn_fwd.3 = (bf16[512,768]{1,0:T(8,128)(2,1)}, bf16[512,192]{1,0:T(8,128)(2,1)}, bf16[512,192]{1,0:T(8,128)(2,1)}, bf16[512,192]{1,0:T(8,128)(2,1)}, bf16[256,...) custom-call(s32[1]{0:T(128)} %bitcast.s_ref, ...), custom_call_target="tpu_custom_call", output_to_operand_aliasing={{6}: (9, {}), {7}: (10, {})} | custom-call | flops 6000000000 | bytes 1000000 | tf_op jit(solution)/shard_map/attn_fwd/pallas_call | solution.py:567
  36.6 1.8 collective-permute-done.6
  39.8 1.6 collective-permute-start.7
  43.1 14.5 %ffn.2 = (bf16[512,768]{1,0:T(8,128)(2,1)}, bf16[256,768]{1,0:T(8,128)(2,1)}, bf16[256,768]{1,0:T(8,128)(2,1)}, f32[2,1,768]{2,1,0:T(1,128)}, f32[16,768]{1,0:T(...) custom-call(s32[1]{0:T(128)} %bitcast.s_ref, ...), custom_call_target="tpu_custom_call" | custom-call | flops 10000000000 | bytes 1000000 | tf_op jit(solution)/shard_map/ffn/pallas_call | solution.py:567
  58.4 1.2 collective-permute-done.12
  62.1 14.8 %ffn.3 = (bf16[512,768]{1,0:T(8,128)(2,1)}, bf16[256,768]{1,0:T(8,128)(2,1)}, bf16[256,768]{1,0:T(8,128)(2,1)}, f32[2,1,768]{2,1,0:T(1,128)}, f32[16,768]{1,0:T(...) custom-call(s32[1]{0:T(128)} %bitcast.s_ref, ...), custom_call_target="tpu_custom_call", output_to_operand_aliasing={{7}: (13, {}), {8}: (14, {}), {9}: (15, {}), {10}: (16, {})} | custom-call | flops 10000000000 | bytes 1000000 | tf_op jit(solution)/shard_map/ffn/pallas_call | solution.py:567
  80.3 1.6 collective-permute-start.18
  82.0 1.6 collective-permute-start.15
  83.6 1.5 multiply_convert_fusion
  85.9 7.8 %attn_bwd.2 = (bf16[512,768]{1,0:T(8,128)(2,1)}, f32[2,8,768]{2,1,0:T(8,128)}, bf16[1024,768]{1,0:T(8,128)(2,1)}, bf16[1024,576]{1,0:T(8,128)(2,1)}) custom-call(s32[1]{0:T(128)} %bitcast.s_ref, bf16[512,768]{1,0:T(8,128)(2,1)} %get-tuple-element.211.refs_4_.refs_0_, bf16[256,768]{1,0:T(8,128)(2,1)} %copy-done.7, bf16[256,768]{1,0:T(8,128)(2,1)} %copy-done.15, ...), custom_call_target="tpu_custom_call" | custom-call | flops 6000000000 | bytes 1000000 | tf_op jit(solution)/shard_map/attn_bwd/pallas_call | solution.py:567
  93.8 1.9 add_convert_fusion.3.refs_3_
  96.1 1.3 add_convert_fusion.15
  97.4 1.6 collective-permute-start.19
  99.1 8.1 %attn_bwd.3 = (bf16[512,768]{1,0:T(8,128)(2,1)}, f32[2,8,768]{2,1,0:T(8,128)}, bf16[1024,768]{1,0:T(8,128)(2,1)}, bf16[1024,576]{1,0:T(8,128)(2,1)}) custom-call(s32[1]{0:T(128)} %bitcast.s_ref, bf16[512,768]{1,0:T(8,128)(2,1)} %get-tuple-element.220.refs_4_.refs_0_, bf16[256,768]{1,0:T(8,128)(2,1)} %copy-done.6, ...), custom_call_target="tpu_custom_call", output_to_operand_aliasing={{2}: (13, {}), {3}: (14, {})} | custom-call | flops 6000000000 | bytes 1000000 | tf_op jit(solution)/shard_map/attn_bwd/pallas_call | solution.py:567
  107.3 2.7 %collective-permute-start.21 = (bf16[96,768]{1,0:T(8,128)(2,1)S(1)}, bf16[96,768]{1,0:T(8,128)(2,1)S(1)}, u32[]{:S(2)}, u32[]{:S(2)}) collective-permute-start(bf16[96,768]{1,0:T(8,128)(2,1)S(1)} %get-tuple-element.399), channel_id=1, source_target_pairs={{0,16},{4,20},{8,24},{12,28},{16,0},{20,4},{24,8},{28,12},{1,17},{... | collective-permute-start | bytes 442376 | tf_op jit(solution)/shard_map/ppermute | solution.py:890
  109.9 1.9 fusion
  111.9 1.1 multiply_convert_fusion.2
  113.2 1.6 collective-permute-start.20
  114.8 2.0 add_convert_fusion.13
  118.4 8.2 %input_bwd.2 = (f32[16,768]{1,0:T(8,128)}, f32[2,8,768]{2,1,0:T(8,128)}, bf16[2,8,192,256]{3,2,1,0:T(8,128)(2,1)}, bf16[2,8,192,256]{3,2,1,0:T(8,128)(2,1)}) custom-call(s32[1]{0:T(128)} %bitcast.s_ref, bf16[512,768]{1,0:T(8,128)(2,1)} %get-tuple-element.211.refs_4_.refs_0_, ...), custom_call_target="tpu_custom_call", output_to_operand_aliasing={{2}: (10, {}), {3}: (11, {})} | custom-call | flops 6000000000 | bytes 1000000 | tf_op jit(solution)/shard_map/input_bwd/pallas_call | solution.py:567
  126.7 1.7 collective-permute-done.24
  129.8 1.1 collective-permute-start.28
  130.9 1.3 add_convert_fusion.11
  132.2 1.9 collective-permute-start.32
  134.1 8.3 %input_bwd.3 = (f32[16,768]{1,0:T(8,128)}, bf16[40,768]{1,0:T(8,128)(2,1)}, bf16[2,8,192,256]{3,2,1,0:T(8,128)(2,1)}, bf16[2,8,192,256]{3,2,1,0:T(8,128)(2,1)}) custom-call(s32[1]{0:T(128)} %bitcast.s_ref, bf16[512,768]{1,0:T(8,128)(2,1)} %get-tuple-element.220.refs_4_.refs_0_, ...), custom_call_target="tpu_custom_call", output_to_operand_aliasing={{2}: (10, {}), {3}: (11, {})} | custom-call | flops 6000000000 | bytes 1000000 | tf_op jit(solution)/shard_map/input_bwd/pallas_call | solution.py:567
  143.8 1.5 collective-permute-start.29
  146.8 1.6 collective-permute-start.34
  148.5 2.1 %collective-permute-done.31 = bf16[40,768]{1,0:T(8,128)(2,1)S(1)} collective-permute-done((bf16[40,768]{1,0:T(8,128)(2,1)S(1)}, bf16[40,768]{1,0:T(8,128)(2,1)S(1)}, u32[]{:S(2)}, u32[]{:S(2)}) %collective-permute-start.31) | collective-permute-done | bytes 61472 | tf_op jit(solution)/shard_map/ppermute | solution.py:874
  150.6 1.5 collective-permute-start.35
  152.2 6.5 %collective-permute-done.29 = bf16[1,1,1,96,768]{4,3,2,1,0:T(8,128)(2,1)S(1)} collective-permute-done((bf16[1,1,1,96,768]{4,3,2,1,0:T(8,128)(2,1)S(1)}, bf16[1,1,1,96,768]{4,3,2,1,0:T(8,128)(2,1)S(1)}, u32[]{:S(2)}, u32[]{:S(2)}) %collective-permute-start.29) | collective-permute-done | bytes 147488 | tf_op jit(solution)/shard_map/ppermute | solution.py:890
  158.8 1.6 select_convert_fusion.1
  161.9 1.2 collective-permute-done.35
  163.1 1.2 collective-permute-start.38
  164.3 1.2 collective-permute-start.36
  165.5 3.1 %collective-permute-done.38 = bf16[1,1,1,96,768]{4,3,2,1,0:T(8,128)(2,1)S(1)} collective-permute-done((bf16[1,1,1,96,768]{4,3,2,1,0:T(8,128)(2,1)S(1)}, bf16[1,1,1,96,768]{4,3,2,1,0:T(8,128)(2,1)S(1)}, u32[]{:S(2)}, u32[]{:S(2)}) %collective-permute-start.38) | collective-permute-done | bytes 147488 | tf_op jit(solution)/shard_map/ppermute | solution.py:890
  168.7 1.6 collective-permute-start.40
  170.3 2.3 %collective-permute-done.36 = bf16[2,42,768]{2,1,0:T(8,128)(2,1)S(1)} collective-permute-done((bf16[2,42,768]{2,1,0:T(8,128)(2,1)S(1)}, bf16[2,42,768]{2,1,0:T(8,128)(2,1)S(1)}, u32[]{:S(2)}, u32[]{:S(2)}) %collective-permute-start.36) | collective-permute-done | bytes 129056 | tf_op jit(solution)/shard_map/ppermute | solution.py:890
  172.6 1.1 collective-permute-start.39
  174.9 5.4 %collective-permute-done.33 = bf16[8,192,256]{2,1,0:T(8,128)(2,1)S(1)} collective-permute-done((bf16[8,192,256]{2,1,0:T(8,128)(2,1)S(1)}, bf16[8,192,256]{2,1,0:T(8,128)(2,1)S(1)}, u32[]{:S(2)}, u32[]{:S(2)}) %collective-permute-start.33) | collective-permute-done | bytes 786464 | tf_op jit(solution)/shard_map/ppermute | solution.py:874
  181.4 1.2 collective-permute-done.39
  184.4 14.5 %condition_back.1 = (f32[256,768]{1,0:T(8,128)}, f32[768,768]{1,0:T(8,128)}, f32[768,4608]{1,0:T(8,128)}) custom-call(bf16[32,4608]{1,0:T(8,128)(2,1)} %reshape.116.gmod, f32[32,256]{1,0:T(8,128)} %get-tuple-element.372.embedded, f32[32,768]{1,0:T(8,128)} %get-tuple-element.373.inner_pre, f32[32,768]{1,0:T(8,128)} %get-tuple-element.374.inner, ...), custom_call_target="tpu_custom_call" | custom-call | flops 1 | bytes 1 | tf_op jit(solution)/shard_map/condition_back/pallas_call | solution.py:773
  199.0 1.6 select_convert_fusion
  203.1 1.4 convert_bitcast_fusion
  (162 shorter events, 31.2 us)
Async XLA Ops:
  0.6 14.8 %collective-permute-start = (bf16[4,192,256]{2,1,0:T(8,128)(2,1)}, bf16[4,192,256]{2,1,0:T(8,128)(2,1)S(1)}, u32[]{:S(2)}, u32[]{:S(2)}) collective-permute-start(bf16[4,192,256]{2,1,0:T(8,128)(2,1)} %bitcast.83), channel_id=1, source_target_pairs={{0,1},{1,0},{2,3},{3,2},{4,5},{5,4},{6,7},{7,6},{8,9},{9,8},{10,11... | collective-permute-start | bytes 1179656 | tf_op jit(solution)/shard_map/ppermute | solution.py:870
  1.2 12.5 %collective-permute-start.1 = (bf16[4,192,256]{2,1,0:T(8,128)(2,1)}, bf16[4,192,256]{2,1,0:T(8,128)(2,1)S(1)}, u32[]{:S(2)}, u32[]{:S(2)}) collective-permute-start(bf16[4,192,256]{2,1,0:T(8,128)(2,1)} %bitcast.84), channel_id=1, source_target_pairs={{0,2},{2,0},{1,3},{3,1},{4,6},{6,4},{5,7},{7,5},{8,10},{10,8},{9,1... | collective-permute-start | bytes 1179656 | tf_op jit(solution)/shard_map/ppermute | solution.py:874
  3.7 9.9 %copy-start.12 = (bf16[4,256,192]{1,2,0:T(8,128)(2,1)S(1)}, bf16[4,256,192]{1,2,0:T(8,128)(2,1)}, u32[]{:S(2)}) copy-start(bf16[4,256,192]{1,2,0:T(8,128)(2,1)} %param.14) | copy-start | bytes 1179652
  13.6 1.8 collective-permute-start.2
  13.7 11.5 %collective-permute-start.3 = (bf16[4,192,256]{2,1,0:T(8,128)(2,1)S(1)}, bf16[4,192,256]{2,1,0:T(8,128)(2,1)S(1)}, u32[]{:S(2)}, u32[]{:S(2)}) collective-permute-start(bf16[4,192,256]{2,1,0:T(8,128)(2,1)S(1)} %bitcast.89), channel_id=1, source_target_pairs={{0,2},{2,0},{1,3},{3,1},{4,6},{6,4},{5,7},{7,5},{8,10},{10,8},{9,1... | collective-permute-start | bytes 1179656 | tf_op jit(solution)/shard_map/ppermute | solution.py:874
  24.1 2.0 collective-permute-start.4
  24.3 17.0 %collective-permute-start.9 = (bf16[4,192,256]{2,1,0:T(8,128)(2,1)S(1)}, bf16[4,192,256]{2,1,0:T(8,128)(2,1)S(1)}, u32[]{:S(2)}, u32[]{:S(2)}) collective-permute-start(bf16[4,192,256]{2,1,0:T(8,128)(2,1)S(1)} %bitcast.90), channel_id=1, source_target_pairs={{0,1},{1,0},{2,3},{3,2},{4,5},{5,4},{6,7},{7,6},{8,9},{9,8},{10,11... | collective-permute-start | bytes 1179656 | tf_op jit(solution)/shard_map/ppermute | solution.py:870
  25.2 11.3 %copy-start.14 = (bf16[4,192,256]{2,1,0:T(8,128)(2,1)}, bf16[4,192,256]{2,1,0:T(8,128)(2,1)S(1)}, u32[]{:S(2)}) copy-start(bf16[4,192,256]{2,1,0:T(8,128)(2,1)S(1)} %collective-permute-done.3.refs_2_) | copy-start | bytes 1179652
  25.2 16.2 %collective-permute-start.10 = (bf16[4,192,256]{2,1,0:T(8,128)(2,1)S(1)}, bf16[4,192,256]{2,1,0:T(8,128)(2,1)S(1)}, u32[]{:S(2)}, u32[]{:S(2)}) collective-permute-start(bf16[4,192,256]{2,1,0:T(8,128)(2,1)S(1)} %collective-permute-done.3.refs_2_), channel_id=1, source_target_pairs={{0,1},{1,0},{2,3},{3,2},{4,5},{5,4},{6,7},{7,6},{8,9},{9,8},{10,11... | collective-permute-start | bytes 1179656 | tf_op jit(solution)/shard_map/ppermute | solution.py:870
  27.2 11.2 %collective-permute-start.6 = (bf16[256,768]{1,0:T(8,128)(2,1)S(1)}, bf16[256,768]{1,0:T(8,128)(2,1)S(1)}, u32[]{:S(2)}, u32[]{:S(2)}) collective-permute-start(bf16[256,768]{1,0:T(8,128)(2,1)S(1)} %add_convert_fusion.10), channel_id=1, source_target_pairs={{0,2},{2,0},{1,3},{3,1},{4,6},{6,4},{5,7},{7,5},{8,10},{10,8},{9,1... | collective-permute-start | bytes 1179656 | tf_op jit(solution)/shard_map/ppermute | solution.py:874
  36.5 2.1 %collective-permute-start.5 = (bf16[256,768]{1,0:T(8,128)(2,1)}, bf16[256,768]{1,0:T(8,128)(2,1)S(1)}, u32[]{:S(2)}, u32[]{:S(2)}) collective-permute-start(bf16[256,768]{1,0:T(8,128)(2,1)} %get-tuple-element.222), channel_id=1, source_target_pairs={{0,1},{1,0},{2,3},{3,2},{4,5},{5,4},{6,7},{7,6},{8,9},{9,8},{10,11... | collective-permute-start | bytes 1179656 | tf_op jit(solution)/shard_map/ppermute | solution.py:870
  38.6 2.8 %collective-permute-start.8 = (bf16[256,768]{1,0:T(8,128)(2,1)S(1)}, bf16[256,768]{1,0:T(8,128)(2,1)S(1)}, u32[]{:S(2)}, u32[]{:S(2)}) collective-permute-start(bf16[256,768]{1,0:T(8,128)(2,1)S(1)} %add_convert_fusion.9.refs_5_.refs_1_), channel_id=1, source_target_pairs={{0,1},{1,0},{2,3},{3,2},{4,5},{5,4},{6,7},{7,6},{8,9},{9,8},{10,11... | collective-permute-start | bytes 1179656 | tf_op jit(solution)/shard_map/ppermute | solution.py:870
  39.8 18.0 %collective-permute-start.7 = (bf16[256,768]{1,0:T(8,128)(2,1)S(1)}, bf16[256,768]{1,0:T(8,128)(2,1)S(1)}, u32[]{:S(2)}, u32[]{:S(2)}) collective-permute-start(bf16[256,768]{1,0:T(8,128)(2,1)S(1)} %add_convert_fusion.8), channel_id=1, source_target_pairs={{0,2},{2,0},{1,3},{3,1},{4,6},{6,4},{5,7},{7,5},{8,10},{10,8},{9,1... | collective-permute-start | bytes 1179656 | tf_op jit(solution)/shard_map/ppermute | solution.py:874
  57.6 2.0 collective-permute-start.12
  57.9 3.4 %collective-permute-start.11 = (bf16[256,768]{1,0:T(8,128)(2,1)S(1)}, bf16[256,768]{1,0:T(8,128)(2,1)S(1)}, u32[]{:S(2)}, u32[]{:S(2)}) collective-permute-start(bf16[256,768]{1,0:T(8,128)(2,1)S(1)} %add_convert_fusion.7.refs_5_.refs_1_), channel_id=1, source_target_pairs={{0,1},{1,0},{2,3},{3,2},{4,5},{5,4},{6,7},{7,6},{8,9},{9,8},{10,11... | collective-permute-start | bytes 1179656 | tf_op jit(solution)/shard_map/ppermute | solution.py:870
  60.7 16.3 %collective-permute-start.14 = (bf16[256,768]{1,0:T(8,128)(2,1)S(1)}, bf16[256,768]{1,0:T(8,128)(2,1)S(1)}, u32[]{:S(2)}, u32[]{:S(2)}) collective-permute-start(bf16[256,768]{1,0:T(8,128)(2,1)S(1)} %add_convert_fusion.6), channel_id=1, source_target_pairs={{0,2},{2,0},{1,3},{3,1},{4,6},{6,4},{5,7},{7,5},{8,10},{10,8},{9,1... | collective-permute-start | bytes 1179656 | tf_op jit(solution)/shard_map/ppermute | solution.py:874
  62.1 15.6 %copy-start.5 = (bf16[512,768]{1,0:T(8,128)(2,1)S(1)}, bf16[512,768]{1,0:T(8,128)(2,1)}, u32[]{:S(2)}) copy-start(bf16[512,768]{1,0:T(8,128)(2,1)} %get-tuple-element.261) | copy-start | bytes 2359300
  76.9 5.0 %collective-permute-start.13 = (bf16[256,768]{1,0:T(8,128)(2,1)}, bf16[256,768]{1,0:T(8,128)(2,1)S(1)}, u32[]{:S(2)}, u32[]{:S(2)}) collective-permute-start(bf16[256,768]{1,0:T(8,128)(2,1)} %get-tuple-element.252), channel_id=1, source_target_pairs={{0,1},{1,0},{2,3},{3,2},{4,5},{5,4},{6,7},{7,6},{8,9},{9,8},{10,11... | collective-permute-start | bytes 1179656 | tf_op jit(solution)/shard_map/ppermute | solution.py:870
  77.1 8.1 %collective-permute-start.16 = (bf16[256,768]{1,0:T(8,128)(2,1)S(1)}, bf16[256,768]{1,0:T(8,128)(2,1)S(1)}, u32[]{:S(2)}, u32[]{:S(2)}) collective-permute-start(bf16[256,768]{1,0:T(8,128)(2,1)S(1)} %add_convert_fusion.5.refs_3_), channel_id=1, source_target_pairs={{0,1},{1,0},{2,3},{3,2},{4,5},{5,4},{6,7},{7,6},{8,9},{9,8},{10,11... | collective-permute-start | bytes 1179656 | tf_op jit(solution)/shard_map/ppermute | solution.py:870
  80.3 15.8 %collective-permute-start.18 = (bf16[384,768]{1,0:T(8,128)(2,1)S(1)}, bf16[384,768]{1,0:T(8,128)(2,1)}, u32[]{:S(2)}, u32[]{:S(2)}) collective-permute-start(bf16[384,768]{1,0:T(8,128)(2,1)S(1)} %constant_dynamic-slice_fusion.2), channel_id=1, source_target_pairs={{0,4},{4,0},{8,12},{12,8},{16,20},{20,16},{24,28},{28,24},{1,5},{5... | collective-permute-start | bytes 1769480 | tf_op jit(solution)/shard_map/ppermute | solution.py:890
  82.0 11.7 %collective-permute-start.15 = (bf16[256,768]{1,0:T(8,128)(2,1)S(1)}, bf16[256,768]{1,0:T(8,128)(2,1)}, u32[]{:S(2)}, u32[]{:S(2)}) collective-permute-start(bf16[256,768]{1,0:T(8,128)(2,1)S(1)} %add_convert_fusion.4), channel_id=1, source_target_pairs={{0,2},{2,0},{1,3},{3,1},{4,6},{6,4},{5,7},{7,5},{8,10},{10,8},{9,1... | collective-permute-start | bytes 1179656 | tf_op jit(solution)/shard_map/ppermute | solution.py:874
  95.6 3.4 %collective-permute-start.17 = (bf16[256,768]{1,0:T(8,128)(2,1)}, bf16[256,768]{1,0:T(8,128)(2,1)}, u32[]{:S(2)}, u32[]{:S(2)}) collective-permute-start(bf16[256,768]{1,0:T(8,128)(2,1)} %add_convert_fusion.3.refs_3_), channel_id=1, source_target_pairs={{0,1},{1,0},{2,3},{3,2},{4,5},{5,4},{6,7},{7,6},{8,9},{9,8},{10,11... | collective-permute-start | bytes 1179656 | tf_op jit(solution)/shard_map/ppermute | solution.py:870
  95.6 19.1 %collective-permute-start.22 = (bf16[384,768]{1,0:T(8,128)(2,1)S(1)}, bf16[384,768]{1,0:T(8,128)(2,1)}, u32[]{:S(2)}, u32[]{:S(2)}) collective-permute-start(bf16[384,768]{1,0:T(8,128)(2,1)S(1)} %constant_dynamic-slice_fusion.1), channel_id=1, source_target_pairs={{0,4},{4,0},{8,12},{12,8},{16,20},{20,16},{24,28},{28,24},{1,5},{5... | collective-permute-start | bytes 1769480 | tf_op jit(solution)/shard_map/ppermute | solution.py:890
  97.4 9.7 %collective-permute-start.19 = (bf16[192,768]{1,0:T(8,128)(2,1)S(1)}, bf16[192,768]{1,0:T(8,128)(2,1)S(1)}, u32[]{:S(2)}, u32[]{:S(2)}) collective-permute-start(bf16[192,768]{1,0:T(8,128)(2,1)S(1)} %get-tuple-element.389), channel_id=1, source_target_pairs={{0,8},{4,12},{8,0},{12,4},{16,24},{20,28},{24,16},{28,20},{1,9},{5... | collective-permute-start | bytes 884744 | tf_op jit(solution)/shard_map/ppermute | solution.py:890
  99.1 10.9 %copy-start.22 = (bf16[1024,192]{1,0:T(8,128)(2,1)S(1)}, bf16[1024,192]{1,0:T(8,128)(2,1)}, u32[]{:S(2)}) copy-start(bf16[1024,192]{1,0:T(8,128)(2,1)} %get-tuple-element.305) | copy-start | bytes 1179652
  107.3 10.5 %collective-permute-start.21 = (bf16[96,768]{1,0:T(8,128)(2,1)S(1)}, bf16[96,768]{1,0:T(8,128)(2,1)S(1)}, u32[]{:S(2)}, u32[]{:S(2)}) collective-permute-start(bf16[96,768]{1,0:T(8,128)(2,1)S(1)} %get-tuple-element.399), channel_id=1, source_target_pairs={{0,16},{4,20},{8,24},{12,28},{16,0},{20,4},{24,8},{28,12},{1,17},{... | collective-permute-start | bytes 442376 | tf_op jit(solution)/shard_map/ppermute | solution.py:890
  113.2 17.8 %collective-permute-start.20 = (bf16[384,768]{1,0:T(8,128)(2,1)S(1)}, bf16[384,768]{1,0:T(8,128)(2,1)}, u32[]{:S(2)}, u32[]{:S(2)}) collective-permute-start(bf16[384,768]{1,0:T(8,128)(2,1)S(1)} %constant_dynamic-slice_fusion), channel_id=1, source_target_pairs={{0,4},{4,0},{8,12},{12,8},{16,20},{20,16},{24,28},{28,24},{1,5},{5... | collective-permute-start | bytes 1769480 | tf_op jit(solution)/shard_map/ppermute | solution.py:890
  116.7 11.7 %collective-permute-start.24 = (bf16[192,768]{1,0:T(8,128)(2,1)}, bf16[192,768]{1,0:T(8,128)(2,1)S(1)}, u32[]{:S(2)}, u32[]{:S(2)}) collective-permute-start(bf16[192,768]{1,0:T(8,128)(2,1)} %get-tuple-element.387), channel_id=1, source_target_pairs={{0,8},{4,12},{8,0},{12,4},{16,24},{20,28},{24,16},{28,20},{1,9},{5... | collective-permute-start | bytes 884744 | tf_op jit(solution)/shard_map/ppermute | solution.py:890
  117.8 8.9 %collective-permute-start.23 = (bf16[1,1,1,96,768]{4,3,2,1,0:T(8,128)(2,1)S(1)}, bf16[1,1,1,96,768]{4,3,2,1,0:T(8,128)(2,1)S(1)}, u32[]{:S(2)}, u32[]{:S(2)}) collective-permute-start(bf16[1,1,1,96,768]{4,3,2,1,0:T(8,128)(2,1)S(1)} %bitcast.67), channel_id=1, source_target_pairs={{0,16},{4,20},{8,24},{12,28},{16,0},{20,4},{24,8},{28,12},{1,17},{... | collective-permute-start | bytes 442376 | tf_op jit(solution)/shard_map/ppermute | solution.py:890
  128.5 14.6 %collective-permute-start.26 = (bf16[1,1,2,96,768]{4,3,2,1,0:T(8,128)(2,1)S(1)}, bf16[1,1,2,96,768]{4,3,2,1,0:T(8,128)(2,1)S(1)}, u32[]{:S(2)}, u32[]{:S(2)}) collective-permute-start(bf16[1,1,2,96,768]{4,3,2,1,0:T(8,128)(2,1)S(1)} %broadcast_select_fusion.6), channel_id=1, source_target_pairs={{0,8},{4,12},{8,0},{12,4},{16,24},{20,28},{24,16},{28,20},{1,9},{5... | collective-permute-start | bytes 884744 | tf_op jit(solution)/shard_map/ppermute | solution.py:890
  129.8 14.0 %collective-permute-start.28 = (bf16[96,768]{1,0:T(8,128)(2,1)}, bf16[96,768]{1,0:T(8,128)(2,1)S(1)}, u32[]{:S(2)}, u32[]{:S(2)}) collective-permute-start(bf16[96,768]{1,0:T(8,128)(2,1)} %get-tuple-element.397), channel_id=1, source_target_pairs={{0,16},{4,20},{8,24},{12,28},{16,0},{20,4},{24,8},{28,12},{1,17},{... | collective-permute-start | bytes 442376 | tf_op jit(solution)/shard_map/ppermute | solution.py:890
  132.2 14.6 %collective-permute-start.32 = (bf16[192,768]{1,0:T(8,128)(2,1)S(1)}, bf16[192,768]{1,0:T(8,128)(2,1)S(1)}, u32[]{:S(2)}, u32[]{:S(2)}) collective-permute-start(bf16[192,768]{1,0:T(8,128)(2,1)S(1)} %get-tuple-element.385), channel_id=1, source_target_pairs={{0,8},{4,12},{8,0},{12,4},{16,24},{20,28},{24,16},{28,20},{1,9},{5... | collective-permute-start | bytes 884744 | tf_op jit(solution)/shard_map/ppermute | solution.py:890
  142.5 18.0 %collective-permute-start.25 = (bf16[2,8,192,256]{3,2,1,0:T(8,128)(2,1)}, bf16[2,8,192,256]{3,2,1,0:T(8,128)(2,1)S(1)}, u32[]{:S(2)}, u32[]{:S(2)}) collective-permute-start(bf16[2,8,192,256]{3,2,1,0:T(8,128)(2,1)} %get-tuple-element.333), channel_id=1, source_target_pairs={{0,1},{1,0},{2,3},{3,2},{4,5},{5,4},{6,7},{7,6},{8,9},{9,8},{10,11... | collective-permute-start | bytes 4718600 | tf_op jit(solution)/shard_map/ppermute | solution.py:870
  142.6 3.7 %collective-permute-start.30 = (bf16[40,768]{1,0:T(8,128)(2,1)}, bf16[40,768]{1,0:T(8,128)(2,1)S(1)}, u32[]{:S(2)}, u32[]{:S(2)}) collective-permute-start(bf16[40,768]{1,0:T(8,128)(2,1)} %get-tuple-element.341), channel_id=1, source_target_pairs={{0,1},{1,0},{2,3},{3,2},{4,5},{5,4},{6,7},{7,6},{8,9},{9,8},{10,11... | collective-permute-start | bytes 184328 | tf_op jit(solution)/shard_map/ppermute | solution.py:870
  143.2 15.6 %collective-permute-start.27 = (bf16[1,2,2,96,768]{4,3,2,1,0:T(8,128)(2,1)S(1)}, bf16[1,2,2,96,768]{4,3,2,1,0:T(8,128)(2,1)S(1)}, u32[]{:S(2)}, u32[]{:S(2)}) collective-permute-start(bf16[1,2,2,96,768]{4,3,2,1,0:T(8,128)(2,1)S(1)} %broadcast_select_fusion.3), channel_id=1, source_target_pairs={{0,4},{4,0},{8,12},{12,8},{16,20},{20,16},{24,28},{28,24},{1,5},{5... | collective-permute-start | bytes 1769480 | tf_op jit(solution)/shard_map/ppermute | solution.py:890
  143.8 14.8 %collective-permute-start.29 = (bf16[1,1,1,96,768]{4,3,2,1,0:T(8,128)(2,1)S(1)}, bf16[1,1,1,96,768]{4,3,2,1,0:T(8,128)(2,1)S(1)}, u32[]{:S(2)}, u32[]{:S(2)}) collective-permute-start(bf16[1,1,1,96,768]{4,3,2,1,0:T(8,128)(2,1)S(1)} %bitcast.66), channel_id=1, source_target_pairs={{0,16},{4,20},{8,24},{12,28},{16,0},{20,4},{24,8},{28,12},{1,17},{... | collective-permute-start | bytes 442376 | tf_op jit(solution)/shard_map/ppermute | solution.py:890
  146.3 4.3 %collective-permute-start.31 = (bf16[40,768]{1,0:T(8,128)(2,1)S(1)}, bf16[40,768]{1,0:T(8,128)(2,1)S(1)}, u32[]{:S(2)}, u32[]{:S(2)}) collective-permute-start(bf16[40,768]{1,0:T(8,128)(2,1)S(1)} %add_convert_fusion.27), channel_id=1, source_target_pairs={{0,2},{2,0},{1,3},{3,1},{4,6},{6,4},{5,7},{7,5},{8,10},{10,8},{9,1... | collective-permute-start | bytes 184328 | tf_op jit(solution)/shard_map/ppermute | solution.py:874
  146.8 16.2 %collective-permute-start.34 = (bf16[96,768]{1,0:T(8,128)(2,1)S(1)}, bf16[96,768]{1,0:T(8,128)(2,1)S(1)}, u32[]{:S(2)}, u32[]{:S(2)}) collective-permute-start(bf16[96,768]{1,0:T(8,128)(2,1)S(1)} %get-tuple-element.395), channel_id=1, source_target_pairs={{0,16},{4,20},{8,24},{12,28},{16,0},{20,4},{24,8},{28,12},{1,17},{... | collective-permute-start | bytes 442376 | tf_op jit(solution)/shard_map/ppermute | solution.py:890
  150.6 12.4 %collective-permute-start.35 = (bf16[1,42,768]{2,1,0:T(8,128)(2,1)S(1)}, bf16[1,42,768]{2,1,0:T(8,128)(2,1)S(1)}, u32[]{:S(2)}, u32[]{:S(2)}) collective-permute-start(bf16[1,42,768]{2,1,0:T(8,128)(2,1)S(1)} %maximum_bitcast_fusion), channel_id=1, source_target_pairs={{0,16},{4,20},{8,24},{12,28},{16,0},{20,4},{24,8},{28,12},{1,17},{... | collective-permute-start | bytes 193544 | tf_op jit(solution)/shard_map/ppermute | solution.py:890
  158.7 11.5 %collective-permute-start.37 = (bf16[1,1,2,96,768]{4,3,2,1,0:T(8,128)(2,1)S(1)}, bf16[1,1,2,96,768]{4,3,2,1,0:T(8,128)(2,1)S(1)}, u32[]{:S(2)}, u32[]{:S(2)}) collective-permute-start(bf16[1,1,2,96,768]{4,3,2,1,0:T(8,128)(2,1)S(1)} %broadcast_select_fusion.5), channel_id=1, source_target_pairs={{0,8},{4,12},{8,0},{12,4},{16,24},{20,28},{24,16},{28,20},{1,9},{5... | collective-permute-start | bytes 884744 | tf_op jit(solution)/shard_map/ppermute | solution.py:890
  161.4 18.8 %collective-permute-start.33 = (bf16[8,192,256]{2,1,0:T(8,128)(2,1)S(1)}, bf16[8,192,256]{2,1,0:T(8,128)(2,1)S(1)}, u32[]{:S(2)}, u32[]{:S(2)}) collective-permute-start(bf16[8,192,256]{2,1,0:T(8,128)(2,1)S(1)} %get-tuple-element.392), channel_id=1, source_target_pairs={{0,2},{2,0},{1,3},{3,1},{4,6},{6,4},{5,7},{7,5},{8,10},{10,8},{9,1... | collective-permute-start | bytes 2359304 | tf_op jit(solution)/shard_map/ppermute | solution.py:874
  163.1 5.5 %collective-permute-start.38 = (bf16[1,1,1,96,768]{4,3,2,1,0:T(8,128)(2,1)S(1)}, bf16[1,1,1,96,768]{4,3,2,1,0:T(8,128)(2,1)S(1)}, u32[]{:S(2)}, u32[]{:S(2)}) collective-permute-start(bf16[1,1,1,96,768]{4,3,2,1,0:T(8,128)(2,1)S(1)} %bitcast.68), channel_id=1, source_target_pairs={{0,4},{4,0},{8,12},{12,8},{16,20},{20,16},{24,28},{28,24},{1,5},{5... | collective-permute-start | bytes 442376 | tf_op jit(solution)/shard_map/ppermute | solution.py:890
  164.3 8.2 %collective-permute-start.36 = (bf16[2,42,768]{2,1,0:T(8,128)(2,1)S(1)}, bf16[2,42,768]{2,1,0:T(8,128)(2,1)S(1)}, u32[]{:S(2)}, u32[]{:S(2)}) collective-permute-start(bf16[2,42,768]{2,1,0:T(8,128)(2,1)S(1)} %constant_dynamic-update-slice_fusion), channel_id=1, source_target_pairs={{0,8},{4,12},{8,0},{12,4},{16,24},{20,28},{24,16},{28,20},{1,9},{5... | collective-permute-start | bytes 387080 | tf_op jit(solution)/shard_map/ppermute | solution.py:890
  168.7 15.0 %collective-permute-start.40 = (bf16[2,1,1,96,768]{4,3,0,2,1:T(8,128)(2,1)S(1)}, bf16[2,1,1,96,768]{4,3,0,2,1:T(8,128)(2,1)S(1)}, u32[]{:S(2)}, u32[]{:S(2)}) collective-permute-start(bf16[2,1,1,96,768]{4,3,0,2,1:T(8,128)(2,1)S(1)} %broadcast_select_fusion.4), channel_id=1, source_target_pairs={{0,16},{4,20},{8,24},{12,28},{16,0},{20,4},{24,8},{28,12},{1,17},{... | collective-permute-start | bytes 884744 | tf_op jit(solution)/shard_map/ppermute | solution.py:890
  172.6 9.9 %collective-permute-start.39 = (bf16[4,42,768]{2,1,0:T(8,128)(2,1)S(1)}, bf16[4,42,768]{2,1,0:T(8,128)(2,1)S(1)}, u32[]{:S(2)}, u32[]{:S(2)}) collective-permute-start(bf16[4,42,768]{2,1,0:T(8,128)(2,1)S(1)} %constant_dynamic-update-slice_fusion.2), channel_id=1, source_target_pairs={{0,4},{4,0},{8,12},{12,8},{16,20},{20,16},{24,28},{28,24},{1,5},{5... | collective-permute-start | bytes 774152 | tf_op jit(solution)/shard_map/ppermute | solution.py:890
  173.9 25.1 %collective-permute-start.42 = (bf16[1,2,2,96,768]{4,3,2,1,0:T(8,128)(2,1)S(1)}, bf16[1,2,2,96,768]{4,3,2,1,0:T(8,128)(2,1)S(1)}, u32[]{:S(2)}, u32[]{:S(2)}) collective-permute-start(bf16[1,2,2,96,768]{4,3,2,1,0:T(8,128)(2,1)S(1)} %broadcast_select_fusion.2), channel_id=1, source_target_pairs={{0,4},{4,0},{8,12},{12,8},{16,20},{20,16},{24,28},{28,24},{1,5},{5... | collective-permute-start | bytes 1769480 | tf_op jit(solution)/shard_map/ppermute | solution.py:890
  183.8 18.2 %collective-permute-start.41 = (bf16[2,1,2,96,768]{4,3,2,0,1:T(8,128)(2,1)S(1)}, bf16[2,1,2,96,768]{4,3,2,0,1:T(8,128)(2,1)S(1)}, u32[]{:S(2)}, u32[]{:S(2)}) collective-permute-start(bf16[2,1,2,96,768]{4,3,2,0,1:T(8,128)(2,1)S(1)} %broadcast_select_fusion.1), channel_id=1, source_target_pairs={{0,8},{4,12},{8,0},{12,4},{16,24},{20,28},{24,16},{28,20},{1,9},{5... | collective-permute-start | bytes 1769480 | tf_op jit(solution)/shard_map/ppermute | solution.py:890
  184.4 14.6 %copy-start = (bf16[32,4608]{1,0:T(8,128)(2,1)S(1)}, bf16[32,4608]{1,0:T(8,128)(2,1)}, u32[]{:S(2)}) copy-start(bf16[32,4608]{1,0:T(8,128)(2,1)} %reshape.116.gmod) | copy-start | bytes 884740
  (22 other events, 52.6 us)
